TPU v7x, 256 devices: a whole 4x4x8 slice. The times are simulated.
256 devices in a mesh: tm: 16 (over z_hi, y), chan: 16 (over z_lo, x, core).
Axes of the slice: x: 4, y: 4, z: 8 (z_hi: 4, z_lo: 2; z = z_hi * 2 + z_lo), core: 2. Of those that a mesh axis runs over, the one named last changes fastest.
Arguments:
- raw_data: bfloat16 [16384, 6144], P('chan', 'tm'), may hold values from -6 to 6
- band_taps: bfloat16 [61], replicated, may hold values from -0.75 to 0.75
- whitening: bfloat16 [16384, 1024], P('chan'), may hold values from -0.1875 to 0.1875
- band_offsets: int32 [128], P('chan'), may hold values from -3 to 3
- spatial: bfloat16 [1024, 3, 16384], P(None, None, 'chan'), may hold values from -0.0625 to 0.0625
- temporal: float32 [1024, 3, 61], replicated, may hold values from -0.4375 to 0.4375
Outputs:
- scores: float32 [1024, 6144], P('chan', 'tm')
All inputs are finite; a program needn't handle non-finite values.
Results may differ from a plain program's by a relative error of at most 0.0041.
Values may be sent and summed in bfloat16 or wider, within the bound.
No kernel may reach another device: no remote copies, remote signals or barrier semaphores. Data moves between devices by JAX's collectives and lax.ppermute only.
A program may use at most 256 MiB of HBM per device.

v0:
```python
import jax
import jax.numpy as jnp
from jax import lax
from jax.sharding import PartitionSpec as P


def with_halo(array, sides, width):
    for axis, dim in sides:
        devices, length = (lax.axis_size(axis), array.shape[dim])
        up = [(i, (i + 1) % devices) for i in range(devices - 1)]
        down = [(j, i) for i, j in up]
        last = lax.slice_in_dim(array, length - width, length, axis=dim)
        first = lax.slice_in_dim(array, 0, width, axis=dim)
        before = lax.ppermute(last, axis, up)
        after = lax.ppermute(first, axis, down)
        array = jnp.concatenate([before, array, after], axis=dim)
    return array


def toeplitz_rows(band_taps, in_width, out_width):
    length = band_taps.shape[0]
    padded = jnp.concatenate([band_taps, jnp.zeros((in_width + 1 - length,), band_taps.dtype)])
    tiled = jnp.tile(padded, out_width)[: out_width * in_width]
    return tiled.reshape(out_width, in_width)


def filter_rows(extended, band_taps, out_width):
    toeplitz = toeplitz_rows(band_taps, extended.shape[1], out_width)
    result = lax.dot_general(
        extended, toeplitz, (((1,), (1,)), ((), ())), preferred_element_type=jnp.float32
    )
    return result.astype(jnp.bfloat16)


def whiten(filtered, whitening, band_offsets, chan_index):
    channels = filtered.shape[0]
    band_width = whitening.shape[1]
    groups = band_offsets.shape[0]
    tile_rows = channels // groups
    all_channels = channels * lax.axis_size("chan")
    first_row = chan_index * channels
    padded = with_halo(filtered, (("chan", 0),), band_width)

    def one_group(group_index):
        row_begin = first_row + group_index * tile_rows
        start_row = (
            row_begin + tile_rows // 2 - band_width // 2 + band_offsets[group_index] * tile_rows
        )
        start_row = jnp.clip(start_row, 0, all_channels - band_width) - first_row + band_width
        window = lax.dynamic_slice_in_dim(padded, start_row, band_width, 0)
        weights = lax.dynamic_slice_in_dim(whitening, group_index * tile_rows, tile_rows, 0)
        return jnp.dot(weights, window, preferred_element_type=jnp.float32)

    stacked = lax.map(one_group, jnp.arange(groups, dtype=jnp.int32))
    return stacked.reshape(channels, filtered.shape[1]).astype(jnp.bfloat16)


def project(white_ext, spatial):
    return jnp.einsum("krc,cs->krs", spatial, white_ext, preferred_element_type=jnp.float32)


def time_filter(projected, temporal):
    tap_count = temporal.shape[2]
    out_len = projected.shape[2] - tap_count + 1
    total = jnp.zeros((projected.shape[0], out_len), jnp.float32)
    for offset in range(tap_count):
        piece = projected[:, :, offset : offset + out_len]
        weight = temporal[:, :, offset : offset + 1]
        total = total + jnp.sum(piece * weight, axis=1)
    return total


def local(raw_data, band_taps, whitening, band_offsets, spatial, temporal):
    samples = raw_data.shape[1]
    half_taps = band_taps.shape[0] // 2
    chan_index = lax.axis_index("chan")
    extended = with_halo(raw_data, (("tm", 1),), half_taps)
    filtered = filter_rows(extended, band_taps, samples)
    whitened = whiten(filtered, whitening, band_offsets, chan_index)
    white_ext = with_halo(whitened, (("tm", 1),), half_taps)
    projected = project(white_ext, spatial)
    own_rows = lax.psum_scatter(projected, "chan", scatter_dimension=0, tiled=True)
    own_count = own_rows.shape[0]
    own_temporal = lax.dynamic_slice_in_dim(temporal, chan_index * own_count, own_count, 0)
    scores = time_filter(own_rows, own_temporal)
    return scores


def solution(mesh):
    placed = (P("chan", "tm"), P(), P("chan", None), P("chan"), P(None, None, "chan"), P())
    return jax.shard_map(
        local, mesh=mesh, in_specs=placed, out_specs=P("chan", "tm"), check_vma=False
    )
```

profile of v0, /device:TPU:128, one launch (start us, length us, event | category | flops | bytes accessed | tf_op | source)
XLA Modules:
  0.0 420.4 jit_solution(380644674133286508)
XLA Ops:
  7.7 4.0 collective-permute-start.1
  11.7 1.9 collective-permute-start
  15.9 7.0 %collective-permute-done.1 = bf16[1024,30]{1,0:T(8,128)(2,1)S(1)} collective-permute-done((bf16[1024,30]{1,0:T(8,128)(2,1)S(1)}, bf16[1024,30]{1,0:T(8,128)(2,1)S(1)}, u32[]{:S(2)}, u32[]{:S(2)}) %collective-permute-start.1) | collective-permute-done | bytes 61472 | tf_op jit(solution)/shard_map/ppermute | solution.py:15
  22.9 8.4 %collective-permute-done = bf16[1024,30]{1,0:T(8,128)(2,1)S(1)} collective-permute-done((bf16[1024,30]{1,0:T(8,128)(2,1)S(1)}, bf16[1024,30]{1,0:T(8,128)(2,1)S(1)}, u32[]{:S(2)}, u32[]{:S(2)}) %collective-permute-start) | collective-permute-done | bytes 61472 | tf_op jit(solution)/shard_map/ppermute | solution.py:14
  31.3 1.9 convolution_convert_fusion
  34.5 3.9 collective-permute-start.2
  41.2 51.5 %while.14 = (s32[]{:T(128)}, bf16[8,128,384]{2,1,0:T(8,128)(2,1)}, s32[8]{0:T(128)S(1)}, bf16[1024,1024]{1,0:T(8,128)(2,1)}, s32[]{:T(128)}, /*index=5*/s32[8]{0...) while((s32[]{:T(128)}, bf16[8,128,384]{2,1,0:T(8,128)(2,1)}, ...), condition=%wide.region_1.2_spmd, body=%wide.region_0.1_spmd.sunk | while | flops 100663312 | bytes 1245587 | solution.py:54
  45.7 1.9 fusion.85
  52.1 1.9 fusion.85
  58.5 1.9 fusion.85
  64.9 2.0 fusion.85
  71.4 1.9 fusion.85
  77.8 1.9 fusion.85
  84.2 1.9 fusion.85
  90.7 1.9 fusion.85
  94.0 1.9 collective-permute-start.5
  96.0 4.1 collective-permute-start.4
  100.2 6.1 %collective-permute-done.4 = bf16[1024,30]{0,1:T(8,128)(2,1)S(1)} collective-permute-done((bf16[1024,30]{0,1:T(8,128)(2,1)S(1)}, bf16[1024,30]{0,1:T(8,128)(2,1)S(1)}, u32[]{:S(2)}, u32[]{:S(2)}) %collective-permute-start.4) | collective-permute-done | bytes 61472 | tf_op jit(solution)/shard_map/ppermute | solution.py:14
  106.4 8.9 %convolution_bitcast_fusion.1 = f32[1024,3,444]{0,2,1:T(8,128)} fusion(bf16[1024,3,1024]{2,0,1:T(8,128)(2,1)} %param.12, bf16[1024,30]{0,1:T(8,128)(2,1)S(1)} %collective-permute-done.5, bf16[1024,384]{0,1:T(8,128)(2,1)S(1)} %copy.134, bf16[1024,30]{0,1:T(8,128)(2,1)S(1)} %collective-permute-done.4), kind=kOutput, calls=%fused_computation.5 | convolution fusion | flops 2796134400 | bytes 12656640 | tf_op jit(solution)/shard_map/krc,cs->krs/dot_general | solution.py:59
  115.2 9.1 %copy.10 = f32[1024,3,444]{2,1,0:T(4,128)} copy(f32[1024,3,444]{0,2,1:T(8,128)} %convolution_bitcast_fusion.1) | data formatting | bytes 10911744 | tf_op jit(solution)/shard_map/krc,cs->krs/dot_general | solution.py:59
  155.8 123.7 %all-reduce.4.cloned.1.call-done = f32[1024,3,444]{2,1,0:T(4,128)} async-done(((f32[1024,3,444]{2,1,0:T(4,128)}), f32[1024,3,444]{2,1,0:T(4,128)}) %all-reduce.4.cloned.1.call-update) | async-done | bytes 5455888
  279.5 3.7 fusion.65
  283.4 6.7 %fusion.72 = (f32[64,384]{1,0:T(8,128)}, f32[64,384]{1,0:T(8,128)S(1)}, f32[64,384]{1,0:T(8,128)S(1)}, f32[64,384]{1,0:T(8,128)S(1)}, f32[64,384]{1,0:T(8,128)S(...) fusion(f32[1024,3,444]{2,1,0:T(4,128)} %all-reduce.4.cloned.1.call-done, ...), kind=kLoop, calls=%fused_computation.137 | loop fusion | flops 1105920 | bytes 3545892 | tf_op jit(solution)/shard_map/reduce_sum | solution.py:69
  291.0 6.5 %fusion.71 = (f32[64,384]{1,0:T(8,128)}, f32[64,384]{1,0:T(8,128)S(1)}, f32[64,384]{1,0:T(8,128)S(1)}, f32[64,384]{1,0:T(8,128)S(1)}, f32[64,384]{1,0:T(8,128)S(...) fusion(f32[1024,3,444]{2,1,0:T(4,128)} %all-reduce.4.cloned.1.call-done, ...), kind=kLoop, calls=%fused_computation.135 | loop fusion | flops 983040 | bytes 3151908 | tf_op jit(solution)/shard_map/reduce_sum | solution.py:69
  298.4 6.7 %fusion.70 = (f32[64,384]{1,0:T(8,128)}, f32[64,384]{1,0:T(8,128)S(1)}, f32[64,384]{1,0:T(8,128)S(1)}, f32[64,384]{1,0:T(8,128)}, f32[64,384]{1,0:T(8,128)}, /*i...) fusion(f32[1024,3,444]{2,1,0:T(4,128)} %all-reduce.4.cloned.1.call-done, u32[]{:T(128)S(6)} %multiply.1, ...), kind=kLoop, calls=%fused_computation.133 | loop fusion | flops 983040 | bytes 3151908 | tf_op jit(solution)/shard_map/reduce_sum | solution.py:69
  306.4 1.7 copy.238
  313.3 7.0 %fusion.69 = (f32[64,384]{1,0:T(8,128)}, f32[64,384]{1,0:T(8,128)}, f32[64,384]{1,0:T(8,128)}, f32[64,384]{1,0:T(8,128)}, f32[64,384]{1,0:T(8,128)}, /*index=5*/...) fusion(f32[1024,3,444]{2,1,0:T(4,128)} %all-reduce.4.cloned.1.call-done, u32[]{:T(128)S(6)} %multiply.1, ...), kind=kLoop, calls=%fused_computation.131 | loop fusion | flops 983040 | bytes 3151908 | tf_op jit(solution)/shard_map/reduce_sum | solution.py:69
  332.2 6.9 %fusion.68 = (f32[64,384]{1,0:T(8,128)}, f32[64,384]{1,0:T(8,128)}, f32[64,384]{1,0:T(8,128)}, f32[64,384]{1,0:T(8,128)}, f32[64,384]{1,0:T(8,128)}, /*index=5*/...) fusion(f32[1024,3,444]{2,1,0:T(4,128)} %all-reduce.4.cloned.1.call-done, u32[]{:T(128)S(6)} %multiply.1, ...), kind=kLoop, calls=%fused_computation.129 | loop fusion | flops 983040 | bytes 3151908 | tf_op jit(solution)/shard_map/reduce_sum | solution.py:69
  351.0 6.8 %fusion.67 = (f32[64,384]{1,0:T(8,128)}, f32[64,384]{1,0:T(8,128)}, f32[64,384]{1,0:T(8,128)}, f32[64,384]{1,0:T(8,128)}, f32[64,384]{1,0:T(8,128)}, /*index=5*/...) fusion(f32[1024,3,444]{2,1,0:T(4,128)} %all-reduce.4.cloned.1.call-done, u32[]{:T(128)S(6)} %multiply.1, ...), kind=kLoop, calls=%fused_computation.127 | loop fusion | flops 983040 | bytes 3151908 | tf_op jit(solution)/shard_map/reduce_sum | solution.py:69
  369.7 6.8 %fusion.66 = (f32[64,384]{1,0:T(8,128)}, f32[64,384]{1,0:T(8,128)}, f32[64,384]{1,0:T(8,128)}, f32[64,384]{1,0:T(8,128)}, f32[64,384]{1,0:T(8,128)}, /*index=5*/...) fusion(f32[1024,3,444]{2,1,0:T(4,128)} %all-reduce.4.cloned.1.call-done, u32[]{:T(128)S(6)} %multiply.1, ...), kind=kLoop, calls=%fused_computation.125 | loop fusion | flops 983040 | bytes 3151908 | tf_op jit(solution)/shard_map/reduce_sum | solution.py:69
  388.4 1.7 copy.206
  407.1 4.8 %add_add_fusion = f32[64,384]{0,1:T(8,128)} fusion(f32[64,384]{0,1:T(8,128)S(1)} %copy.256, f32[64,384]{0,1:T(8,128)S(1)} %copy.255, f32[64,384]{0,1:T(8,128)S(1)} %copy.254, f32[64,384]{0,1:T(8,128)S(1)} %copy.253, f32[64,384]{0,1:T(8,128)S(1)} %copy.252, f32[64,384]{0,1:T(8,128)S(1)} %copy.251, f32[64,384]{0,1:T(8,128)S(1)} %copy.250, ...), kind=kLoop, calls=%fused_computation.140 | loop fusion | flops 1474560 | bytes 6094848 | tf_op jit(solution)/shard_map/add | solution.py:69
  (164 shorter events, 124.7 us)
Async XLA Ops:
  6.5 273.0 %all-reduce.4.cloned.1.call-start = ((), (), s32[]{:S(2)}) async-start(), calls=%async_computation | async-start | bytes 16777216
  7.7 15.2 %collective-permute-start.1 = (bf16[1024,30]{1,0:T(8,128)(2,1)S(1)}, bf16[1024,30]{1,0:T(8,128)(2,1)S(1)}, u32[]{:S(2)}, u32[]{:S(2)}) collective-permute-start(bf16[1024,30]{1,0:T(8,128)(2,1)S(1)} %get-tuple-element.287), channel_id=1, source_target_pairs={{16,0},{32,16},{48,32},{64,48},{80,64},{96,80},{112,96},{128,112},... | collective-permute-start | bytes 184328 | tf_op jit(solution)/shard_map/ppermute | solution.py:15
  11.7 19.5 %collective-permute-start = (bf16[1024,30]{1,0:T(8,128)(2,1)S(1)}, bf16[1024,30]{1,0:T(8,128)(2,1)S(1)}, u32[]{:S(2)}, u32[]{:S(2)}) collective-permute-start(bf16[1024,30]{1,0:T(8,128)(2,1)S(1)} %get-tuple-element.286), channel_id=1, source_target_pairs={{0,16},{16,32},{32,48},{48,64},{64,80},{80,96},{96,112},{112,128},... | collective-permute-start | bytes 184328 | tf_op jit(solution)/shard_map/ppermute | solution.py:14
  15.1 26.1 %copy-start.1 = (s32[8]{0:T(128)S(1)}, s32[8]{0:T(128)}, u32[]{:S(2)}) copy-start(s32[8]{0:T(128)} %param.11) | copy-start | bytes 100
  33.2 5.2 %collective-permute-start.3 = (bf16[1024,384]{1,0:T(8,128)(2,1)S(1)}, bf16[1024,384]{1,0:T(8,128)(2,1)S(1)}, u32[]{:S(2)}, u32[]{:S(2)}) collective-permute-start(bf16[1024,384]{1,0:T(8,128)(2,1)S(1)} %convolution_convert_fusion), channel_id=1, source_target_pairs={{1,0},{2,1},{3,2},{4,3},{5,4},{6,5},{7,6},{8,7},{9,8},{10,9},{11,1... | collective-permute-start | bytes 2359304 | tf_op jit(solution)/shard_map/ppermute | solution.py:15
  34.5 5.1 %collective-permute-start.2 = (bf16[1024,384]{1,0:T(8,128)(2,1)S(1)}, bf16[1024,384]{1,0:T(8,128)(2,1)}, u32[]{:S(2)}, u32[]{:S(2)}) collective-permute-start(bf16[1024,384]{1,0:T(8,128)(2,1)S(1)} %convolution_convert_fusion), channel_id=1, source_target_pairs={{0,1},{1,2},{2,3},{3,4},{4,5},{5,6},{6,7},{7,8},{8,9},{9,10},{10,1... | collective-permute-start | bytes 2359304 | tf_op jit(solution)/shard_map/ppermute | solution.py:14
  38.4 0.9 copy-start
  94.0 6.2 %collective-permute-start.5 = (bf16[1024,30]{0,1:T(8,128)(2,1)S(1)}, bf16[1024,30]{0,1:T(8,128)(2,1)S(1)}, u32[]{:S(2)}, u32[]{:S(2)}) collective-permute-start(bf16[1024,30]{0,1:T(8,128)(2,1)S(1)} %get-tuple-element.285), channel_id=1, source_target_pairs={{16,0},{32,16},{48,32},{64,48},{80,64},{96,80},{112,96},{128,112},... | collective-permute-start | bytes 184328 | tf_op jit(solution)/shard_map/ppermute | solution.py:15
  96.0 10.4 %collective-permute-start.4 = (bf16[1024,30]{0,1:T(8,128)(2,1)S(1)}, bf16[1024,30]{0,1:T(8,128)(2,1)S(1)}, u32[]{:S(2)}, u32[]{:S(2)}) collective-permute-start(bf16[1024,30]{0,1:T(8,128)(2,1)S(1)} %get-tuple-element.284), channel_id=1, source_target_pairs={{0,16},{16,32},{32,48},{48,64},{64,80},{80,96},{96,112},{112,128},... | collective-permute-start | bytes 184328 | tf_op jit(solution)/shard_map/ppermute | solution.py:14
  124.3 30.3 %copy-start.2 = (u32[256]{0:T(256)S(1)}, u32[256]{0:T(256)}, u32[]{:S(2)}) copy-start(u32[256]{0:T(256)} %constant.98) | copy-start | bytes 3076
Sparse Core Ops, SparseCore 0:
  124.4 155.0 all-reduce.3
where the time goes:
time: 428 us; the launch traced here: 420 us
  waiting for transfers between devices  146 us (34%)
  local copies, waits for them, and re-layouts  134 us (31%)
  other arithmetic  57.5 us (13%)
  matrix products  26.3 us (6%)
  loops' own time  25.6 us (6%)
  starting transfers between devices  17.2 us (4%)
  between operations  14.4 us (3%)
    unnamed x2, waiting for transfers between devices  124 us
    unnamed x68, local copies, waits for them, and re-layouts  77.8 us
    reduce_sum x8, other arithmetic, time_filter(): total = total + jnp.sum(piece * weight, axis=1)  51.1 us
    another operation x1, loops' own time, whiten(): stacked = lax.map(one_group, jnp.arange(groups, dtype=jnp.int32))  25.6 us
    mul x61, local copies, waits for them, and re-layouts, time_filter(): total = total + jnp.sum(piece * weight, axis=1)  25 us
    dot_general x8, matrix products, one_group(): return jnp.dot(weights, window, preferred_element_type=jnp.float32)  15.5 us
    ppermute x3, waiting for transfers between devices, with_halo(): before = lax.ppermute(last, axis, up)  14.7 us
    ppermute x3, starting transfers between devices, with_halo(): before = lax.ppermute(last, axis, up)  9.97 us
  transfers between devices with their start and end apart: 7, of which 6 were waited for; matrix products, arithmetic and copies ran while one was open for 8% of the time, Pallas kernels for 0%

commit v1 on v0

v1 whole, which is shorter than its diff:
```python
import functools

import jax
import jax.numpy as jnp
import numpy as np
from jax import lax
from jax.experimental import pallas as pl
from jax.experimental.pallas import tpu as pltpu
from jax.sharding import PartitionSpec as P

LANES = 128
EDGE = 64
F = 256
POINTS = 2 * F - 1
WIDE = 512
REACH = 832


def halves(matrix):
    high = matrix.astype(jnp.bfloat16)
    low = (matrix - high.astype(np.float64)).astype(jnp.bfloat16)
    return high, low


def angles(samples):
    steps = np.outer(np.arange(samples), np.arange(F)) % POINTS
    return 2.0 * np.pi * steps / POINTS


def forward_matrix(samples, rows):
    turn = angles(samples)
    full = np.zeros((rows, 2 * F))
    full[:samples] = np.concatenate([np.cos(turn), np.sin(turn)], axis=1)
    return full


def inverse_matrix(samples):
    turn = angles(samples).T
    weight = np.full((F, 1), 2.0 / POINTS)
    weight[0] = 1.0 / POINTS
    return np.concatenate([weight * np.cos(turn), -weight * np.sin(turn)], axis=0)


def pack(edge):
    half = edge.shape[0] // 2
    return jnp.concatenate([edge[:half], edge[half:]], axis=1)


def rolled(row, rows, shift):
    wide = jnp.broadcast_to(row, (rows, row.shape[1]))
    return pltpu.roll(wide, shift % row.shape[1], 1, stride=1, stride_axis=0)


def filter_kernel(taps, samples, span_ref, raw_ref, prev_ref, next_ref, row_ref, own_ref, up_ref, down_ref, toep_ref):
    rows = raw_ref.shape[0]
    half = rows // 2
    row = row_ref[...]
    reach = (taps - 1) // 8 * 8
    column = lax.broadcasted_iota(jnp.int32, (1, WIDE), 1)
    keep = (column >= span_ref[0]) & (column < span_ref[1])
    toep_ref[:samples] = jnp.where(keep, rolled(row, samples, reach), 0.0).astype(jnp.bfloat16)
    toep_ref[samples : samples + EDGE] = jnp.where(keep, rolled(row, EDGE, reach - EDGE), 0.0).astype(jnp.bfloat16)
    toep_ref[samples + EDGE :] = jnp.where(keep, rolled(row, EDGE, reach + samples), 0.0).astype(jnp.bfloat16)

    lane = lax.broadcasted_iota(jnp.int32, (half, LANES), 1)
    prev = prev_ref[...].astype(jnp.float32)
    after = next_ref[...].astype(jnp.float32)
    low = lane < EDGE
    sides = (
        jnp.where(low, prev, pltpu.roll(after, EDGE, 1)).astype(jnp.bfloat16),
        jnp.where(low, pltpu.roll(prev, EDGE, 1), after).astype(jnp.bfloat16),
    )
    for part in range(2):
        body = slice(part * half, (part + 1) * half)
        value = jnp.dot(raw_ref[body], toep_ref[:samples], preferred_element_type=jnp.float32)
        value += jnp.dot(sides[part], toep_ref[samples:], preferred_element_type=jnp.float32)
        own_ref[body] = value.astype(jnp.bfloat16)
    whole = samples // LANES
    fold = REACH // 2
    for ref, begin in ((up_ref, rows - REACH), (down_ref, 0)):
        for block in range(whole):
            ref[block * REACH : (block + 1) * REACH] = own_ref[begin : begin + REACH, block * LANES : (block + 1) * LANES]
        first = own_ref[begin : begin + fold, samples:].astype(jnp.float32)
        second = own_ref[begin + fold : begin + REACH, samples:].astype(jnp.float32)
        ref[whole * REACH :] = (first + pltpu.roll(second, EDGE, 1)).astype(jnp.bfloat16)


def score_kernel(groups, samples, meta_ref, own_ref, before_ref, after_ref, white_ref, fh_ref, fl_ref, ih_ref, il_ref, spatial_ref, hat_ref, keep_ref, send_ref, ext_ref, what_ref):
    rows = own_ref.shape[0]
    tile = rows // groups
    band = white_ref.shape[1]

    @pl.when(pl.program_id(0) == 0)
    def _():
        whole = samples // LANES
        fold = REACH // 2
        low = lax.broadcasted_iota(jnp.int32, (fold, LANES), 1) < EDGE
        ext_ref[REACH : REACH + rows] = own_ref[...]
        for ref, begin in ((before_ref, 0), (after_ref, REACH + rows)):
            for block in range(whole):
                ext_ref[begin : begin + REACH, block * LANES : (block + 1) * LANES] = ref[block * REACH : (block + 1) * REACH]
            last = ref[whole * REACH :].astype(jnp.float32)
            ext_ref[begin : begin + fold, samples:] = jnp.where(low, last, 0.0).astype(jnp.bfloat16)
            ext_ref[begin + fold : begin + REACH, samples:] = jnp.where(low, pltpu.roll(last, EDGE, 1), 0.0).astype(jnp.bfloat16)
        for group in range(groups):
            start = pl.multiple_of(meta_ref[group], EDGE)
            body = slice(group * tile, (group + 1) * tile)
            value = jnp.dot(white_ref[body], ext_ref[pl.ds(start, band)], preferred_element_type=jnp.float32)
            value = value.astype(jnp.bfloat16)
            hat = jnp.dot(value, fh_ref[...], preferred_element_type=jnp.float32)
            hat += jnp.dot(value, fl_ref[...], preferred_element_type=jnp.float32)
            what_ref[body] = hat.astype(jnp.bfloat16)

    rank, block, _ = spatial_ref.shape
    weights = spatial_ref[...].reshape(rank * block, rows)
    product = jnp.dot(weights, what_ref[...], preferred_element_type=jnp.float32)
    real = imag = 0.0
    for r in range(rank):
        a = product[r * block : (r + 1) * block, :F]
        b = product[r * block : (r + 1) * block, F:]
        c = hat_ref[r, :, :F]
        d = hat_ref[r, :, F:]
        real += a * c + b * d
        imag += a * d - b * c
    real = real.astype(jnp.bfloat16)
    imag = imag.astype(jnp.bfloat16)
    value = jnp.dot(real, ih_ref[:F], preferred_element_type=jnp.float32)
    value += jnp.dot(real, il_ref[:F], preferred_element_type=jnp.float32)
    value += jnp.dot(imag, ih_ref[F:], preferred_element_type=jnp.float32)
    value += jnp.dot(imag, il_ref[F:], preferred_element_type=jnp.float32)
    own = keep_ref.shape[1]
    core = meta_ref[groups]
    for pair in range(block // (2 * own)):
        even = value[2 * pair * own : (2 * pair + 1) * own]
        odd = value[(2 * pair + 1) * own : (2 * pair + 2) * own]
        keep_ref[pair] = jnp.where(core == 0, even, odd)
        send_ref[pair] = jnp.where(core == 0, odd, even).astype(jnp.bfloat16)


def local(raw, band_taps, whitening, band_offsets, spatial, temporal):
    rows, samples = raw.shape
    taps = band_taps.shape[0]
    groups = band_offsets.shape[0]
    tile = rows // groups
    band = whitening.shape[1]
    templates, rank, _ = spatial.shape
    half_taps = taps // 2
    window = samples + taps - 1
    n_tm = lax.axis_size("tm")
    n_chan = lax.axis_size("chan")
    t = lax.axis_index("tm")
    c = lax.axis_index("chan")
    own = templates // n_chan

    up = [(i, i + 1) for i in range(n_tm - 1)]
    down = [(j, i) for i, j in up]
    prev = lax.ppermute(pack(raw[:, samples - EDGE :]), "tm", up)
    after = lax.ppermute(pack(raw[:, :EDGE]), "tm", down)

    reverse = band_taps.astype(jnp.float32)
    row = jnp.concatenate([reverse[:1], jnp.zeros((WIDE - taps,), jnp.float32), reverse[1:][::-1]])
    row = jnp.roll(row, (taps - 1) % 8)[None]
    begin = jnp.where(t == 0, half_taps, 0)
    end = jnp.where(t == n_tm - 1, samples + half_taps, window)
    span = jnp.stack([begin, end]).astype(jnp.int32)
    payload = (samples // LANES) * REACH + REACH // 2
    vmem = pl.BlockSpec(memory_space=pltpu.VMEM)
    smem = pl.BlockSpec(memory_space=pltpu.SMEM)
    filtered, to_up, to_down = pl.pallas_call(
        functools.partial(filter_kernel, taps, samples),
        out_shape=(
            jax.ShapeDtypeStruct((rows, WIDE), jnp.bfloat16),
            jax.ShapeDtypeStruct((payload, LANES), jnp.bfloat16),
            jax.ShapeDtypeStruct((payload, LANES), jnp.bfloat16),
        ),
        in_specs=[smem, vmem, vmem, vmem, vmem],
        out_specs=(vmem, vmem, vmem),
        scratch_shapes=[pltpu.VMEM((WIDE, WIDE), jnp.bfloat16)],
        compiler_params=pltpu.CompilerParams(vmem_limit_bytes=24 << 20),
        name="filter",
    )(span, raw, prev, after, row)

    up = [(i, i + 1) for i in range(n_chan - 1)]
    down = [(j, i) for i, j in up]
    before_rows = lax.ppermute(to_up, "chan", up)
    after_rows = lax.ppermute(to_down, "chan", down)

    hat = jnp.einsum(
        "krj,jf->rkf",
        temporal,
        jnp.asarray(forward_matrix(taps, taps), jnp.float32),
        precision=lax.Precision.HIGHEST,
    )
    first_row = c * rows
    row_begin = first_row + jnp.arange(groups, dtype=jnp.int32) * tile
    start = row_begin + tile // 2 - band // 2 + band_offsets * tile
    start = jnp.clip(start, 0, n_chan * rows - band) - first_row + REACH
    start = jnp.clip(start, 0, 2 * REACH + rows - band)
    meta = jnp.concatenate([start, (c % 2)[None]]).astype(jnp.int32)

    fh, fl = (jnp.asarray(m) for m in halves(forward_matrix(window, WIDE)))
    ih, il = (jnp.asarray(m) for m in halves(inverse_matrix(samples)))
    block = 256
    pairs = block // (2 * own)

    def fixed(shape):
        return pl.BlockSpec(shape, lambda i, m: (0,) * len(shape), pipeline_mode=pl.Buffered(1))

    keep, send = pl.pallas_call(
        functools.partial(score_kernel, groups, samples),
        out_shape=(
            jax.ShapeDtypeStruct((n_chan // 2, own, samples), jnp.float32),
            jax.ShapeDtypeStruct((n_chan // 2, own, samples), jnp.bfloat16),
        ),
        grid_spec=pltpu.PrefetchScalarGridSpec(
            num_scalar_prefetch=1,
            grid=(templates // block,),
            in_specs=[
                fixed((rows, WIDE)),
                fixed((payload, LANES)),
                fixed((payload, LANES)),
                fixed((rows, band)),
                fixed(fh.shape),
                fixed(fl.shape),
                fixed(ih.shape),
                fixed(il.shape),
                pl.BlockSpec((rank, block, rows), lambda i, m: (0, i, 0)),
                pl.BlockSpec((rank, block, 2 * F), lambda i, m: (0, i, 0)),
            ],
            out_specs=(
                pl.BlockSpec((pairs, own, samples), lambda i, m: (i, 0, 0)),
                pl.BlockSpec((pairs, own, samples), lambda i, m: (i, 0, 0)),
            ),
            scratch_shapes=[
                pltpu.VMEM((2 * REACH + rows, WIDE), jnp.bfloat16),
                pltpu.VMEM((rows, 2 * F), jnp.bfloat16),
            ],
        ),
        compiler_params=pltpu.CompilerParams(vmem_limit_bytes=40 << 20),
        name="score",
    )(meta, filtered, before_rows, after_rows, whitening, fh, fl, ih, il, spatial.transpose(1, 0, 2), hat)

    other = lax.ppermute(send, "chan", [(i, i ^ 1) for i in range(n_chan)])
    both = (keep + other.astype(jnp.float32)).astype(jnp.bfloat16)
    members = [[2 * i + core for i in range(n_chan // 2)] for core in range(2)]
    shares = lax.all_to_all(both, "chan", 0, 0, axis_index_groups=members)
    return jnp.sum(shares.astype(jnp.float32), axis=0)


def solution(mesh):
    placed = (P("chan", "tm"), P(), P("chan", None), P("chan"), P(None, None, "chan"), P())
    return jax.shard_map(local, mesh=mesh, in_specs=placed, out_specs=P("chan", "tm"), check_vma=False)
```

time: 428 us -> 74.1 us (0.17)
  the two profiles are of different devices: /device:TPU:128 before, /device:TPU:88 now
where the time goes in v1:
time: 74.1 us; the launch traced here: 73.7 us
  starting transfers between devices  15.3 us (21%)
  Pallas kernels  14.4 us (19%)
  blocking collectives  14.3 us (19%)
  waiting for transfers between devices  9.46 us (13%)
  local copies, waits for them, and re-layouts  8.93 us (12%)
  matrix products  8.32 us (11%)
  other arithmetic  2.75 us (4%)
    all_to_all x1, blocking collectives, local(): shares = lax.all_to_all(both, 'chan', 0, 0, axis_index_groups=members)  14.3 us
    pallas_call x1, Pallas kernels, local(): pl.pallas_call(functools.partial(score_kernel, groups, samples), out_shap...  11.5 us
    dot_general x1, matrix products, local(): jnp.einsum('krj,jf->rkf', temporal, jnp.asarray(forward_matrix(taps, taps...  8.32 us
    ppermute x1, waiting for transfers between devices, local(): after = lax.ppermute(pack(raw[:, :EDGE]), 'tm', down)  8.1 us
    ppermute x1, starting transfers between devices, local(): prev = lax.ppermute(pack(raw[:, samples - EDGE:]), 'tm', up)  6.05 us
    unnamed x16, local copies, waits for them, and re-layouts  4.78 us
    ppermute x1, starting transfers between devices, local(): other = lax.ppermute(send, 'chan', [(i, i ^ 1) for i in range(n_chan)])  4.66 us
    pallas_call x1, Pallas kernels, local(): pl.pallas_call(functools.partial(filter_kernel, taps, samples), out_shape...  2.91 us
  transfers between devices with their start and end apart: 5, of which 2 were waited for; matrix products, arithmetic and copies ran while one was open for 18% of the time, Pallas kernels for 0%

profile of v1, /device:TPU:88, one launch (start us, length us, event | category | flops | bytes accessed | tf_op | source)
XLA Modules:
  0.0 73.7 jit_solution(2335665017561551303)
XLA Ops:
  0.0 1.3 %fusion = (bf16[512,64]{1,0:T(8,128)(2,1)S(1)}, bf16[512,64]{1,0:T(8,128)(2,1)S(1)}, bf16[512,64]{1,0:T(8,128)(2,1)S(1)}, bf16[512,64]{1,0:T(8,128)(2,1)S(1)}) fusion(bf16[1024,384]{1,0:T(8,128)(2,1)} %raw_ref.1), kind=kLoop, calls=%fused_computation.10 | loop fusion | bytes 524288 | tf_op jit(solution)/shard_map/slice | solution.py:46
  1.3 0.1 pad_maximum_fusion
  1.4 6.0 %collective-permute-start = (bf16[512,128]{1,0:T(8,128)(2,1)S(1)}, bf16[512,128]{1,0:T(8,128)(2,1)S(1)}, u32[]{:S(2)}, u32[]{:S(2)}) collective-permute-start(bf16[512,128]{1,0:T(8,128)(2,1)S(1)} %pad_maximum_fusion), channel_id=1, source_target_pairs={{0,16},{16,32},{32,48},{48,64},{64,80},{80,96},{96,112},{112,128},... | collective-permute-start | bytes 393224 | tf_op jit(solution)/shard_map/ppermute | solution.py:157
  7.5 0.1 pad_maximum_fusion.1
  7.6 1.9 %collective-permute-start.1 = (bf16[512,128]{1,0:T(8,128)(2,1)S(1)}, bf16[512,128]{1,0:T(8,128)(2,1)S(1)}, u32[]{:S(2)}, u32[]{:S(2)}) collective-permute-start(bf16[512,128]{1,0:T(8,128)(2,1)S(1)} %pad_maximum_fusion.1), channel_id=1, source_target_pairs={{16,0},{32,16},{48,32},{64,48},{80,64},{96,80},{112,96},{128,112},... | collective-permute-start | bytes 393224 | tf_op jit(solution)/shard_map/ppermute | solution.py:158
  9.5 1.2 %slice.43 = f32[1]{0:T(128)} slice(bf16[61]{0:T(256)(128)(2,1)} %param.12), slice={[0:1]} | slice | bytes 8 | tf_op jit(solution)/shard_map/slice | solution.py:161
  10.7 0.7 slice.44
  11.5 0.1 rev.3
  11.6 0.7 pad_maximum_fusion.2
  12.3 0.1 pad_add_fusion.1.span_ref
  12.3 0.7 slice.41
  13.1 0.1 slice.42
  13.2 0.1 pad_maximum_fusion.3
  13.2 8.1 %collective-permute-done.1.next_ref = bf16[512,128]{1,0:T(8,128)(2,1)S(1)} collective-permute-done((bf16[512,128]{1,0:T(8,128)(2,1)S(1)}, bf16[512,128]{1,0:T(8,128)(2,1)S(1)}, u32[]{:S(2)}, u32[]{:S(2)}) %collective-permute-start.1) | collective-permute-done | bytes 131104 | tf_op jit(solution)/shard_map/ppermute | solution.py:158
  21.3 1.1 %copy-done.2 = bf16[1024,384]{1,0:T(8,128)(2,1)S(1)} copy-done((bf16[1024,384]{1,0:T(8,128)(2,1)S(1)}, bf16[1024,384]{1,0:T(8,128)(2,1)}, u32[]{:S(2)}) %copy-start.2) | copy-done | bytes 786456
  22.5 2.9 %filter.1 = (bf16[1024,512]{1,0:T(8,128)(2,1)S(1)}, bf16[2912,128]{1,0:T(8,128)(2,1)}, bf16[2912,128]{1,0:T(8,128)(2,1)}) custom-call(s32[2]{0:T(128)S(1)} %pad_add_fusion.1.span_ref, bf16[1024,384]{1,0:T(8,128)(2,1)S(1)} %copy-done.2, bf16[512,128]{1,0:T(8,128)(2,1)S(1)} %collective-permute-done.prev_ref, ...), custom_call_target="tpu_custom_call" | custom-call | tf_op jit(solution)/shard_map/filter/pallas_call | solution.py:169
  25.4 1.4 %collective-permute-start.2 = (bf16[2912,128]{1,0:T(8,128)(2,1)}, bf16[2912,128]{1,0:T(8,128)(2,1)S(1)}, u32[]{:S(2)}, u32[]{:S(2)}) collective-permute-start(bf16[2912,128]{1,0:T(8,128)(2,1)} %get-tuple-element.11), channel_id=1, source_target_pairs={{0,1},{1,2},{2,3},{3,4},{4,5},{5,6},{6,7},{7,8},{8,9},{9,10},{10,1... | collective-permute-start | bytes 2236424 | tf_op jit(solution)/shard_map/ppermute | solution.py:185
  26.8 1.3 %collective-permute-start.3 = (bf16[2912,128]{1,0:T(8,128)(2,1)}, bf16[2912,128]{1,0:T(8,128)(2,1)S(1)}, u32[]{:S(2)}, u32[]{:S(2)}) collective-permute-start(bf16[2912,128]{1,0:T(8,128)(2,1)} %get-tuple-element.12), channel_id=1, source_target_pairs={{1,0},{2,1},{3,2},{4,3},{5,4},{6,5},{7,6},{8,7},{9,8},{10,9},{11,1... | collective-permute-start | bytes 2236424 | tf_op jit(solution)/shard_map/ppermute | solution.py:186
  28.2 0.0 copy-start.4
  28.2 0.0 copy-start.6
  28.2 0.8 %add_clamp_fusion = s32[8]{0:T(128)S(1)} fusion(s32[8]{0:T(128)} %param.14, s32[]{:T(128)S(6)} %mul.9), kind=kLoop, calls=%fused_computation.9 | loop fusion | flops 72 | bytes 68 | tf_op jit(solution)/shard_map/jit(clip)/min | solution.py:198
  29.0 0.1 pad_add_fusion.meta_ref
  29.1 8.3 %convolution_bitcast_fusion.hat_ref = f32[3,1024,512]{2,1,0:T(8,128)} fusion(f32[61,512,1]{1,0,2:T(8,128)} %constant.63, f32[1024,3,61]{0,2,1:T(8,128)S(1)} %copy-done), kind=kOutput, calls=%fused_computation | convolution fusion | flops 1151336448 | bytes 7165952 | tf_op jit(solution)/shard_map/krj,jf->rkf/dot_general | solution.py:188
  37.4 1.6 %copy-done.3 = bf16[1024,1024]{1,0:T(8,128)(2,1)S(1)} copy-done((bf16[1024,1024]{1,0:T(8,128)(2,1)S(1)}, bf16[1024,1024]{1,0:T(8,128)(2,1)}, u32[]{:S(2)}) %copy-start.3) | copy-done | bytes 2097176
  39.0 1.0 %copy-done.5 = bf16[512,512]{1,0:T(8,128)(2,1)S(1)} copy-done((bf16[512,512]{1,0:T(8,128)(2,1)S(1)}, bf16[512,512]{1,0:T(8,128)(2,1)}, u32[]{:S(2)}) %copy-start.5) | copy-done | bytes 524312
  40.1 1.0 %copy-done.7 = bf16[512,384]{1,0:T(8,128)(2,1)S(1)} copy-done((bf16[512,384]{1,0:T(8,128)(2,1)S(1)}, bf16[512,384]{1,0:T(8,128)(2,1)}, u32[]{:S(2)}) %copy-start.7) | copy-done | bytes 393240
  41.1 11.5 %score.1 = (f32[8,64,384]{2,1,0:T(8,128)S(1)}, bf16[8,64,384]{2,1,0:T(8,128)(2,1)S(1)}) custom-call(s32[9]{0:T(128)S(1)} %pad_add_fusion.meta_ref, bf16[1024,512]{1,0:T(8,128)(2,1)S(1)} %get-tuple-element.10.own_ref, bf16[2912,128]{1,0:T(8,128)(2,1)S(1)} %collective-permute-done.2.before_ref, bf16[2912,128]{1,0:T(8,128)(2,1)S(1)} %collective-permute-done.3.after_ref, ...), custom_call_target="tpu_custom_call" | custom-call | tf_op jit(solution)/shard_map/score/pallas_call | solution.py:209
  52.6 4.7 %collective-permute-start.4 = (bf16[8,64,384]{2,1,0:T(8,128)(2,1)S(1)}, bf16[8,64,384]{2,1,0:T(8,128)(2,1)S(1)}, u32[]{:S(2)}, u32[]{:S(2)}) collective-permute-start(bf16[8,64,384]{2,1,0:T(8,128)(2,1)S(1)} %get-tuple-element.14), channel_id=1, source_target_pairs={{0,1},{1,0},{2,3},{3,2},{4,5},{5,4},{6,7},{7,6},{8,9},{9,8},{10,11... | collective-permute-start | bytes 1179656 | tf_op jit(solution)/shard_map/ppermute | solution.py:243
  57.3 1.3 %collective-permute-done.4 = bf16[8,64,384]{2,1,0:T(8,128)(2,1)S(1)} collective-permute-done((bf16[8,64,384]{2,1,0:T(8,128)(2,1)S(1)}, bf16[8,64,384]{2,1,0:T(8,128)(2,1)S(1)}, u32[]{:S(2)}, u32[]{:S(2)}) %collective-permute-start.4) | collective-permute-done | bytes 393248 | tf_op jit(solution)/shard_map/ppermute | solution.py:243
  58.6 0.1 add_convert_fusion
  58.7 14.3 %all_to_all.5 = bf16[8,64,384]{2,1,0:T(8,128)(2,1)S(1)} all-to-all(bf16[8,64,384]{2,1,0:T(8,128)(2,1)S(1)} %add_convert_fusion), channel_id=1, replica_groups={{0,2,4,6,8,10,12,14},{1,3,5,7,9,11,13,15},{16,18,20,22,24,26,28,30},{17..., dimensions={0} | all-to-all | bytes 786432 | tf_op jit(solution)/shard_map/all_to_all | solution.py:246
  73.0 0.7 convert_reduce_fusion
  (14 shorter events, 0.0 us)
Async XLA Ops:
  0.0 29.1 %copy-start = (f32[1024,3,61]{0,2,1:T(8,128)S(1)}, f32[1024,3,61]{0,2,1:T(8,128)}, u32[]{:S(2)}) copy-start(f32[1024,3,61]{0,2,1:T(8,128)} %param.16) | copy-start | bytes 2248708
  1.4 11.8 %collective-permute-start = (bf16[512,128]{1,0:T(8,128)(2,1)S(1)}, bf16[512,128]{1,0:T(8,128)(2,1)S(1)}, u32[]{:S(2)}, u32[]{:S(2)}) collective-permute-start(bf16[512,128]{1,0:T(8,128)(2,1)S(1)} %pad_maximum_fusion), channel_id=1, source_target_pairs={{0,16},{16,32},{32,48},{48,64},{64,80},{80,96},{96,112},{112,128},... | collective-permute-start | bytes 393224 | tf_op jit(solution)/shard_map/ppermute | solution.py:157
  7.6 13.7 %collective-permute-start.1 = (bf16[512,128]{1,0:T(8,128)(2,1)S(1)}, bf16[512,128]{1,0:T(8,128)(2,1)S(1)}, u32[]{:S(2)}, u32[]{:S(2)}) collective-permute-start(bf16[512,128]{1,0:T(8,128)(2,1)S(1)} %pad_maximum_fusion.1), channel_id=1, source_target_pairs={{16,0},{32,16},{48,32},{64,48},{80,64},{96,80},{112,96},{128,112},... | collective-permute-start | bytes 393224 | tf_op jit(solution)/shard_map/ppermute | solution.py:158
  21.3 1.1 %copy-start.2 = (bf16[1024,384]{1,0:T(8,128)(2,1)S(1)}, bf16[1024,384]{1,0:T(8,128)(2,1)}, u32[]{:S(2)}) copy-start(bf16[1024,384]{1,0:T(8,128)(2,1)} %raw_ref.1) | copy-start | bytes 2359300
  25.4 12.0 %collective-permute-start.2 = (bf16[2912,128]{1,0:T(8,128)(2,1)}, bf16[2912,128]{1,0:T(8,128)(2,1)S(1)}, u32[]{:S(2)}, u32[]{:S(2)}) collective-permute-start(bf16[2912,128]{1,0:T(8,128)(2,1)} %get-tuple-element.11), channel_id=1, source_target_pairs={{0,1},{1,2},{2,3},{3,4},{4,5},{5,6},{6,7},{7,8},{8,9},{9,10},{10,1... | collective-permute-start | bytes 2236424 | tf_op jit(solution)/shard_map/ppermute | solution.py:185
  26.8 10.6 %collective-permute-start.3 = (bf16[2912,128]{1,0:T(8,128)(2,1)}, bf16[2912,128]{1,0:T(8,128)(2,1)S(1)}, u32[]{:S(2)}, u32[]{:S(2)}) collective-permute-start(bf16[2912,128]{1,0:T(8,128)(2,1)} %get-tuple-element.12), channel_id=1, source_target_pairs={{1,0},{2,1},{3,2},{4,3},{5,4},{6,5},{7,6},{8,7},{9,8},{10,9},{11,1... | collective-permute-start | bytes 2236424 | tf_op jit(solution)/shard_map/ppermute | solution.py:186
  28.1 9.3 %copy-start.1 = (bf16[1024,3,1024]{2,0,1:T(8,128)(2,1)S(1)}, bf16[1024,3,1024]{2,0,1:T(8,128)(2,1)}, u32[]{:S(2)}) copy-start(bf16[1024,3,1024]{2,0,1:T(8,128)(2,1)} %param.15) | copy-start | bytes 18874372
  28.2 9.3 %copy-start.4 = (bf16[512,512]{1,0:T(8,128)(2,1)S(1)}, bf16[512,512]{1,0:T(8,128)(2,1)}, u32[]{:S(2)}) copy-start(bf16[512,512]{1,0:T(8,128)(2,1)} %constant.59.clone.fl_ref) | copy-start | bytes 1572868
  28.2 9.3 %copy-start.6 = (bf16[512,384]{1,0:T(8,128)(2,1)S(1)}, bf16[512,384]{1,0:T(8,128)(2,1)}, u32[]{:S(2)}) copy-start(bf16[512,384]{1,0:T(8,128)(2,1)} %constant.61.clone.il_ref) | copy-start | bytes 1179652
  37.4 1.6 %copy-start.3 = (bf16[1024,1024]{1,0:T(8,128)(2,1)S(1)}, bf16[1024,1024]{1,0:T(8,128)(2,1)}, u32[]{:S(2)}) copy-start(bf16[1024,1024]{1,0:T(8,128)(2,1)} %white_ref.1) | copy-start | bytes 6291460
  39.0 1.0 %copy-start.5 = (bf16[512,512]{1,0:T(8,128)(2,1)S(1)}, bf16[512,512]{1,0:T(8,128)(2,1)}, u32[]{:S(2)}) copy-start(bf16[512,512]{1,0:T(8,128)(2,1)} %constant.58.clone.fh_ref) | copy-start | bytes 1572868
  40.1 1.0 %copy-start.7 = (bf16[512,384]{1,0:T(8,128)(2,1)S(1)}, bf16[512,384]{1,0:T(8,128)(2,1)}, u32[]{:S(2)}) copy-start(bf16[512,384]{1,0:T(8,128)(2,1)} %constant.60.clone.ih_ref) | copy-start | bytes 1179652
  52.6 6.0 %collective-permute-start.4 = (bf16[8,64,384]{2,1,0:T(8,128)(2,1)S(1)}, bf16[8,64,384]{2,1,0:T(8,128)(2,1)S(1)}, u32[]{:S(2)}, u32[]{:S(2)}) collective-permute-start(bf16[8,64,384]{2,1,0:T(8,128)(2,1)S(1)} %get-tuple-element.14), channel_id=1, source_target_pairs={{0,1},{1,0},{2,3},{3,2},{4,5},{5,4},{6,7},{7,6},{8,9},{9,8},{10,11... | collective-permute-start | bytes 1179656 | tf_op jit(solution)/shard_map/ppermute | solution.py:243

commit v2 on v0

v2 whole, which is shorter than its diff:
```python
import functools

import jax
import jax.numpy as jnp
import numpy as np
from jax import lax
from jax.experimental import pallas as pl
from jax.experimental.pallas import tpu as pltpu
from jax.sharding import PartitionSpec as P

LANES = 128
EDGE = 64
F = 256
POINTS = 2 * F - 1
WIDE = 512
REACH = 832


def halves(matrix):
    high = matrix.astype(jnp.bfloat16)
    low = (matrix - high.astype(np.float64)).astype(jnp.bfloat16)
    return np.stack([high, low])


def angles(samples):
    steps = np.outer(np.arange(samples), np.arange(F)) % POINTS
    return 2.0 * np.pi * steps / POINTS


def forward_matrix(samples, rows):
    turn = angles(samples)
    full = np.zeros((rows, 2 * F))
    full[:samples] = np.concatenate([np.cos(turn), np.sin(turn)], axis=1)
    return full


def inverse_matrix(samples):
    turn = angles(samples).T
    weight = np.full((F, 1), 2.0 / POINTS)
    weight[0] = 1.0 / POINTS
    return np.concatenate([weight * np.cos(turn), -weight * np.sin(turn)], axis=0)


def pack(edge):
    half = edge.shape[0] // 2
    return jnp.concatenate([edge[:half], edge[half:]], axis=1)


def rolled(row, rows, shift):
    wide = jnp.broadcast_to(row, (rows, row.shape[1]))
    return pltpu.roll(wide, shift % row.shape[1], 1, stride=1, stride_axis=0)


def toeplitz_kernel(samples, taps_ref, toep_ref):
    taps = taps_ref.shape[1]
    t = lax.axis_index("tm")
    last = lax.axis_size("tm") - 1
    rest = (taps - 1) % 8
    reach = taps - 1 - rest
    tap = lax.broadcasted_iota(jnp.int32, (taps, WIDE), 0)
    lane = lax.broadcasted_iota(jnp.int32, (taps, WIDE), 1)
    place = (lane == rest - tap) | (lane == rest - tap + WIDE)
    picked = jnp.broadcast_to(taps_ref[...], (8, taps))
    row = jnp.dot(picked, place.astype(jnp.bfloat16), preferred_element_type=jnp.float32)[:1]
    begin = jnp.where(t == 0, taps // 2, 0)
    end = samples + jnp.where(t == last, taps // 2, taps - 1)
    column = lax.broadcasted_iota(jnp.int32, (1, WIDE), 1)
    keep = (column >= begin) & (column < end)
    toep_ref[:samples] = jnp.where(keep, rolled(row, samples, reach), 0.0).astype(jnp.bfloat16)
    toep_ref[samples : samples + EDGE] = jnp.where(keep, rolled(row, EDGE, reach - EDGE), 0.0).astype(jnp.bfloat16)
    toep_ref[samples + EDGE :] = jnp.where(keep, rolled(row, EDGE, reach + samples), 0.0).astype(jnp.bfloat16)


def score_kernel(
    chunks,
    offsets_ref,
    toep_ref,
    sides_ref,
    before_ref,
    before_sides_ref,
    after_ref,
    after_sides_ref,
    raw_hbm,
    white_hbm,
    forward_hbm,
    inverse_hbm,
    spatial_hbm,
    hat_hbm,
    keep_ref,
    send_ref,
    raw_ref,
    white_ref,
    forward_ref,
    inverse_ref,
    spatial_ref,
    hat_ref,
    wide_ref,
    filtered_ref,
    what_ref,
    raw_sem,
    white_sem,
    forward_sem,
    inverse_sem,
    spatial_sem,
    hat_sem,
):
    rows, samples = raw_ref.shape
    groups = offsets_ref.shape[0]
    tile = rows // groups
    band = white_ref.shape[1]
    c = lax.axis_index("chan")
    all_rows = lax.axis_size("chan") * rows
    rank, templates, _ = spatial_ref.shape
    block = templates // chunks

    first = [
        pltpu.make_async_copy(raw_hbm, raw_ref, raw_sem),
        pltpu.make_async_copy(white_hbm, white_ref, white_sem),
        pltpu.make_async_copy(forward_hbm, forward_ref, forward_sem),
    ]
    for copy in first:
        copy.start()
    later = []
    for chunk in range(chunks):
        part = (slice(None), slice(chunk * block, (chunk + 1) * block))
        later.append(
            (
                pltpu.make_async_copy(spatial_hbm.at[part], spatial_ref.at[part], spatial_sem.at[chunk]),
                pltpu.make_async_copy(hat_hbm.at[part], hat_ref.at[part], hat_sem.at[chunk]),
            )
        )
        later[-1][0].start()
        later[-1][1].start()
        if chunk == 0:
            last = pltpu.make_async_copy(inverse_hbm, inverse_ref, inverse_sem)
            last.start()

    def filter_rows(main, sides, begin):
        count = main.shape[0]
        wide_ref[begin : begin + count, :samples] = main[...]
        wide_ref[begin : begin + count, samples:] = sides[...]
        value = jnp.dot(wide_ref[begin : begin + count], toep_ref[...], preferred_element_type=jnp.float32)
        filtered_ref[begin : begin + count] = value.astype(jnp.bfloat16)

    first[0].wait()
    filter_rows(raw_ref, sides_ref, REACH)
    filter_rows(before_ref.at[rows - REACH :], before_sides_ref, 0)
    filter_rows(after_ref.at[:REACH], after_sides_ref, REACH + rows)

    first[1].wait()
    first[2].wait()
    for group in range(groups):
        begin = c * rows + group * tile
        start = begin + tile // 2 - band // 2 + offsets_ref[group] * tile
        start = jnp.clip(start, 0, all_rows - band) - c * rows + REACH
        start = pl.multiple_of(jnp.clip(start, 0, 2 * REACH + rows - band), EDGE)
        body = slice(group * tile, (group + 1) * tile)
        value = jnp.dot(white_ref[body], filtered_ref[pl.ds(start, band)], preferred_element_type=jnp.float32)
        value = value.astype(jnp.bfloat16)
        hat = jnp.dot(value, forward_ref[0], preferred_element_type=jnp.float32)
        hat += jnp.dot(value, forward_ref[1], preferred_element_type=jnp.float32)
        what_ref[body] = hat.astype(jnp.bfloat16)

    own = keep_ref.shape[1]
    even_core = c % 2 == 0
    last.wait()
    for chunk in range(chunks):
        later[chunk][0].wait()
        later[chunk][1].wait()
        body = slice(chunk * block, (chunk + 1) * block)
        weights = spatial_ref[:, body].reshape(rank * block, rows)
        product = jnp.dot(weights, what_ref[...], preferred_element_type=jnp.float32)
        real = imag = 0.0
        for r in range(rank):
            a = product[r * block : (r + 1) * block, :F]
            b = product[r * block : (r + 1) * block, F:]
            x = hat_ref[r, body, :F]
            y = hat_ref[r, body, F:]
            real += a * x + b * y
            imag += a * y - b * x
        both = jnp.concatenate([real, imag], axis=1).astype(jnp.bfloat16)
        value = jnp.dot(both, inverse_ref[0], preferred_element_type=jnp.float32)
        value += jnp.dot(both, inverse_ref[1], preferred_element_type=jnp.float32)
        pairs = block // (2 * own)
        for pair in range(pairs):
            even = value[2 * pair * own : (2 * pair + 1) * own]
            odd = value[(2 * pair + 1) * own : (2 * pair + 2) * own]
            keep_ref[chunk * pairs + pair] = jnp.where(even_core, even, odd)
            send_ref[chunk * pairs + pair] = jnp.where(even_core, odd, even).astype(jnp.bfloat16)


def local(raw, band_taps, whitening, band_offsets, spatial, temporal):
    rows, samples = raw.shape
    taps = band_taps.shape[0]
    band = whitening.shape[1]
    templates, rank, _ = spatial.shape
    window = samples + taps - 1
    n_tm = lax.axis_size("tm")
    n_chan = lax.axis_size("chan")
    own = templates // n_chan
    half = rows // 2
    chunks = 4

    up = [(i, i + 1) for i in range(n_chan - 1)]
    down = [(j, i) for i, j in up]
    up_tm = [(i, i + 1) for i in range(n_tm - 1)]
    down_tm = [(j, i) for i, j in up_tm]
    before = lax.ppermute(raw, "chan", up)
    after = lax.ppermute(raw, "chan", down)
    prev = lax.ppermute(pack(raw[:, samples - EDGE :]), "tm", up_tm)
    follow = lax.ppermute(pack(raw[:, :EDGE]), "tm", down_tm)
    sides = jnp.concatenate(
        [
            jnp.concatenate([prev[:, :EDGE], follow[:, :EDGE]], axis=1),
            jnp.concatenate([prev[:, EDGE:], follow[:, EDGE:]], axis=1),
        ],
        axis=0,
    )
    before_sides = lax.ppermute(sides[rows - REACH :], "chan", up)
    after_sides = lax.ppermute(sides[:REACH], "chan", down)

    vmem = pl.BlockSpec(memory_space=pltpu.VMEM)
    smem = pl.BlockSpec(memory_space=pltpu.SMEM)
    hbm = pl.BlockSpec(memory_space=pltpu.MemorySpace.HBM)
    toep = pl.pallas_call(
        functools.partial(toeplitz_kernel, samples),
        out_shape=jax.ShapeDtypeStruct((WIDE, WIDE), jnp.bfloat16),
        in_specs=[vmem],
        out_specs=vmem,
        cost_estimate=pl.CostEstimate(flops=WIDE * WIDE * 64, bytes_accessed=WIDE * WIDE * 4, transcendentals=0),
        compiler_params=pltpu.CompilerParams(vmem_limit_bytes=8 << 20),
        name="toeplitz",
    )(band_taps[None])
    hat = jnp.einsum(
        "krj,jf->rkf",
        temporal,
        jnp.asarray(forward_matrix(taps, taps), jnp.float32),
        precision=lax.Precision.HIGH,
    )
    forward = jnp.asarray(halves(forward_matrix(window, WIDE)))
    inverse = jnp.asarray(halves(inverse_matrix(samples)))

    out_shape = (n_chan // 2, own, samples)
    work = 2 * (2 * REACH + rows) * WIDE * WIDE + 2 * rows * WIDE * (band + 2 * WIDE) + 2 * templates * WIDE * (rank * rows + 2 * samples)
    keep, send = pl.pallas_call(
        functools.partial(score_kernel, chunks),
        out_shape=(
            jax.ShapeDtypeStruct(out_shape, jnp.float32),
            jax.ShapeDtypeStruct(out_shape, jnp.bfloat16),
        ),
        in_specs=[smem] + [vmem] * 6 + [hbm] * 6,
        out_specs=(vmem, vmem),
        scratch_shapes=[
            pltpu.VMEM((rows, samples), jnp.bfloat16),
            pltpu.VMEM((rows, band), jnp.bfloat16),
            pltpu.VMEM(forward.shape, jnp.bfloat16),
            pltpu.VMEM(inverse.shape, jnp.bfloat16),
            pltpu.VMEM((rank, templates, rows), jnp.bfloat16),
            pltpu.VMEM((rank, templates, 2 * F), jnp.float32),
            pltpu.VMEM((2 * REACH + rows, WIDE), jnp.bfloat16),
            pltpu.VMEM((2 * REACH + rows, WIDE), jnp.bfloat16),
            pltpu.VMEM((rows, 2 * F), jnp.bfloat16),
            pltpu.SemaphoreType.DMA,
            pltpu.SemaphoreType.DMA,
            pltpu.SemaphoreType.DMA,
            pltpu.SemaphoreType.DMA,
            pltpu.SemaphoreType.DMA((chunks,)),
            pltpu.SemaphoreType.DMA((chunks,)),
        ],
        cost_estimate=pl.CostEstimate(flops=work, bytes_accessed=24 << 20, transcendentals=0),
        compiler_params=pltpu.CompilerParams(vmem_limit_bytes=44 << 20),
        name="score",
    )(band_offsets, toep, sides, before, before_sides, after, after_sides, raw, whitening, forward, inverse, spatial.transpose(1, 0, 2), hat)

    other = lax.ppermute(send, "chan", [(i, i ^ 1) for i in range(n_chan)])
    both = (keep + other.astype(jnp.float32)).astype(jnp.bfloat16)
    members = [[2 * i + core for i in range(n_chan // 2)] for core in range(2)]
    shares = lax.all_to_all(both, "chan", 0, 0, axis_index_groups=members)
    return jnp.sum(shares.astype(jnp.float32), axis=0)


def solution(mesh):
    placed = (P("chan", "tm"), P(), P("chan", None), P("chan"), P(None, None, "chan"), P())
    return jax.shard_map(local, mesh=mesh, in_specs=placed, out_specs=P("chan", "tm"), check_vma=False)
```

time: 428 us -> 66.5 us (0.16); the launches traced: 420 us -> 65.5 us
  waiting for transfers between devices: 146 us -> 11.2 us
  local copies, waits for them, and re-layouts: 134 us -> 2.31 us
  other arithmetic: 57.5 us -> 1.15 us
  loops' own time: 25.6 us -> 0 us
  matrix products: 26.3 us -> 5.51 us
  blocking collectives: 0 us -> 15.1 us
  between operations: 14.4 us -> 0.2 us
  Pallas kernels: 0 us -> 11.6 us
    unnamed x2 -> x0, waiting for transfers between devices: 124 us -> none
    unnamed x68 -> x14, local copies, waits for them, and re-layouts: 77.8 us -> 0.67 us
    reduce_sum x8 -> x1, other arithmetic: 51.1 us -> 0.69 us  [local(): return jnp.sum(shares.astype(jnp.float32), axis=0)]
    another operation x1 -> x0, loops' own time: 25.6 us -> none  [whiten(): stacked = lax.map(one_group, jnp.arange(groups, dtype=jnp.int32))]
    mul x61 -> x0, local copies, waits for them, and re-layouts: 25 us -> none  [time_filter(): total = total + jnp.sum(piece * weight, axis=1)]
    dot_general x10 -> x1, matrix products: 26.3 us -> 5.51 us  [local(): jnp.einsum('krj,jf->rkf', temporal, jnp.asarray(forward_matrix(taps, taps...]
    all_to_all x0 -> x1, blocking collectives: none -> 15.1 us  [local(): shares = lax.all_to_all(both, 'chan', 0, 0, axis_index_groups=members)]
    pallas_call x0 -> x2, Pallas kernels: none -> 11.6 us  [the longest x1 11.3 us: local(): pl.pallas_call(functools.partial(score_kernel, chunks), out_shape=(jax.Sh...]
  transfers between devices with their start and end apart: 7 -> 7, of which waited for: 6 -> 2; matrix products, arithmetic and copies ran while one was open for 8% -> 9% of each run, Pallas kernels for 0% -> 0%
where the time goes in v2:
time: 66.5 us; the launch traced here: 65.5 us
  starting transfers between devices  18.3 us (28%)
  blocking collectives  15.1 us (23%)
  Pallas kernels  11.6 us (17%)
  waiting for transfers between devices  11.2 us (17%)
  matrix products  5.51 us (8%)
  local copies, waits for them, and re-layouts  2.31 us (3%)
  other arithmetic  1.15 us (2%)
    all_to_all x1, blocking collectives, local(): shares = lax.all_to_all(both, 'chan', 0, 0, axis_index_groups=members)  15.1 us
    pallas_call x1, Pallas kernels, local(): pl.pallas_call(functools.partial(score_kernel, chunks), out_shape=(jax.Sh...  11.3 us
    ppermute x1, waiting for transfers between devices, local(): prev = lax.ppermute(pack(raw[:, samples - EDGE:]), 'tm', up_tm)  9.89 us
    dot_general x1, matrix products, local(): jnp.einsum('krj,jf->rkf', temporal, jnp.asarray(forward_matrix(taps, taps...  5.51 us
    ppermute x1, starting transfers between devices, local(): before_sides = lax.ppermute(sides[rows - REACH:], 'chan', up)  4.81 us
    ppermute x1, starting transfers between devices, local(): follow = lax.ppermute(pack(raw[:, :EDGE]), 'tm', down_tm)  4.01 us
    ppermute x1, starting transfers between devices, local(): other = lax.ppermute(send, 'chan', [(i, i ^ 1) for i in range(n_chan)])  3.5 us
    ppermute x1, starting transfers between devices, local(): prev = lax.ppermute(pack(raw[:, samples - EDGE:]), 'tm', up_tm)  1.92 us
  transfers between devices with their start and end apart: 7, of which 2 were waited for; matrix products, arithmetic and copies ran while one was open for 9% of the time, Pallas kernels for 0%

profile of v2, /device:TPU:128, one launch (start us, length us, event | category | flops | bytes accessed | tf_op | source)
XLA Modules:
  0.0 65.5 jit_solution(2233011134946079570)
XLA Ops:
  0.0 0.0 copy-start
  0.0 0.0 copy-start.4
  0.0 1.4 %fusion = (bf16[512,64]{1,0:T(8,128)(2,1)S(1)}, bf16[512,64]{1,0:T(8,128)(2,1)S(1)}, bf16[512,64]{1,0:T(8,128)(2,1)S(1)}, bf16[512,64]{1,0:T(8,128)(2,1)S(1)}) fusion(bf16[1024,384]{1,0:T(8,128)(2,1)} %raw_hbm.1), kind=kLoop, calls=%fused_computation.6 | loop fusion | bytes 524288 | tf_op jit(solution)/shard_map/slice | solution.py:46
  1.4 0.1 pad_maximum_fusion.1
  1.5 4.0 %collective-permute-start.1 = (bf16[512,128]{1,0:T(8,128)(2,1)S(1)}, bf16[512,128]{1,0:T(8,128)(2,1)S(1)}, u32[]{:S(2)}, u32[]{:S(2)}) collective-permute-start(bf16[512,128]{1,0:T(8,128)(2,1)S(1)} %pad_maximum_fusion.1), channel_id=1, source_target_pairs={{16,0},{32,16},{48,32},{64,48},{80,64},{96,80},{112,96},{128,112},... | collective-permute-start | bytes 393224 | tf_op jit(solution)/shard_map/ppermute | solution.py:211
  5.5 1.5 %collective-permute-start.2 = (bf16[1024,384]{1,0:T(8,128)(2,1)}, bf16[1024,384]{1,0:T(8,128)(2,1)S(1)}, u32[]{:S(2)}, u32[]{:S(2)}) collective-permute-start(bf16[1024,384]{1,0:T(8,128)(2,1)} %raw_hbm.1), channel_id=1, source_target_pairs={{0,1},{1,2},{2,3},{3,4},{4,5},{5,6},{6,7},{7,8},{8,9},{9,10},{10,1... | collective-permute-start | bytes 2359304 | tf_op jit(solution)/shard_map/ppermute | solution.py:208
  7.1 1.3 %collective-permute-start.4 = (bf16[1024,384]{1,0:T(8,128)(2,1)}, bf16[1024,384]{1,0:T(8,128)(2,1)S(1)}, u32[]{:S(2)}, u32[]{:S(2)}) collective-permute-start(bf16[1024,384]{1,0:T(8,128)(2,1)} %raw_hbm.1), channel_id=1, source_target_pairs={{1,0},{2,1},{3,2},{4,3},{5,4},{6,5},{7,6},{8,7},{9,8},{10,9},{11,1... | collective-permute-start | bytes 2359304 | tf_op jit(solution)/shard_map/ppermute | solution.py:209
  8.4 0.1 pad_maximum_fusion
  8.5 1.9 %collective-permute-start = (bf16[512,128]{1,0:T(8,128)(2,1)S(1)}, bf16[512,128]{1,0:T(8,128)(2,1)S(1)}, u32[]{:S(2)}, u32[]{:S(2)}) collective-permute-start(bf16[512,128]{1,0:T(8,128)(2,1)S(1)} %pad_maximum_fusion), channel_id=1, source_target_pairs={{0,16},{16,32},{32,48},{48,64},{64,80},{80,96},{96,112},{112,128},... | collective-permute-start | bytes 393224 | tf_op jit(solution)/shard_map/ppermute | solution.py:210
  10.4 0.0 copy-start.2
  10.4 0.6 copy-done.2
  11.1 0.3 toeplitz.1.toep_ref
  11.3 0.0 collective-permute-done.1
  11.4 0.1 fusion.3
  11.5 9.9 %collective-permute-done = bf16[512,128]{1,0:T(8,128)(2,1)S(1)} collective-permute-done((bf16[512,128]{1,0:T(8,128)(2,1)S(1)}, bf16[512,128]{1,0:T(8,128)(2,1)S(1)}, u32[]{:S(2)}, u32[]{:S(2)}) %collective-permute-start) | collective-permute-done | bytes 131104 | tf_op jit(solution)/shard_map/ppermute | solution.py:210
  21.4 0.1 fusion.2
  21.5 0.1 maximum_maximum_fusion.sides_ref
  21.7 1.3 %collective-permute-start.5 = (bf16[832,128]{1,0:T(8,128)(2,1)S(1)}, bf16[832,128]{1,0:T(8,128)(2,1)S(1)}, u32[]{:S(2)}, u32[]{:S(2)}) collective-permute-start(bf16[832,128]{1,0:T(8,128)(2,1)S(1)} %get-tuple-element.13), channel_id=1, source_target_pairs={{1,0},{2,1},{3,2},{4,3},{5,4},{6,5},{7,6},{8,7},{9,8},{10,9},{11,1... | collective-permute-start | bytes 638984 | tf_op jit(solution)/shard_map/ppermute | solution.py:220
  23.0 4.8 %collective-permute-start.3 = (bf16[832,128]{1,0:T(8,128)(2,1)S(1)}, bf16[832,128]{1,0:T(8,128)(2,1)S(1)}, u32[]{:S(2)}, u32[]{:S(2)}) collective-permute-start(bf16[832,128]{1,0:T(8,128)(2,1)S(1)} %get-tuple-element.14), channel_id=1, source_target_pairs={{0,1},{1,2},{2,3},{3,4},{4,5},{5,6},{6,7},{7,8},{8,9},{9,10},{10,1... | collective-permute-start | bytes 638984 | tf_op jit(solution)/shard_map/ppermute | solution.py:219
  27.8 0.0 copy-done
  27.8 5.5 %convolution_bitcast_fusion.hat_hbm = f32[3,1024,512]{2,1,0:T(8,128)} fusion(f32[61,512,1]{1,0,2:T(8,128)} %constant.12, f32[1024,3,61]{0,2,1:T(8,128)S(1)} %copy-done), kind=kOutput, calls=%fused_computation | convolution fusion | flops 575668224 | bytes 7165952 | tf_op jit(solution)/shard_map/krj,jf->rkf/dot_general | solution.py:234
  33.3 0.0 collective-permute-done.5.after_sides_ref
  33.3 0.0 collective-permute-done.3.before_sides_ref
  33.3 0.0 collective-permute-done.2.before_ref
  33.3 0.0 collective-permute-done.4.after_ref
  33.3 0.0 copy-done.5
  33.4 11.3 %score.1 = (f32[8,64,384]{2,1,0:T(8,128)S(1)}, bf16[8,64,384]{2,1,0:T(8,128)(2,1)S(1)}) custom-call(s32[8]{0:T(128)S(1)} %copy-done.4, bf16[512,512]{1,0:T(8,128)(2,1)S(1)} %toeplitz.1.toep_ref, bf16[1024,128]{1,0:T(8,128)(2,1)S(1)} %maximum_maximum_fusion.sides_ref, bf16[1024,384]{1,0:T(8,128)(2,1)S(1)} %collective-permute-done.2.before_ref, ...), custom_call_target="tpu_custom_call" | custom-call | flops 7583301632 | bytes 25165824 | tf_op jit(solution)/shard_map/score/pallas_call | solution.py:245
  44.7 3.5 %collective-permute-start.6 = (bf16[8,64,384]{2,1,0:T(8,128)(2,1)S(1)}, bf16[8,64,384]{2,1,0:T(8,128)(2,1)S(1)}, u32[]{:S(2)}, u32[]{:S(2)}) collective-permute-start(bf16[8,64,384]{2,1,0:T(8,128)(2,1)S(1)} %get-tuple-element.8), channel_id=1, source_target_pairs={{0,1},{1,0},{2,3},{3,2},{4,5},{5,4},{6,7},{7,6},{8,9},{9,8},{10,11... | collective-permute-start | bytes 1179656 | tf_op jit(solution)/shard_map/ppermute | solution.py:275
  48.2 1.3 %collective-permute-done.6 = bf16[8,64,384]{2,1,0:T(8,128)(2,1)S(1)} collective-permute-done((bf16[8,64,384]{2,1,0:T(8,128)(2,1)S(1)}, bf16[8,64,384]{2,1,0:T(8,128)(2,1)S(1)}, u32[]{:S(2)}, u32[]{:S(2)}) %collective-permute-start.6) | collective-permute-done | bytes 393248 | tf_op jit(solution)/shard_map/ppermute | solution.py:275
  49.6 0.1 add_convert_fusion
  49.7 15.1 %all_to_all.5 = bf16[8,64,384]{2,1,0:T(8,128)(2,1)S(1)} all-to-all(bf16[8,64,384]{2,1,0:T(8,128)(2,1)S(1)} %add_convert_fusion), channel_id=1, replica_groups={{0,2,4,6,8,10,12,14},{1,3,5,7,9,11,13,15},{16,18,20,22,24,26,28,30},{17..., dimensions={0} | all-to-all | bytes 786432 | tf_op jit(solution)/shard_map/all_to_all | solution.py:278
  64.8 0.7 %convert_reduce_fusion = f32[64,384]{1,0:T(8,128)} fusion(bf16[8,64,384]{2,1,0:T(8,128)(2,1)S(1)} %all_to_all.5), kind=kLoop, calls=%fused_computation.1 | loop fusion | flops 368640 | bytes 491520 | tf_op jit(solution)/shard_map/reduce_sum | solution.py:279
  (9 shorter events, 0.0 us)
Async XLA Ops:
  0.0 27.8 %copy-start = (f32[1024,3,61]{0,2,1:T(8,128)S(1)}, f32[1024,3,61]{0,2,1:T(8,128)}, u32[]{:S(2)}) copy-start(f32[1024,3,61]{0,2,1:T(8,128)} %param.14) | copy-start | bytes 2248708
  0.0 33.3 %copy-start.5 = (bf16[2,512,512]{2,1,0:T(8,128)(2,1)S(1)}, bf16[2,512,512]{2,1,0:T(8,128)(2,1)}, u32[]{:S(2)}) copy-start(bf16[2,512,512]{2,1,0:T(8,128)(2,1)} %constant.9.clone.forward_hbm) | copy-start | bytes 3145732
  0.0 33.3 %copy-start.1 = (bf16[1024,384]{1,0:T(8,128)(2,1)S(1)}, bf16[1024,384]{1,0:T(8,128)(2,1)}, u32[]{:S(2)}) copy-start(bf16[1024,384]{1,0:T(8,128)(2,1)} %raw_hbm.1) | copy-start | bytes 2359300
  0.0 33.3 %copy-start.4 = (s32[8]{0:T(128)S(1)}, s32[8]{0:T(128)}, u32[]{:S(2)}) copy-start(s32[8]{0:T(128)} %offsets_ref.1) | copy-start | bytes 100
  1.5 9.8 %collective-permute-start.1 = (bf16[512,128]{1,0:T(8,128)(2,1)S(1)}, bf16[512,128]{1,0:T(8,128)(2,1)S(1)}, u32[]{:S(2)}, u32[]{:S(2)}) collective-permute-start(bf16[512,128]{1,0:T(8,128)(2,1)S(1)} %pad_maximum_fusion.1), channel_id=1, source_target_pairs={{16,0},{32,16},{48,32},{64,48},{80,64},{96,80},{112,96},{128,112},... | collective-permute-start | bytes 393224 | tf_op jit(solution)/shard_map/ppermute | solution.py:211
  5.5 27.8 %collective-permute-start.2 = (bf16[1024,384]{1,0:T(8,128)(2,1)}, bf16[1024,384]{1,0:T(8,128)(2,1)S(1)}, u32[]{:S(2)}, u32[]{:S(2)}) collective-permute-start(bf16[1024,384]{1,0:T(8,128)(2,1)} %raw_hbm.1), channel_id=1, source_target_pairs={{0,1},{1,2},{2,3},{3,4},{4,5},{5,6},{6,7},{7,8},{8,9},{9,10},{10,1... | collective-permute-start | bytes 2359304 | tf_op jit(solution)/shard_map/ppermute | solution.py:208
  7.1 26.3 %collective-permute-start.4 = (bf16[1024,384]{1,0:T(8,128)(2,1)}, bf16[1024,384]{1,0:T(8,128)(2,1)S(1)}, u32[]{:S(2)}, u32[]{:S(2)}) collective-permute-start(bf16[1024,384]{1,0:T(8,128)(2,1)} %raw_hbm.1), channel_id=1, source_target_pairs={{1,0},{2,1},{3,2},{4,3},{5,4},{6,5},{7,6},{8,7},{9,8},{10,9},{11,1... | collective-permute-start | bytes 2359304 | tf_op jit(solution)/shard_map/ppermute | solution.py:209
  8.5 12.9 %collective-permute-start = (bf16[512,128]{1,0:T(8,128)(2,1)S(1)}, bf16[512,128]{1,0:T(8,128)(2,1)S(1)}, u32[]{:S(2)}, u32[]{:S(2)}) collective-permute-start(bf16[512,128]{1,0:T(8,128)(2,1)S(1)} %pad_maximum_fusion), channel_id=1, source_target_pairs={{0,16},{16,32},{32,48},{48,64},{64,80},{80,96},{96,112},{112,128},... | collective-permute-start | bytes 393224 | tf_op jit(solution)/shard_map/ppermute | solution.py:210
  10.4 0.7 %copy-start.2 = (bf16[61]{0:T(256)(128)(2,1)S(1)}, bf16[61]{0:T(256)(128)(2,1)}, u32[]{:S(2)}) copy-start(bf16[61]{0:T(256)(128)(2,1)} %param.10) | copy-start | bytes 370
  11.1 22.3 %copy-start.3 = (bf16[1024,1024]{1,0:T(8,128)(2,1)S(1)}, bf16[1024,1024]{1,0:T(8,128)(2,1)}, u32[]{:S(2)}) copy-start(bf16[1024,1024]{1,0:T(8,128)(2,1)} %white_hbm.1) | copy-start | bytes 6291460
  11.1 22.3 %copy-start.6 = (bf16[2,512,384]{2,1,0:T(8,128)(2,1)S(1)}, bf16[2,512,384]{2,1,0:T(8,128)(2,1)}, u32[]{:S(2)}) copy-start(bf16[2,512,384]{2,1,0:T(8,128)(2,1)} %constant.10.clone.inverse_hbm) | copy-start | bytes 2359300
  21.7 11.6 %collective-permute-start.5 = (bf16[832,128]{1,0:T(8,128)(2,1)S(1)}, bf16[832,128]{1,0:T(8,128)(2,1)S(1)}, u32[]{:S(2)}, u32[]{:S(2)}) collective-permute-start(bf16[832,128]{1,0:T(8,128)(2,1)S(1)} %get-tuple-element.13), channel_id=1, source_target_pairs={{1,0},{2,1},{3,2},{4,3},{5,4},{6,5},{7,6},{8,7},{9,8},{10,9},{11,1... | collective-permute-start | bytes 638984 | tf_op jit(solution)/shard_map/ppermute | solution.py:220
  23.0 10.4 %collective-permute-start.3 = (bf16[832,128]{1,0:T(8,128)(2,1)S(1)}, bf16[832,128]{1,0:T(8,128)(2,1)S(1)}, u32[]{:S(2)}, u32[]{:S(2)}) collective-permute-start(bf16[832,128]{1,0:T(8,128)(2,1)S(1)} %get-tuple-element.14), channel_id=1, source_target_pairs={{0,1},{1,2},{2,3},{3,4},{4,5},{5,6},{6,7},{7,8},{8,9},{9,10},{10,1... | collective-permute-start | bytes 638984 | tf_op jit(solution)/shard_map/ppermute | solution.py:219
  44.7 4.9 %collective-permute-start.6 = (bf16[8,64,384]{2,1,0:T(8,128)(2,1)S(1)}, bf16[8,64,384]{2,1,0:T(8,128)(2,1)S(1)}, u32[]{:S(2)}, u32[]{:S(2)}) collective-permute-start(bf16[8,64,384]{2,1,0:T(8,128)(2,1)S(1)} %get-tuple-element.8), channel_id=1, source_target_pairs={{0,1},{1,0},{2,3},{3,2},{4,5},{5,4},{6,7},{7,6},{8,9},{9,8},{10,11... | collective-permute-start | bytes 1179656 | tf_op jit(solution)/shard_map/ppermute | solution.py:275

commit v3 on v2

--- a/solution.py
+++ b/solution.py
@@ -34,16 +34,13 @@
     return full
 
 
-def inverse_matrix(samples):
-    turn = angles(samples).T
+def inverse_matrix(samples, reach):
+    place = np.concatenate([np.arange(samples + EDGE), np.arange(-EDGE, 0)])
+    used = (place >= -reach) & (place < samples + reach)
+    turn = 2.0 * np.pi * (np.outer(np.arange(F), place) % POINTS) / POINTS
     weight = np.full((F, 1), 2.0 / POINTS)
     weight[0] = 1.0 / POINTS
-    return np.concatenate([weight * np.cos(turn), -weight * np.sin(turn)], axis=0)
-
-
-def pack(edge):
-    half = edge.shape[0] // 2
-    return jnp.concatenate([edge[:half], edge[half:]], axis=1)
+    return np.concatenate([weight * np.cos(turn), -weight * np.sin(turn)], axis=0) * used
 
 
 def rolled(row, rows, shift):
@@ -66,20 +63,15 @@
     end = samples + jnp.where(t == last, taps // 2, taps - 1)
     column = lax.broadcasted_iota(jnp.int32, (1, WIDE), 1)
     keep = (column >= begin) & (column < end)
-    toep_ref[:samples] = jnp.where(keep, rolled(row, samples, reach), 0.0).astype(jnp.bfloat16)
-    toep_ref[samples : samples + EDGE] = jnp.where(keep, rolled(row, EDGE, reach - EDGE), 0.0).astype(jnp.bfloat16)
-    toep_ref[samples + EDGE :] = jnp.where(keep, rolled(row, EDGE, reach + samples), 0.0).astype(jnp.bfloat16)
+    toep_ref[...] = jnp.where(keep, rolled(row, samples, reach), 0.0).astype(jnp.bfloat16)
 
 
 def score_kernel(
     chunks,
     offsets_ref,
     toep_ref,
-    sides_ref,
     before_ref,
-    before_sides_ref,
     after_ref,
-    after_sides_ref,
     raw_hbm,
     white_hbm,
     forward_hbm,
@@ -94,7 +86,6 @@
     inverse_ref,
     spatial_ref,
     hat_ref,
-    wide_ref,
     filtered_ref,
     what_ref,
     raw_sem,
@@ -135,17 +126,14 @@
             last = pltpu.make_async_copy(inverse_hbm, inverse_ref, inverse_sem)
             last.start()
 
-    def filter_rows(main, sides, begin):
-        count = main.shape[0]
-        wide_ref[begin : begin + count, :samples] = main[...]
-        wide_ref[begin : begin + count, samples:] = sides[...]
-        value = jnp.dot(wide_ref[begin : begin + count], toep_ref[...], preferred_element_type=jnp.float32)
-        filtered_ref[begin : begin + count] = value.astype(jnp.bfloat16)
+    def filter_rows(main, begin):
+        value = jnp.dot(main[...], toep_ref[...], preferred_element_type=jnp.float32)
+        filtered_ref[begin : begin + main.shape[0]] = value.astype(jnp.bfloat16)
 
     first[0].wait()
-    filter_rows(raw_ref, sides_ref, REACH)
-    filter_rows(before_ref.at[rows - REACH :], before_sides_ref, 0)
-    filter_rows(after_ref.at[:REACH], after_sides_ref, REACH + rows)
+    filter_rows(raw_ref, REACH)
+    filter_rows(before_ref, 0)
+    filter_rows(after_ref, REACH + rows)
 
     first[1].wait()
     first[2].wait()
@@ -198,33 +186,19 @@
     n_tm = lax.axis_size("tm")
     n_chan = lax.axis_size("chan")
     own = templates // n_chan
-    half = rows // 2
     chunks = 4
 
     up = [(i, i + 1) for i in range(n_chan - 1)]
     down = [(j, i) for i, j in up]
-    up_tm = [(i, i + 1) for i in range(n_tm - 1)]
-    down_tm = [(j, i) for i, j in up_tm]
-    before = lax.ppermute(raw, "chan", up)
-    after = lax.ppermute(raw, "chan", down)
-    prev = lax.ppermute(pack(raw[:, samples - EDGE :]), "tm", up_tm)
-    follow = lax.ppermute(pack(raw[:, :EDGE]), "tm", down_tm)
-    sides = jnp.concatenate(
-        [
-            jnp.concatenate([prev[:, :EDGE], follow[:, :EDGE]], axis=1),
-            jnp.concatenate([prev[:, EDGE:], follow[:, EDGE:]], axis=1),
-        ],
-        axis=0,
-    )
-    before_sides = lax.ppermute(sides[rows - REACH :], "chan", up)
-    after_sides = lax.ppermute(sides[:REACH], "chan", down)
+    before = lax.ppermute(raw[rows - REACH :], "chan", up)
+    after = lax.ppermute(raw[:REACH], "chan", down)
 
     vmem = pl.BlockSpec(memory_space=pltpu.VMEM)
     smem = pl.BlockSpec(memory_space=pltpu.SMEM)
     hbm = pl.BlockSpec(memory_space=pltpu.MemorySpace.HBM)
     toep = pl.pallas_call(
         functools.partial(toeplitz_kernel, samples),
-        out_shape=jax.ShapeDtypeStruct((WIDE, WIDE), jnp.bfloat16),
+        out_shape=jax.ShapeDtypeStruct((samples, WIDE), jnp.bfloat16),
         in_specs=[vmem],
         out_specs=vmem,
         cost_estimate=pl.CostEstimate(flops=WIDE * WIDE * 64, bytes_accessed=WIDE * WIDE * 4, transcendentals=0),
@@ -238,17 +212,17 @@
         precision=lax.Precision.HIGH,
     )
     forward = jnp.asarray(halves(forward_matrix(window, WIDE)))
-    inverse = jnp.asarray(halves(inverse_matrix(samples)))
-
-    out_shape = (n_chan // 2, own, samples)
-    work = 2 * (2 * REACH + rows) * WIDE * WIDE + 2 * rows * WIDE * (band + 2 * WIDE) + 2 * templates * WIDE * (rank * rows + 2 * samples)
+    inverse = jnp.asarray(halves(inverse_matrix(samples, taps - 1)))
+
+    out_shape = (n_chan // 2, own, WIDE)
+    work = 2 * (2 * REACH + rows) * WIDE * samples + 2 * rows * WIDE * (band + 2 * WIDE) + 2 * templates * WIDE * (rank * rows + 2 * WIDE)
     keep, send = pl.pallas_call(
         functools.partial(score_kernel, chunks),
         out_shape=(
             jax.ShapeDtypeStruct(out_shape, jnp.float32),
             jax.ShapeDtypeStruct(out_shape, jnp.bfloat16),
         ),
-        in_specs=[smem] + [vmem] * 6 + [hbm] * 6,
+        in_specs=[smem] + [vmem] * 3 + [hbm] * 6,
         out_specs=(vmem, vmem),
         scratch_shapes=[
             pltpu.VMEM((rows, samples), jnp.bfloat16),
@@ -258,7 +232,6 @@
             pltpu.VMEM((rank, templates, rows), jnp.bfloat16),
             pltpu.VMEM((rank, templates, 2 * F), jnp.float32),
             pltpu.VMEM((2 * REACH + rows, WIDE), jnp.bfloat16),
-            pltpu.VMEM((2 * REACH + rows, WIDE), jnp.bfloat16),
             pltpu.VMEM((rows, 2 * F), jnp.bfloat16),
             pltpu.SemaphoreType.DMA,
             pltpu.SemaphoreType.DMA,
@@ -270,10 +243,24 @@
         cost_estimate=pl.CostEstimate(flops=work, bytes_accessed=24 << 20, transcendentals=0),
         compiler_params=pltpu.CompilerParams(vmem_limit_bytes=44 << 20),
         name="score",
-    )(band_offsets, toep, sides, before, before_sides, after, after_sides, raw, whitening, forward, inverse, spatial.transpose(1, 0, 2), hat)
+    )(band_offsets, toep, before, after, raw, whitening, forward, inverse, spatial.transpose(1, 0, 2), hat)
 
     other = lax.ppermute(send, "chan", [(i, i ^ 1) for i in range(n_chan)])
-    both = (keep + other.astype(jnp.float32)).astype(jnp.bfloat16)
+    total = keep + other.astype(jnp.float32)
+    edges = total[..., samples:].astype(jnp.bfloat16)
+    up_tm = [(i, i + 1) for i in range(n_tm - 1)]
+    down_tm = [(j, i) for i, j in up_tm]
+    prev = lax.ppermute(edges, "tm", up_tm).astype(jnp.float32)
+    follow = lax.ppermute(edges, "tm", down_tm).astype(jnp.float32)
+    low = lax.broadcasted_iota(jnp.int32, (1, 1, LANES), 2) < EDGE
+    both = jnp.concatenate(
+        [
+            total[..., :LANES] + jnp.where(low, prev, 0.0),
+            total[..., LANES : samples - LANES],
+            total[..., samples - LANES : samples] + jnp.where(low, 0.0, follow),
+        ],
+        axis=-1,
+    ).astype(jnp.bfloat16)
     members = [[2 * i + core for i in range(n_chan // 2)] for core in range(2)]
     shares = lax.all_to_all(both, "chan", 0, 0, axis_index_groups=members)
     return jnp.sum(shares.astype(jnp.float32), axis=0)

time: 66.5 us -> 63.7 us (0.958)
  the two profiles are of different devices: /device:TPU:128 before, /device:TPU:88 now
where the time goes in v3:
time: 63.7 us; the launch traced here: 63.5 us
  starting transfers between devices  16.7 us (26%)
  waiting for transfers between devices  13.9 us (22%)
  blocking collectives  12.2 us (19%)
  Pallas kernels  11.6 us (18%)
  matrix products  5.64 us (9%)
  local copies, waits for them, and re-layouts  2.29 us (4%)
  other arithmetic  1.06 us (2%)
    all_to_all x1, blocking collectives, local(): shares = lax.all_to_all(both, 'chan', 0, 0, axis_index_groups=members)  12.2 us
    pallas_call x1, Pallas kernels, local(): pl.pallas_call(functools.partial(score_kernel, chunks), out_shape=(jax.Sh...  11.3 us
    ppermute x1, waiting for transfers between devices, local(): follow = lax.ppermute(edges, 'tm', down_tm).astype(jnp.float32)  8.25 us
    ppermute x1, starting transfers between devices, local(): prev = lax.ppermute(edges, 'tm', up_tm).astype(jnp.float32)  6.06 us
    ppermute x1, starting transfers between devices, local(): other = lax.ppermute(send, 'chan', [(i, i ^ 1) for i in range(n_chan)])  5.66 us
    dot_general x1, matrix products, local(): jnp.einsum('krj,jf->rkf', temporal, jnp.asarray(forward_matrix(taps, taps...  5.64 us
    ppermute x1, waiting for transfers between devices, local(): prev = lax.ppermute(edges, 'tm', up_tm).astype(jnp.float32)  4.07 us
    ppermute x1, starting transfers between devices, local(): follow = lax.ppermute(edges, 'tm', down_tm).astype(jnp.float32)  1.92 us
  transfers between devices with their start and end apart: 5, of which 3 were waited for; matrix products, arithmetic and copies ran while one was open for 9% of the time, Pallas kernels for 0%

profile of v3, /device:TPU:88, one launch (start us, length us, event | category | flops | bytes accessed | tf_op | source)
XLA Modules:
  0.0 63.5 jit_solution(1636305730305813818)
XLA Ops:
  0.0 0.0 copy-start
  0.0 0.0 copy-start.5
  0.0 0.0 copy-start.1
  0.0 0.0 copy-start.4
  0.0 1.6 %fusion.3 = (bf16[832,384]{1,0:T(8,128)(2,1)S(1)}, bf16[832,384]{1,0:T(8,128)(2,1)S(1)}) fusion(bf16[1024,384]{1,0:T(8,128)(2,1)} %raw_hbm.1), kind=kLoop, calls=%fused_computation.10 | loop fusion | bytes 2555904 | tf_op jit(solution)/shard_map/slice | solution.py:194
  1.6 1.8 %collective-permute-start = (bf16[832,384]{1,0:T(8,128)(2,1)S(1)}, bf16[832,384]{1,0:T(8,128)(2,1)S(1)}, u32[]{:S(2)}, u32[]{:S(2)}) collective-permute-start(bf16[832,384]{1,0:T(8,128)(2,1)S(1)} %get-tuple-element.14), channel_id=1, source_target_pairs={{0,1},{1,2},{2,3},{3,4},{4,5},{5,6},{6,7},{7,8},{8,9},{9,10},{10,1... | collective-permute-start | bytes 1916936 | tf_op jit(solution)/shard_map/ppermute | solution.py:193
  3.4 1.3 %collective-permute-start.1 = (bf16[832,384]{1,0:T(8,128)(2,1)S(1)}, bf16[832,384]{1,0:T(8,128)(2,1)S(1)}, u32[]{:S(2)}, u32[]{:S(2)}) collective-permute-start(bf16[832,384]{1,0:T(8,128)(2,1)S(1)} %get-tuple-element.13), channel_id=1, source_target_pairs={{1,0},{2,1},{3,2},{4,3},{5,4},{6,5},{7,6},{8,7},{9,8},{10,9},{11,1... | collective-permute-start | bytes 1916936 | tf_op jit(solution)/shard_map/ppermute | solution.py:194
  4.7 0.0 copy-start.2
  4.7 0.6 %copy-done.2 = bf16[61]{0:T(256)(128)(2,1)S(1)} copy-done((bf16[61]{0:T(256)(128)(2,1)S(1)}, bf16[61]{0:T(256)(128)(2,1)}, u32[]{:S(2)}) %copy-start.2) | copy-done | bytes 146
  5.3 0.2 toeplitz.1.toep_ref
  5.6 0.0 copy-done
  5.6 5.6 %convolution_bitcast_fusion.hat_hbm = f32[3,1024,512]{2,1,0:T(8,128)} fusion(f32[61,512,1]{1,0,2:T(8,128)} %constant.14, f32[1024,3,61]{0,2,1:T(8,128)S(1)} %copy-done), kind=kOutput, calls=%fused_computation | convolution fusion | flops 575668224 | bytes 7165952 | tf_op jit(solution)/shard_map/krj,jf->rkf/dot_general | solution.py:208
  11.2 0.0 collective-permute-done.before_ref
  11.2 0.0 collective-permute-done.1.after_ref
  11.2 0.0 copy-done.5
  11.3 0.0 copy-done.1
  11.3 0.0 copy-done.4
  11.3 0.0 copy-done.3
  11.3 0.0 copy-done.6
  11.3 11.3 %score.1 = (f32[8,64,512]{2,1,0:T(8,128)S(1)}, bf16[8,64,512]{2,1,0:T(8,128)(2,1)S(1)}) custom-call(s32[8]{0:T(128)S(1)} %copy-done.4, bf16[384,512]{1,0:T(8,128)(2,1)S(1)} %toeplitz.1.toep_ref, bf16[832,384]{1,0:T(8,128)(2,1)S(1)} %collective-permute-done.before_ref, bf16[832,384]{1,0:T(8,128)(2,1)S(1)} %collective-permute-done.1.after_ref, ...), custom_call_target="tpu_custom_call" | custom-call | flops 7499415552 | bytes 25165824 | tf_op jit(solution)/shard_map/score/pallas_call | solution.py:219
  22.6 5.7 %collective-permute-start.2 = (bf16[8,64,512]{2,1,0:T(8,128)(2,1)S(1)}, bf16[8,64,512]{2,1,0:T(8,128)(2,1)S(1)}, u32[]{:S(2)}, u32[]{:S(2)}) collective-permute-start(bf16[8,64,512]{2,1,0:T(8,128)(2,1)S(1)} %get-tuple-element.8), channel_id=1, source_target_pairs={{0,1},{1,0},{2,3},{3,2},{4,5},{5,4},{6,7},{7,6},{8,9},{9,8},{10,11... | collective-permute-start | bytes 1572872 | tf_op jit(solution)/shard_map/ppermute | solution.py:248
  28.3 1.5 %collective-permute-done.2 = bf16[8,64,512]{2,1,0:T(8,128)(2,1)S(1)} collective-permute-done((bf16[8,64,512]{2,1,0:T(8,128)(2,1)S(1)}, bf16[8,64,512]{2,1,0:T(8,128)(2,1)S(1)}, u32[]{:S(2)}, u32[]{:S(2)}) %collective-permute-start.2) | collective-permute-done | bytes 524320 | tf_op jit(solution)/shard_map/ppermute | solution.py:248
  29.8 0.2 fusion.2
  30.1 0.1 fusion.4
  30.1 6.1 %collective-permute-start.3 = (bf16[8,64,128]{2,1,0:T(8,128)(2,1)S(1)}, bf16[8,64,128]{2,1,0:T(8,128)(2,1)S(1)}, u32[]{:S(2)}, u32[]{:S(2)}) collective-permute-start(bf16[8,64,128]{2,1,0:T(8,128)(2,1)S(1)} %get-tuple-element.16), channel_id=1, source_target_pairs={{0,16},{16,32},{32,48},{48,64},{64,80},{80,96},{96,112},{112,128},... | collective-permute-start | bytes 393224 | tf_op jit(solution)/shard_map/ppermute | solution.py:253
  36.2 1.9 %collective-permute-start.4 = (bf16[8,64,128]{2,1,0:T(8,128)(2,1)S(1)}, bf16[8,64,128]{2,1,0:T(8,128)(2,1)S(1)}, u32[]{:S(2)}, u32[]{:S(2)}) collective-permute-start(bf16[8,64,128]{2,1,0:T(8,128)(2,1)S(1)} %get-tuple-element.16), channel_id=1, source_target_pairs={{16,0},{32,16},{48,32},{64,48},{80,64},{96,80},{112,96},{128,112},... | collective-permute-start | bytes 393224 | tf_op jit(solution)/shard_map/ppermute | solution.py:254
  38.1 4.1 %collective-permute-done.3 = bf16[8,64,128]{2,1,0:T(8,128)(2,1)S(1)} collective-permute-done((bf16[8,64,128]{2,1,0:T(8,128)(2,1)S(1)}, bf16[8,64,128]{2,1,0:T(8,128)(2,1)S(1)}, u32[]{:S(2)}, u32[]{:S(2)}) %collective-permute-start.3) | collective-permute-done | bytes 131104 | tf_op jit(solution)/shard_map/ppermute | solution.py:253
  42.2 8.3 %collective-permute-done.4 = bf16[8,64,128]{2,1,0:T(8,128)(2,1)S(1)} collective-permute-done((bf16[8,64,128]{2,1,0:T(8,128)(2,1)S(1)}, bf16[8,64,128]{2,1,0:T(8,128)(2,1)S(1)}, u32[]{:S(2)}, u32[]{:S(2)}) %collective-permute-start.4) | collective-permute-done | bytes 131104 | tf_op jit(solution)/shard_map/ppermute | solution.py:254
  50.5 0.1 fusion.1
  50.6 0.1 pad_maximum_fusion
  50.6 12.2 %all_to_all.5 = bf16[8,64,384]{2,1,0:T(8,128)(2,1)S(1)} all-to-all(bf16[8,64,384]{2,1,0:T(8,128)(2,1)S(1)} %pad_maximum_fusion), channel_id=1, replica_groups={{0,2,4,6,8,10,12,14},{1,3,5,7,9,11,13,15},{16,18,20,22,24,26,28,30},{17..., dimensions={0} | all-to-all | bytes 786432 | tf_op jit(solution)/shard_map/all_to_all | solution.py:265
  62.8 0.7 %convert_reduce_fusion = f32[64,384]{1,0:T(8,128)} fusion(bf16[8,64,384]{2,1,0:T(8,128)(2,1)S(1)} %all_to_all.5), kind=kLoop, calls=%fused_computation.2 | loop fusion | flops 368640 | bytes 491520 | tf_op jit(solution)/shard_map/reduce_sum | solution.py:266
  (3 shorter events, 0.0 us)
Async XLA Ops:
  0.0 5.6 %copy-start = (f32[1024,3,61]{0,2,1:T(8,128)S(1)}, f32[1024,3,61]{0,2,1:T(8,128)}, u32[]{:S(2)}) copy-start(f32[1024,3,61]{0,2,1:T(8,128)} %param.14) | copy-start | bytes 2248708
  0.0 11.2 %copy-start.5 = (bf16[2,512,512]{2,1,0:T(8,128)(2,1)S(1)}, bf16[2,512,512]{2,1,0:T(8,128)(2,1)}, u32[]{:S(2)}) copy-start(bf16[2,512,512]{2,1,0:T(8,128)(2,1)} %constant.11.clone.forward_hbm) | copy-start | bytes 3145732
  0.0 11.2 %copy-start.1 = (bf16[1024,384]{1,0:T(8,128)(2,1)S(1)}, bf16[1024,384]{1,0:T(8,128)(2,1)}, u32[]{:S(2)}) copy-start(bf16[1024,384]{1,0:T(8,128)(2,1)} %raw_hbm.1) | copy-start | bytes 2359300
  0.0 11.3 %copy-start.4 = (s32[8]{0:T(128)S(1)}, s32[8]{0:T(128)}, u32[]{:S(2)}) copy-start(s32[8]{0:T(128)} %offsets_ref.1) | copy-start | bytes 100
  1.6 9.7 %collective-permute-start = (bf16[832,384]{1,0:T(8,128)(2,1)S(1)}, bf16[832,384]{1,0:T(8,128)(2,1)S(1)}, u32[]{:S(2)}, u32[]{:S(2)}) collective-permute-start(bf16[832,384]{1,0:T(8,128)(2,1)S(1)} %get-tuple-element.14), channel_id=1, source_target_pairs={{0,1},{1,2},{2,3},{3,4},{4,5},{5,6},{6,7},{7,8},{8,9},{9,10},{10,1... | collective-permute-start | bytes 1916936 | tf_op jit(solution)/shard_map/ppermute | solution.py:193
  3.4 7.9 %collective-permute-start.1 = (bf16[832,384]{1,0:T(8,128)(2,1)S(1)}, bf16[832,384]{1,0:T(8,128)(2,1)S(1)}, u32[]{:S(2)}, u32[]{:S(2)}) collective-permute-start(bf16[832,384]{1,0:T(8,128)(2,1)S(1)} %get-tuple-element.13), channel_id=1, source_target_pairs={{1,0},{2,1},{3,2},{4,3},{5,4},{6,5},{7,6},{8,7},{9,8},{10,9},{11,1... | collective-permute-start | bytes 1916936 | tf_op jit(solution)/shard_map/ppermute | solution.py:194
  4.7 0.7 %copy-start.2 = (bf16[61]{0:T(256)(128)(2,1)S(1)}, bf16[61]{0:T(256)(128)(2,1)}, u32[]{:S(2)}) copy-start(bf16[61]{0:T(256)(128)(2,1)} %param.10) | copy-start | bytes 370
  5.3 5.9 %copy-start.3 = (bf16[1024,1024]{1,0:T(8,128)(2,1)S(1)}, bf16[1024,1024]{1,0:T(8,128)(2,1)}, u32[]{:S(2)}) copy-start(bf16[1024,1024]{1,0:T(8,128)(2,1)} %white_hbm.1) | copy-start | bytes 6291460
  5.3 6.0 %copy-start.6 = (bf16[2,512,512]{2,1,0:T(8,128)(2,1)S(1)}, bf16[2,512,512]{2,1,0:T(8,128)(2,1)}, u32[]{:S(2)}) copy-start(bf16[2,512,512]{2,1,0:T(8,128)(2,1)} %constant.12.clone.inverse_hbm) | copy-start | bytes 3145732
  22.6 7.2 %collective-permute-start.2 = (bf16[8,64,512]{2,1,0:T(8,128)(2,1)S(1)}, bf16[8,64,512]{2,1,0:T(8,128)(2,1)S(1)}, u32[]{:S(2)}, u32[]{:S(2)}) collective-permute-start(bf16[8,64,512]{2,1,0:T(8,128)(2,1)S(1)} %get-tuple-element.8), channel_id=1, source_target_pairs={{0,1},{1,0},{2,3},{3,2},{4,5},{5,4},{6,7},{7,6},{8,9},{9,8},{10,11... | collective-permute-start | bytes 1572872 | tf_op jit(solution)/shard_map/ppermute | solution.py:248
  30.1 12.1 %collective-permute-start.3 = (bf16[8,64,128]{2,1,0:T(8,128)(2,1)S(1)}, bf16[8,64,128]{2,1,0:T(8,128)(2,1)S(1)}, u32[]{:S(2)}, u32[]{:S(2)}) collective-permute-start(bf16[8,64,128]{2,1,0:T(8,128)(2,1)S(1)} %get-tuple-element.16), channel_id=1, source_target_pairs={{0,16},{16,32},{32,48},{48,64},{64,80},{80,96},{96,112},{112,128},... | collective-permute-start | bytes 393224 | tf_op jit(solution)/shard_map/ppermute | solution.py:253
  36.2 14.3 %collective-permute-start.4 = (bf16[8,64,128]{2,1,0:T(8,128)(2,1)S(1)}, bf16[8,64,128]{2,1,0:T(8,128)(2,1)S(1)}, u32[]{:S(2)}, u32[]{:S(2)}) collective-permute-start(bf16[8,64,128]{2,1,0:T(8,128)(2,1)S(1)} %get-tuple-element.16), channel_id=1, source_target_pairs={{16,0},{32,16},{48,32},{64,48},{80,64},{96,80},{112,96},{128,112},... | collective-permute-start | bytes 393224 | tf_op jit(solution)/shard_map/ppermute | solution.py:254

commit v4 on v2

--- a/solution.py
+++ b/solution.py
@@ -13,6 +13,7 @@
 F = 256
 POINTS = 2 * F - 1
 WIDE = 512
+SLOT = 64
 REACH = 832
 
 
@@ -25,6 +26,11 @@
 def angles(samples):
     steps = np.outer(np.arange(samples), np.arange(F)) % POINTS
     return 2.0 * np.pi * steps / POINTS
+
+
+def split_matrix(taps):
+    high, low = halves(forward_matrix(taps, SLOT))
+    return np.concatenate([high, low, high])
 
 
 def forward_matrix(samples, rows):
@@ -51,7 +57,14 @@
     return pltpu.roll(wide, shift % row.shape[1], 1, stride=1, stride_axis=0)
 
 
-def toeplitz_kernel(samples, taps_ref, toep_ref):
+def prepare_kernel(samples, taps_ref, temporal_ref, toep_ref, split_ref):
+    rank, count, templates = temporal_ref.shape
+    blank = jnp.zeros((SLOT - count, templates), jnp.float32)
+    for r in range(rank):
+        value = jnp.concatenate([temporal_ref[r], blank], axis=0)
+        high = value.astype(jnp.bfloat16).astype(jnp.float32)
+        stacked = jnp.concatenate([high, high, value - high], axis=0)
+        split_ref[r] = stacked.T.astype(jnp.bfloat16)
     taps = taps_ref.shape[1]
     t = lax.axis_index("tm")
     last = lax.axis_size("tm") - 1
@@ -80,12 +93,13 @@
     before_sides_ref,
     after_ref,
     after_sides_ref,
+    split_ref,
+    spread_ref,
     raw_hbm,
     white_hbm,
     forward_hbm,
     inverse_hbm,
     spatial_hbm,
-    hat_hbm,
     keep_ref,
     send_ref,
     raw_ref,
@@ -93,7 +107,6 @@
     forward_ref,
     inverse_ref,
     spatial_ref,
-    hat_ref,
     wide_ref,
     filtered_ref,
     what_ref,
@@ -102,7 +115,6 @@
     forward_sem,
     inverse_sem,
     spatial_sem,
-    hat_sem,
 ):
     rows, samples = raw_ref.shape
     groups = offsets_ref.shape[0]
@@ -123,14 +135,8 @@
     later = []
     for chunk in range(chunks):
         part = (slice(None), slice(chunk * block, (chunk + 1) * block))
-        later.append(
-            (
-                pltpu.make_async_copy(spatial_hbm.at[part], spatial_ref.at[part], spatial_sem.at[chunk]),
-                pltpu.make_async_copy(hat_hbm.at[part], hat_ref.at[part], hat_sem.at[chunk]),
-            )
-        )
-        later[-1][0].start()
-        later[-1][1].start()
+        later.append(pltpu.make_async_copy(spatial_hbm.at[part], spatial_ref.at[part], spatial_sem.at[chunk]))
+        later[-1].start()
         if chunk == 0:
             last = pltpu.make_async_copy(inverse_hbm, inverse_ref, inverse_sem)
             last.start()
@@ -144,8 +150,8 @@
 
     first[0].wait()
     filter_rows(raw_ref, sides_ref, REACH)
-    filter_rows(before_ref.at[rows - REACH :], before_sides_ref, 0)
-    filter_rows(after_ref.at[:REACH], after_sides_ref, REACH + rows)
+    filter_rows(before_ref, before_sides_ref, 0)
+    filter_rows(after_ref, after_sides_ref, REACH + rows)
 
     first[1].wait()
     first[2].wait()
@@ -165,17 +171,18 @@
     even_core = c % 2 == 0
     last.wait()
     for chunk in range(chunks):
-        later[chunk][0].wait()
-        later[chunk][1].wait()
+        later[chunk].wait()
         body = slice(chunk * block, (chunk + 1) * block)
         weights = spatial_ref[:, body].reshape(rank * block, rows)
         product = jnp.dot(weights, what_ref[...], preferred_element_type=jnp.float32)
+        split = split_ref[:, body].reshape(rank * block, split_ref.shape[2])
+        hat = jnp.dot(split, spread_ref[...], preferred_element_type=jnp.float32)
         real = imag = 0.0
         for r in range(rank):
             a = product[r * block : (r + 1) * block, :F]
             b = product[r * block : (r + 1) * block, F:]
-            x = hat_ref[r, body, :F]
-            y = hat_ref[r, body, F:]
+            x = hat[r * block : (r + 1) * block, :F]
+            y = hat[r * block : (r + 1) * block, F:]
             real += a * x + b * y
             imag += a * y - b * x
         both = jnp.concatenate([real, imag], axis=1).astype(jnp.bfloat16)
@@ -205,8 +212,8 @@
     down = [(j, i) for i, j in up]
     up_tm = [(i, i + 1) for i in range(n_tm - 1)]
     down_tm = [(j, i) for i, j in up_tm]
-    before = lax.ppermute(raw, "chan", up)
-    after = lax.ppermute(raw, "chan", down)
+    before = lax.ppermute(raw[rows - REACH :], "chan", up)
+    after = lax.ppermute(raw[:REACH], "chan", down)
     prev = lax.ppermute(pack(raw[:, samples - EDGE :]), "tm", up_tm)
     follow = lax.ppermute(pack(raw[:, :EDGE]), "tm", down_tm)
     sides = jnp.concatenate(
@@ -222,33 +229,31 @@
     vmem = pl.BlockSpec(memory_space=pltpu.VMEM)
     smem = pl.BlockSpec(memory_space=pltpu.SMEM)
     hbm = pl.BlockSpec(memory_space=pltpu.MemorySpace.HBM)
-    toep = pl.pallas_call(
-        functools.partial(toeplitz_kernel, samples),
-        out_shape=jax.ShapeDtypeStruct((WIDE, WIDE), jnp.bfloat16),
-        in_specs=[vmem],
-        out_specs=vmem,
-        cost_estimate=pl.CostEstimate(flops=WIDE * WIDE * 64, bytes_accessed=WIDE * WIDE * 4, transcendentals=0),
-        compiler_params=pltpu.CompilerParams(vmem_limit_bytes=8 << 20),
-        name="toeplitz",
-    )(band_taps[None])
-    hat = jnp.einsum(
-        "krj,jf->rkf",
-        temporal,
-        jnp.asarray(forward_matrix(taps, taps), jnp.float32),
-        precision=lax.Precision.HIGH,
-    )
+    toep, split = pl.pallas_call(
+        functools.partial(prepare_kernel, samples),
+        out_shape=(
+            jax.ShapeDtypeStruct((WIDE, WIDE), jnp.bfloat16),
+            jax.ShapeDtypeStruct((rank, templates, 3 * SLOT), jnp.bfloat16),
+        ),
+        in_specs=[vmem, vmem],
+        out_specs=(vmem, vmem),
+        cost_estimate=pl.CostEstimate(flops=WIDE * WIDE * 64, bytes_accessed=4 << 20, transcendentals=0),
+        compiler_params=pltpu.CompilerParams(vmem_limit_bytes=12 << 20),
+        name="prepare",
+    )(band_taps[None], temporal.transpose(1, 2, 0))
+    spread = jnp.asarray(split_matrix(taps))
     forward = jnp.asarray(halves(forward_matrix(window, WIDE)))
     inverse = jnp.asarray(halves(inverse_matrix(samples)))
 
     out_shape = (n_chan // 2, own, samples)
-    work = 2 * (2 * REACH + rows) * WIDE * WIDE + 2 * rows * WIDE * (band + 2 * WIDE) + 2 * templates * WIDE * (rank * rows + 2 * samples)
+    work = 2 * (2 * REACH + rows) * WIDE * WIDE + 2 * rows * WIDE * (band + 2 * WIDE) + 2 * templates * WIDE * (rank * (rows + 3 * SLOT) + 2 * samples)
     keep, send = pl.pallas_call(
         functools.partial(score_kernel, chunks),
         out_shape=(
             jax.ShapeDtypeStruct(out_shape, jnp.float32),
             jax.ShapeDtypeStruct(out_shape, jnp.bfloat16),
         ),
-        in_specs=[smem] + [vmem] * 6 + [hbm] * 6,
+        in_specs=[smem] + [vmem] * 8 + [hbm] * 5,
         out_specs=(vmem, vmem),
         scratch_shapes=[
             pltpu.VMEM((rows, samples), jnp.bfloat16),
@@ -256,7 +261,6 @@
             pltpu.VMEM(forward.shape, jnp.bfloat16),
             pltpu.VMEM(inverse.shape, jnp.bfloat16),
             pltpu.VMEM((rank, templates, rows), jnp.bfloat16),
-            pltpu.VMEM((rank, templates, 2 * F), jnp.float32),
             pltpu.VMEM((2 * REACH + rows, WIDE), jnp.bfloat16),
             pltpu.VMEM((2 * REACH + rows, WIDE), jnp.bfloat16),
             pltpu.VMEM((rows, 2 * F), jnp.bfloat16),
@@ -265,12 +269,11 @@
             pltpu.SemaphoreType.DMA,
             pltpu.SemaphoreType.DMA,
             pltpu.SemaphoreType.DMA((chunks,)),
-            pltpu.SemaphoreType.DMA((chunks,)),
         ],
-        cost_estimate=pl.CostEstimate(flops=work, bytes_accessed=24 << 20, transcendentals=0),
-        compiler_params=pltpu.CompilerParams(vmem_limit_bytes=44 << 20),
+        cost_estimate=pl.CostEstimate(flops=work, bytes_accessed=16 << 20, transcendentals=0),
+        compiler_params=pltpu.CompilerParams(vmem_limit_bytes=40 << 20),
         name="score",
-    )(band_offsets, toep, sides, before, before_sides, after, after_sides, raw, whitening, forward, inverse, spatial.transpose(1, 0, 2), hat)
+    )(band_offsets, toep, sides, before, before_sides, after, after_sides, split, spread, raw, whitening, forward, inverse, spatial.transpose(1, 0, 2))
 
     other = lax.ppermute(send, "chan", [(i, i ^ 1) for i in range(n_chan)])
     both = (keep + other.astype(jnp.float32)).astype(jnp.bfloat16)

time: 66.5 us -> 59.7 us (0.90)
  matrix products: 5.51 us -> 0 us
  waiting for transfers between devices: 11.2 us -> 8.8 us
  blocking collectives: 15.1 us -> 16.3 us
  Pallas kernels: 11.6 us -> 12.7 us
    dot_general x1 -> x0, matrix products: 5.51 us -> none  [local(): jnp.einsum('krj,jf->rkf', temporal, jnp.asarray(forward_matrix(taps, taps...]
    ppermute x1, waiting for transfers between devices: 9.89 us -> 6.99 us  [local(): prev = lax.ppermute(pack(raw[:, samples - EDGE:]), 'tm', up_tm)]
    ppermute x2, starting transfers between devices: 2.8 us -> 4.63 us  [the longest x1 3.07 us: local(): before = lax.ppermute(raw[rows - REACH:], 'chan', up)]
    ppermute x1, starting transfers between devices: 4.81 us -> 3.04 us  [local(): before_sides = lax.ppermute(sides[rows - REACH:], 'chan', up)]
    all_to_all x1, blocking collectives: 15.1 us -> 16.3 us  [local(): shares = lax.all_to_all(both, 'chan', 0, 0, axis_index_groups=members)]
    pallas_call x1, Pallas kernels: 11.3 us -> 12.1 us  [local(): pl.pallas_call(functools.partial(score_kernel, chunks), out_shape=(jax.Sh...]
  transfers between devices with their start and end apart: 7 -> 7, of which waited for: 2 -> 3; matrix products, arithmetic and copies ran while one was open for 9% -> 1% of each run, Pallas kernels for 0% -> 1%
where the time goes in v4:
time: 59.7 us; the launch traced here: 58.9 us
  starting transfers between devices  17.9 us (30%)
  blocking collectives  16.3 us (27%)
  Pallas kernels  12.7 us (21%)
  waiting for transfers between devices  8.8 us (15%)
  local copies, waits for them, and re-layouts  1.72 us (3%)
  other arithmetic  1.18 us (2%)
    all_to_all x1, blocking collectives, local(): shares = lax.all_to_all(both, 'chan', 0, 0, axis_index_groups=members)  16.3 us
    pallas_call x1, Pallas kernels, local(): pl.pallas_call(functools.partial(score_kernel, chunks), out_shape=(jax.Sh...  12.1 us
    ppermute x1, waiting for transfers between devices, local(): prev = lax.ppermute(pack(raw[:, samples - EDGE:]), 'tm', up_tm)  6.99 us
    ppermute x1, starting transfers between devices, local(): follow = lax.ppermute(pack(raw[:, :EDGE]), 'tm', down_tm)  4.01 us
    ppermute x1, starting transfers between devices, local(): before = lax.ppermute(raw[rows - REACH:], 'chan', up)  3.07 us
    ppermute x1, starting transfers between devices, local(): before_sides = lax.ppermute(sides[rows - REACH:], 'chan', up)  3.04 us
    ppermute x1, starting transfers between devices, local(): other = lax.ppermute(send, 'chan', [(i, i ^ 1) for i in range(n_chan)])  2.9 us
    ppermute x1, starting transfers between devices, local(): prev = lax.ppermute(pack(raw[:, samples - EDGE:]), 'tm', up_tm)  2.05 us
  transfers between devices with their start and end apart: 7, of which 3 were waited for; matrix products, arithmetic and copies ran while one was open for 1% of the time, Pallas kernels for 1%

profile of v4, /device:TPU:128, one launch (start us, length us, event | category | flops | bytes accessed | tf_op | source)
XLA Modules:
  0.0 58.9 jit_solution(7180689134065306134)
XLA Ops:
  0.0 1.3 %fusion.1 = (bf16[512,64]{1,0:T(8,128)(2,1)S(1)}, bf16[512,64]{1,0:T(8,128)(2,1)S(1)}, bf16[512,64]{1,0:T(8,128)(2,1)S(1)}, bf16[512,64]{1,0:T(8,128)(2,1)S(1)}) fusion(bf16[1024,384]{1,0:T(8,128)(2,1)} %raw_hbm.1), kind=kLoop, calls=%fused_computation.6 | loop fusion | bytes 524288 | tf_op jit(solution)/shard_map/slice | solution.py:52
  1.3 0.1 pad_maximum_fusion.1
  1.4 4.0 %collective-permute-start.1 = (bf16[512,128]{1,0:T(8,128)(2,1)S(1)}, bf16[512,128]{1,0:T(8,128)(2,1)S(1)}, u32[]{:S(2)}, u32[]{:S(2)}) collective-permute-start(bf16[512,128]{1,0:T(8,128)(2,1)S(1)} %pad_maximum_fusion.1), channel_id=1, source_target_pairs={{16,0},{32,16},{48,32},{64,48},{80,64},{96,80},{112,96},{128,112},... | collective-permute-start | bytes 393224 | tf_op jit(solution)/shard_map/ppermute | solution.py:218
  5.4 0.1 pad_maximum_fusion
  5.6 0.0 copy-start.1
  5.6 0.0 copy-start.2
  5.6 2.1 %collective-permute-start = (bf16[512,128]{1,0:T(8,128)(2,1)S(1)}, bf16[512,128]{1,0:T(8,128)(2,1)S(1)}, u32[]{:S(2)}, u32[]{:S(2)}) collective-permute-start(bf16[512,128]{1,0:T(8,128)(2,1)S(1)} %pad_maximum_fusion), channel_id=1, source_target_pairs={{0,16},{16,32},{32,48},{48,64},{64,80},{80,96},{96,112},{112,128},... | collective-permute-start | bytes 393224 | tf_op jit(solution)/shard_map/ppermute | solution.py:217
  7.7 0.0 copy-start.6
  7.7 0.1 fusion
  7.8 0.0 copy-start.3
  7.8 0.0 copy-start.4
  7.8 0.0 copy-start.5
  7.8 0.0 copy-start.7
  7.8 1.6 %collective-permute-start.4 = (bf16[832,384]{1,0:T(8,128)(2,1)S(1)}, bf16[832,384]{1,0:T(8,128)(2,1)S(1)}, u32[]{:S(2)}, u32[]{:S(2)}) collective-permute-start(bf16[832,384]{1,0:T(8,128)(2,1)S(1)} %get-tuple-element.13), channel_id=1, source_target_pairs={{1,0},{2,1},{3,2},{4,3},{5,4},{6,5},{7,6},{8,7},{9,8},{10,9},{11,1... | collective-permute-start | bytes 1916936 | tf_op jit(solution)/shard_map/ppermute | solution.py:216
  9.4 3.1 %collective-permute-start.2 = (bf16[832,384]{1,0:T(8,128)(2,1)S(1)}, bf16[832,384]{1,0:T(8,128)(2,1)S(1)}, u32[]{:S(2)}, u32[]{:S(2)}) collective-permute-start(bf16[832,384]{1,0:T(8,128)(2,1)S(1)} %get-tuple-element.14), channel_id=1, source_target_pairs={{0,1},{1,2},{2,3},{3,4},{4,5},{5,6},{6,7},{7,8},{8,9},{9,10},{10,1... | collective-permute-start | bytes 1916936 | tf_op jit(solution)/shard_map/ppermute | solution.py:215
  12.5 0.0 collective-permute-done.1
  12.5 0.1 fusion.4
  12.6 7.0 %collective-permute-done = bf16[512,128]{1,0:T(8,128)(2,1)S(1)} collective-permute-done((bf16[512,128]{1,0:T(8,128)(2,1)S(1)}, bf16[512,128]{1,0:T(8,128)(2,1)S(1)}, u32[]{:S(2)}, u32[]{:S(2)}) %collective-permute-start) | collective-permute-done | bytes 131104 | tf_op jit(solution)/shard_map/ppermute | solution.py:217
  19.6 0.1 fusion.3
  19.7 0.1 maximum_maximum_fusion.sides_ref
  19.9 1.3 %collective-permute-start.5 = (bf16[832,128]{1,0:T(8,128)(2,1)S(1)}, bf16[832,128]{1,0:T(8,128)(2,1)S(1)}, u32[]{:S(2)}, u32[]{:S(2)}) collective-permute-start(bf16[832,128]{1,0:T(8,128)(2,1)S(1)} %get-tuple-element.19), channel_id=1, source_target_pairs={{1,0},{2,1},{3,2},{4,3},{5,4},{6,5},{7,6},{8,7},{9,8},{10,9},{11,1... | collective-permute-start | bytes 638984 | tf_op jit(solution)/shard_map/ppermute | solution.py:227
  21.2 3.0 %collective-permute-start.3 = (bf16[832,128]{1,0:T(8,128)(2,1)S(1)}, bf16[832,128]{1,0:T(8,128)(2,1)S(1)}, u32[]{:S(2)}, u32[]{:S(2)}) collective-permute-start(bf16[832,128]{1,0:T(8,128)(2,1)S(1)} %get-tuple-element.20), channel_id=1, source_target_pairs={{0,1},{1,2},{2,3},{3,4},{4,5},{5,6},{6,7},{7,8},{8,9},{9,10},{10,1... | collective-permute-start | bytes 638984 | tf_op jit(solution)/shard_map/ppermute | solution.py:226
  24.3 0.6 prepare.1
  24.9 0.0 collective-permute-done.5.after_sides_ref
  24.9 0.4 collective-permute-done.3.before_sides_ref
  25.3 0.0 collective-permute-done.4.after_ref
  25.4 12.1 %score.1 = (f32[8,64,384]{2,1,0:T(8,128)S(1)}, bf16[8,64,384]{2,1,0:T(8,128)(2,1)S(1)}) custom-call(s32[8]{0:T(128)S(1)} %copy-done.4, bf16[512,512]{1,0:T(8,128)(2,1)S(1)} %get-tuple-element.9.toep_ref, bf16[1024,128]{1,0:T(8,128)(2,1)S(1)} %maximum_maximum_fusion.sides_ref, bf16[832,384]{1,0:T(8,128)(2,1)S(1)} %collective-permute-done.2.before_ref, ...), custom_call_target="tpu_custom_call" | custom-call | flops 8187281408 | bytes 16777216 | tf_op jit(solution)/shard_map/score/pallas_call | solution.py:250
  37.5 2.9 %collective-permute-start.6 = (bf16[8,64,384]{2,1,0:T(8,128)(2,1)S(1)}, bf16[8,64,384]{2,1,0:T(8,128)(2,1)S(1)}, u32[]{:S(2)}, u32[]{:S(2)}) collective-permute-start(bf16[8,64,384]{2,1,0:T(8,128)(2,1)S(1)} %get-tuple-element.12), channel_id=1, source_target_pairs={{0,1},{1,0},{2,3},{3,2},{4,5},{5,4},{6,7},{7,6},{8,9},{9,8},{10,11... | collective-permute-start | bytes 1179656 | tf_op jit(solution)/shard_map/ppermute | solution.py:278
  40.4 1.3 %collective-permute-done.6 = bf16[8,64,384]{2,1,0:T(8,128)(2,1)S(1)} collective-permute-done((bf16[8,64,384]{2,1,0:T(8,128)(2,1)S(1)}, bf16[8,64,384]{2,1,0:T(8,128)(2,1)S(1)}, u32[]{:S(2)}, u32[]{:S(2)}) %collective-permute-start.6) | collective-permute-done | bytes 393248 | tf_op jit(solution)/shard_map/ppermute | solution.py:278
  41.7 0.1 add_convert_fusion
  41.8 16.3 %all_to_all.5 = bf16[8,64,384]{2,1,0:T(8,128)(2,1)S(1)} all-to-all(bf16[8,64,384]{2,1,0:T(8,128)(2,1)S(1)} %add_convert_fusion), channel_id=1, replica_groups={{0,2,4,6,8,10,12,14},{1,3,5,7,9,11,13,15},{16,18,20,22,24,26,28,30},{17..., dimensions={0} | all-to-all | bytes 786432 | tf_op jit(solution)/shard_map/all_to_all | solution.py:281
  58.2 0.7 %convert_reduce_fusion = f32[64,384]{1,0:T(8,128)} fusion(bf16[8,64,384]{2,1,0:T(8,128)(2,1)S(1)} %all_to_all.5), kind=kLoop, calls=%fused_computation | loop fusion | flops 368640 | bytes 491520 | tf_op jit(solution)/shard_map/reduce_sum | solution.py:282
  (11 shorter events, 0.1 us)
Async XLA Ops:
  0.0 7.6 %copy-start = (bf16[1024,384]{1,0:T(8,128)(2,1)S(1)}, bf16[1024,384]{1,0:T(8,128)(2,1)}, u32[]{:S(2)}) copy-start(bf16[1024,384]{1,0:T(8,128)(2,1)} %raw_hbm.1) | copy-start | bytes 2359300
  1.4 11.1 %collective-permute-start.1 = (bf16[512,128]{1,0:T(8,128)(2,1)S(1)}, bf16[512,128]{1,0:T(8,128)(2,1)S(1)}, u32[]{:S(2)}, u32[]{:S(2)}) collective-permute-start(bf16[512,128]{1,0:T(8,128)(2,1)S(1)} %pad_maximum_fusion.1), channel_id=1, source_target_pairs={{16,0},{32,16},{48,32},{64,48},{80,64},{96,80},{112,96},{128,112},... | collective-permute-start | bytes 393224 | tf_op jit(solution)/shard_map/ppermute | solution.py:218
  5.6 18.7 %copy-start.1 = (f32[1024,3,61]{0,2,1:T(8,128)S(1)}, f32[1024,3,61]{0,2,1:T(8,128)}, u32[]{:S(2)}) copy-start(f32[1024,3,61]{0,2,1:T(8,128)} %param.14) | copy-start | bytes 2248708
  5.6 18.7 %copy-start.2 = (bf16[61]{0:T(256)(128)(2,1)S(1)}, bf16[61]{0:T(256)(128)(2,1)}, u32[]{:S(2)}) copy-start(bf16[61]{0:T(256)(128)(2,1)} %param.10) | copy-start | bytes 370
  5.6 14.0 %collective-permute-start = (bf16[512,128]{1,0:T(8,128)(2,1)S(1)}, bf16[512,128]{1,0:T(8,128)(2,1)S(1)}, u32[]{:S(2)}, u32[]{:S(2)}) collective-permute-start(bf16[512,128]{1,0:T(8,128)(2,1)S(1)} %pad_maximum_fusion), channel_id=1, source_target_pairs={{0,16},{16,32},{32,48},{48,64},{64,80},{80,96},{96,112},{112,128},... | collective-permute-start | bytes 393224 | tf_op jit(solution)/shard_map/ppermute | solution.py:217
  7.7 17.7 %copy-start.6 = (bf16[2,512,384]{2,1,0:T(8,128)(2,1)S(1)}, bf16[2,512,384]{2,1,0:T(8,128)(2,1)}, u32[]{:S(2)}) copy-start(bf16[2,512,384]{2,1,0:T(8,128)(2,1)} %constant.10.clone.inverse_hbm) | copy-start | bytes 2359300
  7.8 17.5 %copy-start.3 = (bf16[1024,1024]{1,0:T(8,128)(2,1)S(1)}, bf16[1024,1024]{1,0:T(8,128)(2,1)}, u32[]{:S(2)}) copy-start(bf16[1024,1024]{1,0:T(8,128)(2,1)} %white_hbm.1) | copy-start | bytes 6291460
  7.8 17.5 %copy-start.4 = (s32[8]{0:T(128)S(1)}, s32[8]{0:T(128)}, u32[]{:S(2)}) copy-start(s32[8]{0:T(128)} %offsets_ref.1) | copy-start | bytes 100
  7.8 17.5 %copy-start.5 = (bf16[2,512,512]{2,1,0:T(8,128)(2,1)S(1)}, bf16[2,512,512]{2,1,0:T(8,128)(2,1)}, u32[]{:S(2)}) copy-start(bf16[2,512,512]{2,1,0:T(8,128)(2,1)} %constant.9.clone.forward_hbm) | copy-start | bytes 3145732
  7.8 17.5 %copy-start.7 = (bf16[192,512]{1,0:T(8,128)(2,1)S(1)}, bf16[192,512]{1,0:T(8,128)(2,1)}, u32[]{:S(2)}) copy-start(bf16[192,512]{1,0:T(8,128)(2,1)} %constant.8.clone.spread_ref) | copy-start | bytes 589828
  7.8 17.5 %collective-permute-start.4 = (bf16[832,384]{1,0:T(8,128)(2,1)S(1)}, bf16[832,384]{1,0:T(8,128)(2,1)S(1)}, u32[]{:S(2)}, u32[]{:S(2)}) collective-permute-start(bf16[832,384]{1,0:T(8,128)(2,1)S(1)} %get-tuple-element.13), channel_id=1, source_target_pairs={{1,0},{2,1},{3,2},{4,3},{5,4},{6,5},{7,6},{8,7},{9,8},{10,9},{11,1... | collective-permute-start | bytes 1916936 | tf_op jit(solution)/shard_map/ppermute | solution.py:216
  9.4 15.9 %collective-permute-start.2 = (bf16[832,384]{1,0:T(8,128)(2,1)S(1)}, bf16[832,384]{1,0:T(8,128)(2,1)S(1)}, u32[]{:S(2)}, u32[]{:S(2)}) collective-permute-start(bf16[832,384]{1,0:T(8,128)(2,1)S(1)} %get-tuple-element.14), channel_id=1, source_target_pairs={{0,1},{1,2},{2,3},{3,4},{4,5},{5,6},{6,7},{7,8},{8,9},{9,10},{10,1... | collective-permute-start | bytes 1916936 | tf_op jit(solution)/shard_map/ppermute | solution.py:215
  19.9 5.0 %collective-permute-start.5 = (bf16[832,128]{1,0:T(8,128)(2,1)S(1)}, bf16[832,128]{1,0:T(8,128)(2,1)S(1)}, u32[]{:S(2)}, u32[]{:S(2)}) collective-permute-start(bf16[832,128]{1,0:T(8,128)(2,1)S(1)} %get-tuple-element.19), channel_id=1, source_target_pairs={{1,0},{2,1},{3,2},{4,3},{5,4},{6,5},{7,6},{8,7},{9,8},{10,9},{11,1... | collective-permute-start | bytes 638984 | tf_op jit(solution)/shard_map/ppermute | solution.py:227
  21.2 4.1 %collective-permute-start.3 = (bf16[832,128]{1,0:T(8,128)(2,1)S(1)}, bf16[832,128]{1,0:T(8,128)(2,1)S(1)}, u32[]{:S(2)}, u32[]{:S(2)}) collective-permute-start(bf16[832,128]{1,0:T(8,128)(2,1)S(1)} %get-tuple-element.20), channel_id=1, source_target_pairs={{0,1},{1,2},{2,3},{3,4},{4,5},{5,6},{6,7},{7,8},{8,9},{9,10},{10,1... | collective-permute-start | bytes 638984 | tf_op jit(solution)/shard_map/ppermute | solution.py:226
  37.5 4.2 %collective-permute-start.6 = (bf16[8,64,384]{2,1,0:T(8,128)(2,1)S(1)}, bf16[8,64,384]{2,1,0:T(8,128)(2,1)S(1)}, u32[]{:S(2)}, u32[]{:S(2)}) collective-permute-start(bf16[8,64,384]{2,1,0:T(8,128)(2,1)S(1)} %get-tuple-element.12), channel_id=1, source_target_pairs={{0,1},{1,0},{2,3},{3,2},{4,5},{5,4},{6,7},{7,6},{8,9},{9,8},{10,11... | collective-permute-start | bytes 1179656 | tf_op jit(solution)/shard_map/ppermute | solution.py:278

commit v5 on v4

v5 whole, which is shorter than its diff:
```python
import functools

import jax
import jax.numpy as jnp
import numpy as np
from jax import lax
from jax.experimental import pallas as pl
from jax.experimental.pallas import tpu as pltpu
from jax.sharding import PartitionSpec as P

LANES = 128
EDGE = 64
F = 256
POINTS = 2 * F - 1
WIDE = 512
SLOT = 64
REACH = 832


def halves(matrix):
    high = matrix.astype(jnp.bfloat16)
    low = (matrix - high.astype(np.float64)).astype(jnp.bfloat16)
    return np.stack([high, low])


def angles(samples):
    steps = np.outer(np.arange(samples), np.arange(F)) % POINTS
    return 2.0 * np.pi * steps / POINTS


def split_matrix(taps):
    high, low = halves(forward_matrix(taps, SLOT))
    return np.concatenate([high, low, high])


def forward_matrix(samples, rows):
    turn = angles(samples)
    full = np.zeros((rows, 2 * F))
    full[:samples] = np.concatenate([np.cos(turn), np.sin(turn)], axis=1)
    return full


def inverse_matrix(samples):
    turn = angles(samples).T
    weight = np.full((F, 1), 2.0 / POINTS)
    weight[0] = 1.0 / POINTS
    return np.concatenate([weight * np.cos(turn), -weight * np.sin(turn)], axis=0)


def pack(edge):
    half = edge.shape[0] // 2
    return jnp.concatenate([edge[:half], edge[half:]], axis=1)


def rolled(row, rows, shift):
    wide = jnp.broadcast_to(row, (rows, row.shape[1]))
    return pltpu.roll(wide, shift % row.shape[1], 1, stride=1, stride_axis=0)


def early_kernel(samples, taps_ref, temporal_ref, spread_ref, raw_ref, sides_ref, mate_ref, mate_sides_ref, toep_ref, hat_ref, own_ref, near_ref, wide_ref):
    taps = taps_ref.shape[1]
    t = lax.axis_index("tm")
    last = lax.axis_size("tm") - 1
    rest = (taps - 1) % 8
    reach = taps - 1 - rest
    tap = lax.broadcasted_iota(jnp.int32, (taps, WIDE), 0)
    lane = lax.broadcasted_iota(jnp.int32, (taps, WIDE), 1)
    place = (lane == rest - tap) | (lane == rest - tap + WIDE)
    picked = jnp.broadcast_to(taps_ref[...], (8, taps))
    row = jnp.dot(picked, place.astype(jnp.bfloat16), preferred_element_type=jnp.float32)[:1]
    begin = jnp.where(t == 0, taps // 2, 0)
    end = samples + jnp.where(t == last, taps // 2, taps - 1)
    column = lax.broadcasted_iota(jnp.int32, (1, WIDE), 1)
    keep = (column >= begin) & (column < end)
    prev = rolled(row, EDGE, reach - EDGE)
    follow = rolled(row, EDGE, reach + samples)
    even = t % 2 == 0
    toep_ref[:samples] = jnp.where(keep, rolled(row, samples, reach), 0.0).astype(jnp.bfloat16)
    toep_ref[samples : samples + EDGE] = jnp.where(keep, jnp.where(even, follow, prev), 0.0).astype(jnp.bfloat16)
    toep_ref[samples + EDGE :] = jnp.where(keep, jnp.where(even, prev, follow), 0.0).astype(jnp.bfloat16)

    rank, count, templates = temporal_ref.shape
    blank = jnp.zeros((SLOT - count, templates), jnp.float32)
    for r in range(rank):
        value = jnp.concatenate([temporal_ref[r], blank], axis=0)
        high = value.astype(jnp.bfloat16).astype(jnp.float32)
        stacked = jnp.concatenate([high, high, value - high], axis=0)
        hat_ref[r] = jnp.dot(stacked.T.astype(jnp.bfloat16), spread_ref[...], preferred_element_type=jnp.float32)

    for main, sides, out in ((raw_ref, sides_ref, own_ref), (mate_ref, mate_sides_ref, near_ref)):
        count = main.shape[0]
        wide_ref[:count, :samples] = main[...]
        wide_ref[:count, samples:] = sides[...]
        out[...] = jnp.dot(wide_ref[:count], toep_ref[...], preferred_element_type=jnp.float32).astype(jnp.bfloat16)


def score_kernel(
    chunks,
    offsets_ref,
    toep_ref,
    far_ref,
    far_sides_ref,
    hat_ref,
    own_hbm,
    near_hbm,
    white_hbm,
    forward_hbm,
    inverse_hbm,
    spatial_hbm,
    keep_ref,
    send_ref,
    white_ref,
    forward_ref,
    inverse_ref,
    spatial_ref,
    wide_ref,
    filtered_ref,
    whitened_ref,
    what_ref,
    own_sem,
    near_sem,
    white_sem,
    forward_sem,
    inverse_sem,
    spatial_sem,
):
    rows, band = white_ref.shape
    samples = far_ref.shape[1]
    groups = offsets_ref.shape[0]
    tile = rows // groups
    c = lax.axis_index("chan")
    all_rows = lax.axis_size("chan") * rows
    rank, templates, _ = spatial_ref.shape
    block = templates // chunks
    even_core = c % 2 == 0
    near = pl.multiple_of(jnp.where(even_core, REACH + rows, 0), EDGE)
    far = pl.multiple_of(jnp.where(even_core, 0, REACH + rows), EDGE)

    own_copy = pltpu.make_async_copy(own_hbm, filtered_ref.at[REACH : REACH + rows], own_sem)
    near_copy = pltpu.make_async_copy(near_hbm, filtered_ref.at[pl.ds(near, REACH)], near_sem)
    white_copy = pltpu.make_async_copy(white_hbm, white_ref, white_sem)
    forward_copy = pltpu.make_async_copy(forward_hbm, forward_ref, forward_sem)
    inverse_copy = pltpu.make_async_copy(inverse_hbm, inverse_ref, inverse_sem)
    for copy in (own_copy, near_copy, white_copy, forward_copy):
        copy.start()
    later = []
    for chunk in range(chunks):
        part = (slice(None), slice(chunk * block, (chunk + 1) * block))
        later.append(pltpu.make_async_copy(spatial_hbm.at[part], spatial_ref.at[part], spatial_sem.at[chunk]))
        later[-1].start()
        if chunk == 0:
            inverse_copy.start()

    wide_ref[:, :samples] = far_ref[...]
    wide_ref[:, samples:] = far_sides_ref[...]
    value = jnp.dot(wide_ref[...], toep_ref[...], preferred_element_type=jnp.float32)
    filtered_ref[pl.ds(far, REACH)] = value.astype(jnp.bfloat16)

    own_copy.wait()
    near_copy.wait()
    white_copy.wait()
    for group in range(groups):
        begin = c * rows + group * tile
        start = begin + tile // 2 - band // 2 + offsets_ref[group] * tile
        start = jnp.clip(start, 0, all_rows - band) - c * rows + REACH
        start = pl.multiple_of(jnp.clip(start, 0, 2 * REACH + rows - band), EDGE)
        body = slice(group * tile, (group + 1) * tile)
        value = jnp.dot(white_ref[body], filtered_ref[pl.ds(start, band)], preferred_element_type=jnp.float32)
        whitened_ref[body] = value.astype(jnp.bfloat16)
    forward_copy.wait()
    value = jnp.dot(whitened_ref[...], forward_ref[0], preferred_element_type=jnp.float32)
    value += jnp.dot(whitened_ref[...], forward_ref[1], preferred_element_type=jnp.float32)
    what_ref[...] = value.astype(jnp.bfloat16)

    own = keep_ref.shape[1]
    inverse_copy.wait()
    for chunk in range(chunks):
        later[chunk].wait()
        body = slice(chunk * block, (chunk + 1) * block)
        weights = spatial_ref[:, body].reshape(rank * block, rows)
        product = jnp.dot(weights, what_ref[...], preferred_element_type=jnp.float32)
        real = imag = 0.0
        for r in range(rank):
            a = product[r * block : (r + 1) * block, :F]
            b = product[r * block : (r + 1) * block, F:]
            x = hat_ref[r, body, :F]
            y = hat_ref[r, body, F:]
            real += a * x + b * y
            imag += a * y - b * x
        both = jnp.concatenate([real, imag], axis=1).astype(jnp.bfloat16)
        value = jnp.dot(both, inverse_ref[0], preferred_element_type=jnp.float32)
        value += jnp.dot(both, inverse_ref[1], preferred_element_type=jnp.float32)
        pairs = block // (2 * own)
        for pair in range(pairs):
            even = value[2 * pair * own : (2 * pair + 1) * own]
            odd = value[(2 * pair + 1) * own : (2 * pair + 2) * own]
            keep_ref[chunk * pairs + pair] = jnp.where(even_core, even, odd)
            send_ref[chunk * pairs + pair] = jnp.where(even_core, odd, even).astype(jnp.bfloat16)


def couples(size):
    first = [(i, i ^ 1) for i in range(size)]
    second = [(i, ((i + 1) ^ 1) - 1) for i in range(1, size - 1)]
    return first, second


def local(raw, band_taps, whitening, band_offsets, spatial, temporal):
    rows, samples = raw.shape
    taps = band_taps.shape[0]
    band = whitening.shape[1]
    templates, rank, _ = spatial.shape
    window = samples + taps - 1
    n_tm = lax.axis_size("tm")
    n_chan = lax.axis_size("chan")
    own = templates // n_chan
    chunks = 2

    near_chan, far_chan = couples(n_chan)
    near_tm, far_tm = couples(n_tm)
    even_tm = lax.axis_index("tm") % 2 == 0
    even_chan = lax.axis_index("chan") % 2 == 0

    def facing(array):
        upper, lower = array[rows - REACH :], array[:REACH]
        return jnp.where(even_chan, upper, lower), jnp.where(even_chan, lower, upper)

    ahead, behind = pack(raw[:, samples - EDGE :]), pack(raw[:, :EDGE])
    first = lax.ppermute(jnp.where(even_tm, ahead, behind), "tm", near_tm)
    second = lax.ppermute(jnp.where(even_tm, behind, ahead), "tm", far_tm)
    to_near, to_far = facing(raw)
    near = lax.ppermute(to_near, "chan", near_chan)
    far = lax.ppermute(to_far, "chan", far_chan)
    sides = jnp.concatenate(
        [
            jnp.concatenate([first[:, :EDGE], second[:, :EDGE]], axis=1),
            jnp.concatenate([first[:, EDGE:], second[:, EDGE:]], axis=1),
        ],
        axis=0,
    )
    to_near, to_far = facing(sides)
    far_sides = lax.ppermute(to_far, "chan", far_chan)
    near_sides = lax.ppermute(to_near, "chan", near_chan)

    vmem = pl.BlockSpec(memory_space=pltpu.VMEM)
    smem = pl.BlockSpec(memory_space=pltpu.SMEM)
    hbm = pl.BlockSpec(memory_space=pl.ANY)
    bf16 = jnp.bfloat16
    early = 2 * (rows + REACH) * WIDE * WIDE + 2 * rank * templates * 3 * SLOT * 2 * F
    toep, hat, own_rows, near_rows = pl.pallas_call(
        functools.partial(early_kernel, samples),
        out_shape=(
            jax.ShapeDtypeStruct((WIDE, WIDE), bf16),
            jax.ShapeDtypeStruct((rank, templates, 2 * F), jnp.float32),
            jax.ShapeDtypeStruct((rows, WIDE), bf16),
            jax.ShapeDtypeStruct((REACH, WIDE), bf16),
        ),
        in_specs=[vmem] * 7,
        out_specs=(vmem,) * 4,
        scratch_shapes=[pltpu.VMEM((rows, WIDE), bf16)],
        cost_estimate=pl.CostEstimate(flops=early, bytes_accessed=12 << 20, transcendentals=0),
        compiler_params=pltpu.CompilerParams(vmem_limit_bytes=24 << 20),
        name="early",
    )(band_taps[None], temporal.transpose(1, 2, 0), jnp.asarray(split_matrix(taps)), raw, sides, near, near_sides)
    forward = jnp.asarray(halves(forward_matrix(window, WIDE)))
    inverse = jnp.asarray(halves(inverse_matrix(samples)))

    out_shape = (n_chan // 2, own, samples)
    work = 2 * REACH * WIDE * WIDE + 2 * rows * WIDE * (band + 2 * WIDE) + 2 * templates * WIDE * (rank * rows + 2 * samples)
    keep, send = pl.pallas_call(
        functools.partial(score_kernel, chunks),
        out_shape=(
            jax.ShapeDtypeStruct(out_shape, jnp.float32),
            jax.ShapeDtypeStruct(out_shape, bf16),
        ),
        in_specs=[smem] + [vmem] * 4 + [hbm] * 6,
        out_specs=(vmem, vmem),
        scratch_shapes=[
            pltpu.VMEM((rows, band), bf16),
            pltpu.VMEM(forward.shape, bf16),
            pltpu.VMEM(inverse.shape, bf16),
            pltpu.VMEM((rank, templates, rows), bf16),
            pltpu.VMEM((REACH, WIDE), bf16),
            pltpu.VMEM((2 * REACH + rows, WIDE), bf16),
            pltpu.VMEM((rows, WIDE), bf16),
            pltpu.VMEM((rows, 2 * F), bf16),
            pltpu.SemaphoreType.DMA,
            pltpu.SemaphoreType.DMA,
            pltpu.SemaphoreType.DMA,
            pltpu.SemaphoreType.DMA,
            pltpu.SemaphoreType.DMA,
            pltpu.SemaphoreType.DMA((chunks,)),
        ],
        cost_estimate=pl.CostEstimate(flops=work, bytes_accessed=16 << 20, transcendentals=0),
        compiler_params=pltpu.CompilerParams(vmem_limit_bytes=36 << 20),
        name="score",
    )(band_offsets, toep, far, far_sides, hat, own_rows, near_rows, whitening, forward, inverse, spatial.transpose(1, 0, 2))

    other = lax.ppermute(send, "chan", near_chan)
    both = (keep + other.astype(jnp.float32)).astype(bf16)
    members = [[2 * i + core for i in range(n_chan // 2)] for core in range(2)]
    shares = lax.all_to_all(both, "chan", 0, 0, axis_index_groups=members)
    return jnp.sum(shares.astype(jnp.float32), axis=0)


def solution(mesh):
    placed = (P("chan", "tm"), P(), P("chan", None), P("chan"), P(None, None, "chan"), P())
    return jax.shard_map(local, mesh=mesh, in_specs=placed, out_specs=P("chan", "tm"), check_vma=False)
```

time: 59.7 us -> 52.9 us (0.89)
  starting transfers between devices: 17.9 us -> 12.1 us
  other arithmetic: 1.18 us -> 3.31 us
  waiting for transfers between devices: 8.8 us -> 7.43 us
  Pallas kernels: 12.7 us -> 11.5 us
  local copies, waits for them, and re-layouts: 1.72 us -> 2.77 us
  blocking collectives: 16.3 us -> 15.3 us
    ppermute x7, starting transfers between devices: 17.9 us -> 12.1 us  [the longest x1 3.17 us: local(): second = lax.ppermute(jnp.where(even_tm, behind, ahead), 'tm', far_tm)]
    pallas_call x1, Pallas kernels: 12.1 us -> 9.36 us  [local(): pl.pallas_call(functools.partial(score_kernel, chunks), out_shape=(jax.Sh...]
    select_n x0 -> x3, other arithmetic: none -> 2.38 us  [the longest x2 1.56 us: facing(): jnp.where(even_chan, lower, upper)]
    pallas_call x1, Pallas kernels: 0.57 us -> 2.12 us  [local(): pl.pallas_call(functools.partial(early_kernel, samples), out_shape=(jax.S...]
    ppermute x7, waiting for transfers between devices: 8.8 us -> 7.43 us  [the longest x1 5.3 us: local(): second = lax.ppermute(jnp.where(even_tm, behind, ahead), 'tm', far_tm)]
    unnamed x16, local copies, waits for them, and re-layouts: 0.05 us -> 1.16 us
    all_to_all x1, blocking collectives: 16.3 us -> 15.3 us  [local(): shares = lax.all_to_all(both, 'chan', 0, 0, axis_index_groups=members)]
  transfers between devices with their start and end apart: 7 -> 7, of which waited for: 3 -> 3; matrix products, arithmetic and copies ran while one was open for 1% -> 4% of each run, Pallas kernels for 1% -> 4%
where the time goes in v5:
time: 52.9 us; the launch traced here: 52.6 us
  blocking collectives  15.3 us (29%)
  starting transfers between devices  12.1 us (23%)
  Pallas kernels  11.5 us (22%)
  waiting for transfers between devices  7.43 us (14%)
  other arithmetic  3.31 us (6%)
  local copies, waits for them, and re-layouts  2.77 us (5%)
    all_to_all x1, blocking collectives, local(): shares = lax.all_to_all(both, 'chan', 0, 0, axis_index_groups=members)  15.3 us
    pallas_call x1, Pallas kernels, local(): pl.pallas_call(functools.partial(score_kernel, chunks), out_shape=(jax.Sh...  9.36 us
    ppermute x1, waiting for transfers between devices, local(): second = lax.ppermute(jnp.where(even_tm, behind, ahead), 'tm', far_tm)  5.3 us
    ppermute x1, starting transfers between devices, local(): second = lax.ppermute(jnp.where(even_tm, behind, ahead), 'tm', far_tm)  3.17 us
    ppermute x1, starting transfers between devices, local(): other = lax.ppermute(send, 'chan', near_chan)  2.97 us
    ppermute x1, starting transfers between devices, local(): near = lax.ppermute(to_near, 'chan', near_chan)  2.9 us
    pallas_call x1, Pallas kernels, local(): pl.pallas_call(functools.partial(early_kernel, samples), out_shape=(jax.S...  2.12 us
    ppermute x1, starting transfers between devices, local(): first = lax.ppermute(jnp.where(even_tm, ahead, behind), 'tm', near_tm)  1.58 us
  transfers between devices with their start and end apart: 7, of which 3 were waited for; matrix products, arithmetic and copies ran while one was open for 4% of the time, Pallas kernels for 4%

profile of v5, /device:TPU:128, one launch (start us, length us, event | category | flops | bytes accessed | tf_op | source)
XLA Modules:
  0.0 52.6 jit_solution(10477625416860790885)
XLA Ops:
  0.0 1.4 %fusion = (bf16[512,64]{1,0:T(8,128)(2,1)S(1)}, bf16[512,64]{1,0:T(8,128)(2,1)S(1)}, bf16[512,64]{1,0:T(8,128)(2,1)S(1)}, bf16[512,64]{1,0:T(8,128)(2,1)S(1)}) fusion(bf16[1024,384]{1,0:T(8,128)(2,1)} %raw_ref.1), kind=kLoop, calls=%fused_computation.11 | loop fusion | bytes 524288 | tf_op jit(solution)/shard_map/slice | solution.py:52
  1.4 0.8 %broadcast_select_fusion.5 = (bf16[512,128]{1,0:T(8,128)(2,1)}, bf16[512,128]{1,0:T(8,128)(2,1)S(1)}) fusion(pred[]{:T(512)S(6)} %eq.9, bf16[512,64]{1,0:T(8,128)(2,1)S(1)} %get-tuple-element.20, bf16[512,64]{1,0:T(8,128)(2,1)S(1)} %get-tuple-element.21, bf16[512,64]{1,0:T(8,128)(2,1)S(1)} %get-tuple-element.22, bf16[512,64]{1,0:T(8,128)(2,1)S(1)} %get-tuple-element.19), kind=kLoop, calls=%fused_computation.10 | loop fusion | flops 655360 | bytes 524289 | tf_op jit(solution)/shard_map/jit(_where)/select_n | solution.py:228
  2.3 1.6 %collective-permute-start = (bf16[512,128]{1,0:T(8,128)(2,1)}, bf16[512,128]{1,0:T(8,128)(2,1)S(1)}, u32[]{:S(2)}, u32[]{:S(2)}) collective-permute-start(bf16[512,128]{1,0:T(8,128)(2,1)} %get-tuple-element.23), channel_id=1, source_target_pairs={{0,16},{16,0},{32,48},{48,32},{64,80},{80,64},{96,112},{112,96},{1... | collective-permute-start | bytes 393224 | tf_op jit(solution)/shard_map/ppermute | solution.py:228
  3.8 3.2 %collective-permute-start.1 = (bf16[512,128]{1,0:T(8,128)(2,1)S(1)}, bf16[512,128]{1,0:T(8,128)(2,1)S(1)}, u32[]{:S(2)}, u32[]{:S(2)}) collective-permute-start(bf16[512,128]{1,0:T(8,128)(2,1)S(1)} %get-tuple-element.24), channel_id=1, source_target_pairs={{16,32},{32,16},{48,64},{64,48},{80,96},{96,80},{112,128},{128,112... | collective-permute-start | bytes 393224 | tf_op jit(solution)/shard_map/ppermute | solution.py:229
  7.0 0.0 copy-start.5
  7.0 0.0 copy-start.6
  7.0 1.5 %broadcast_select_fusion = (bf16[832,384]{1,0:T(8,128)(2,1)S(1)}, bf16[832,384]{1,0:T(8,128)(2,1)S(1)}) fusion(pred[]{:T(512)S(6)} %eq.10, bf16[1024,384]{1,0:T(8,128)(2,1)} %raw_ref.1), kind=kLoop, calls=%fused_computation.2 | loop fusion | flops 638976 | bytes 2555905 | tf_op jit(solution)/shard_map/jit(_where)/select_n | solution.py:225
  8.6 0.7 %collective-permute-start.4 = (bf16[832,384]{1,0:T(8,128)(2,1)S(1)}, bf16[832,384]{1,0:T(8,128)(2,1)S(1)}, u32[]{:S(2)}, u32[]{:S(2)}) collective-permute-start(bf16[832,384]{1,0:T(8,128)(2,1)S(1)} %get-tuple-element.17), channel_id=1, source_target_pairs={{1,2},{2,1},{3,4},{4,3},{5,6},{6,5},{7,8},{8,7},{9,10},{10,9},{11,... | collective-permute-start | bytes 1916936 | tf_op jit(solution)/shard_map/ppermute | solution.py:232
  9.3 2.9 %collective-permute-start.2 = (bf16[832,384]{1,0:T(8,128)(2,1)S(1)}, bf16[832,384]{1,0:T(8,128)(2,1)S(1)}, u32[]{:S(2)}, u32[]{:S(2)}) collective-permute-start(bf16[832,384]{1,0:T(8,128)(2,1)S(1)} %get-tuple-element.18), channel_id=1, source_target_pairs={{0,1},{1,0},{2,3},{3,2},{4,5},{5,4},{6,7},{7,6},{8,9},{9,8},{10,11... | collective-permute-start | bytes 1916936 | tf_op jit(solution)/shard_map/ppermute | solution.py:231
  12.2 0.0 collective-permute-done
  12.2 0.1 fusion.1
  12.3 5.3 %collective-permute-done.1 = bf16[512,128]{1,0:T(8,128)(2,1)S(1)} collective-permute-done((bf16[512,128]{1,0:T(8,128)(2,1)S(1)}, bf16[512,128]{1,0:T(8,128)(2,1)S(1)}, u32[]{:S(2)}, u32[]{:S(2)}) %collective-permute-start.1) | collective-permute-done | bytes 131104 | tf_op jit(solution)/shard_map/ppermute | solution.py:229
  17.6 0.1 fusion.2
  17.7 0.1 maximum_maximum_fusion.sides_ref
  17.9 0.1 collective-permute-start.3
  18.0 0.7 %collective-permute-start.5 = (bf16[832,128]{1,0:T(8,128)(2,1)S(1)}, bf16[832,128]{1,0:T(8,128)(2,1)S(1)}, u32[]{:S(2)}, u32[]{:S(2)}) collective-permute-start(bf16[832,128]{1,0:T(8,128)(2,1)S(1)} %get-tuple-element.25), channel_id=1, source_target_pairs={{1,2},{2,1},{3,4},{4,3},{5,6},{6,5},{7,8},{8,7},{9,10},{10,9},{11,... | collective-permute-start | bytes 638984 | tf_op jit(solution)/shard_map/ppermute | solution.py:241
  18.7 0.8 %collective-permute-done.3.mate_sides_ref = bf16[832,128]{1,0:T(8,128)(2,1)S(1)} collective-permute-done((bf16[832,128]{1,0:T(8,128)(2,1)S(1)}, bf16[832,128]{1,0:T(8,128)(2,1)S(1)}, u32[]{:S(2)}, u32[]{:S(2)}) %collective-permute-start.3) | collective-permute-done | bytes 213024 | tf_op jit(solution)/shard_map/ppermute | solution.py:242
  19.5 0.0 collective-permute-done.2.mate_ref
  19.5 0.0 copy-done.7
  19.5 0.0 copy-start.2
  19.5 1.1 %copy-done.2 = f32[1024,3,61]{0,2,1:T(8,128)S(1)} copy-done((f32[1024,3,61]{0,2,1:T(8,128)S(1)}, f32[1024,3,61]{0,2,1:T(8,128)}, u32[]{:S(2)}) %copy-start.2) | copy-done | bytes 749592
  20.6 2.1 %early.1 = (bf16[512,512]{1,0:T(8,128)(2,1)S(1)}, f32[3,1024,512]{2,1,0:T(8,128)S(1)}, bf16[1024,512]{1,0:T(8,128)(2,1)S(1)}, bf16[832,512]{1,0:T(8,128)(2,1)S(1)}) custom-call(bf16[1,61]{1,0:T(2,128)(2,1)S(1)} %bitcast.4, f32[3,61,1024]{2,1,0:T(8,128)S(1)} %bitcast.3, bf16[192,512]{1,0:T(8,128)(2,1)S(1)} %copy-done.7, bf16[1024,384]{1,0:T(8,128)(2,1)S(1)} %copy-done, ...), custom_call_target="tpu_custom_call" | custom-call | flops 1577058304 | bytes 12582912 | tf_op jit(solution)/shard_map/early/pallas_call | solution.py:249
  22.7 0.0 collective-permute-done.5.far_sides_ref
  22.8 0.0 collective-permute-done.4.far_ref
  22.8 0.0 copy-done.1
  22.8 0.0 copy-done.4
  22.8 9.4 %score.1 = (f32[8,64,384]{2,1,0:T(8,128)S(1)}, bf16[8,64,384]{2,1,0:T(8,128)(2,1)S(1)}) custom-call(s32[8]{0:T(128)S(1)} %copy-done.4, bf16[512,512]{1,0:T(8,128)(2,1)S(1)} %get-tuple-element.11.toep_ref, bf16[832,384]{1,0:T(8,128)(2,1)S(1)} %collective-permute-done.4.far_ref, bf16[832,128]{1,0:T(8,128)(2,1)S(1)} %collective-permute-done.5.far_sides_ref, ...), custom_call_target="tpu_custom_call" | custom-call | flops 6610223104 | bytes 16777216 | tf_op jit(solution)/shard_map/score/pallas_call | solution.py:269
  32.2 3.0 %collective-permute-start.6 = (bf16[8,64,384]{2,1,0:T(8,128)(2,1)S(1)}, bf16[8,64,384]{2,1,0:T(8,128)(2,1)S(1)}, u32[]{:S(2)}, u32[]{:S(2)}) collective-permute-start(bf16[8,64,384]{2,1,0:T(8,128)(2,1)S(1)} %get-tuple-element.16), channel_id=1, source_target_pairs={{0,1},{1,0},{2,3},{3,2},{4,5},{5,4},{6,7},{7,6},{8,9},{9,8},{10,11... | collective-permute-start | bytes 1179656 | tf_op jit(solution)/shard_map/ppermute | solution.py:298
  35.1 1.3 %collective-permute-done.6 = bf16[8,64,384]{2,1,0:T(8,128)(2,1)S(1)} collective-permute-done((bf16[8,64,384]{2,1,0:T(8,128)(2,1)S(1)}, bf16[8,64,384]{2,1,0:T(8,128)(2,1)S(1)}, u32[]{:S(2)}, u32[]{:S(2)}) %collective-permute-start.6) | collective-permute-done | bytes 393248 | tf_op jit(solution)/shard_map/ppermute | solution.py:298
  36.5 0.1 add_convert_fusion
  36.6 15.3 %all_to_all.5 = bf16[8,64,384]{2,1,0:T(8,128)(2,1)S(1)} all-to-all(bf16[8,64,384]{2,1,0:T(8,128)(2,1)S(1)} %add_convert_fusion), channel_id=1, replica_groups={{0,2,4,6,8,10,12,14},{1,3,5,7,9,11,13,15},{16,18,20,22,24,26,28,30},{17..., dimensions={0} | all-to-all | bytes 786432 | tf_op jit(solution)/shard_map/all_to_all | solution.py:301
  51.9 0.7 %convert_reduce_fusion = f32[64,384]{1,0:T(8,128)} fusion(bf16[8,64,384]{2,1,0:T(8,128)(2,1)S(1)} %all_to_all.5), kind=kLoop, calls=%fused_computation | loop fusion | flops 368640 | bytes 491520 | tf_op jit(solution)/shard_map/reduce_sum | solution.py:302
  (10 shorter events, 0.1 us)
Async XLA Ops:
  0.0 19.5 %copy-start.7 = (bf16[192,512]{1,0:T(8,128)(2,1)S(1)}, bf16[192,512]{1,0:T(8,128)(2,1)}, u32[]{:S(2)}) copy-start(bf16[192,512]{1,0:T(8,128)(2,1)} %constant.33.clone.spread_ref) | copy-start | bytes 589828
  0.0 19.5 %copy-start = (bf16[1024,384]{1,0:T(8,128)(2,1)S(1)}, bf16[1024,384]{1,0:T(8,128)(2,1)}, u32[]{:S(2)}) copy-start(bf16[1024,384]{1,0:T(8,128)(2,1)} %raw_ref.1) | copy-start | bytes 2359300
  0.0 19.5 %copy-start.3 = (bf16[61]{0:T(256)(128)(2,1)S(1)}, bf16[61]{0:T(256)(128)(2,1)}, u32[]{:S(2)}) copy-start(bf16[61]{0:T(256)(128)(2,1)} %param.10) | copy-start | bytes 370
  0.0 22.7 %copy-start.1 = (bf16[1024,1024]{1,0:T(8,128)(2,1)S(1)}, bf16[1024,1024]{1,0:T(8,128)(2,1)}, u32[]{:S(2)}) copy-start(bf16[1024,1024]{1,0:T(8,128)(2,1)} %white_hbm.1) | copy-start | bytes 6291460
  0.0 22.7 %copy-start.4 = (s32[8]{0:T(128)S(1)}, s32[8]{0:T(128)}, u32[]{:S(2)}) copy-start(s32[8]{0:T(128)} %offsets_ref.1) | copy-start | bytes 100
  2.3 9.9 %collective-permute-start = (bf16[512,128]{1,0:T(8,128)(2,1)}, bf16[512,128]{1,0:T(8,128)(2,1)S(1)}, u32[]{:S(2)}, u32[]{:S(2)}) collective-permute-start(bf16[512,128]{1,0:T(8,128)(2,1)} %get-tuple-element.23), channel_id=1, source_target_pairs={{0,16},{16,0},{32,48},{48,32},{64,80},{80,64},{96,112},{112,96},{1... | collective-permute-start | bytes 393224 | tf_op jit(solution)/shard_map/ppermute | solution.py:228
  3.8 13.8 %collective-permute-start.1 = (bf16[512,128]{1,0:T(8,128)(2,1)S(1)}, bf16[512,128]{1,0:T(8,128)(2,1)S(1)}, u32[]{:S(2)}, u32[]{:S(2)}) collective-permute-start(bf16[512,128]{1,0:T(8,128)(2,1)S(1)} %get-tuple-element.24), channel_id=1, source_target_pairs={{16,32},{32,16},{48,64},{64,48},{80,96},{96,80},{112,128},{128,112... | collective-permute-start | bytes 393224 | tf_op jit(solution)/shard_map/ppermute | solution.py:229
  7.0 15.8 %copy-start.5 = (bf16[2,512,512]{2,1,0:T(8,128)(2,1)S(1)}, bf16[2,512,512]{2,1,0:T(8,128)(2,1)}, u32[]{:S(2)}) copy-start(bf16[2,512,512]{2,1,0:T(8,128)(2,1)} %constant.34.clone.forward_hbm) | copy-start | bytes 3145732
  7.0 15.8 %copy-start.6 = (bf16[2,512,384]{2,1,0:T(8,128)(2,1)S(1)}, bf16[2,512,384]{2,1,0:T(8,128)(2,1)}, u32[]{:S(2)}) copy-start(bf16[2,512,384]{2,1,0:T(8,128)(2,1)} %constant.35.clone.inverse_hbm) | copy-start | bytes 2359300
  8.6 14.2 %collective-permute-start.4 = (bf16[832,384]{1,0:T(8,128)(2,1)S(1)}, bf16[832,384]{1,0:T(8,128)(2,1)S(1)}, u32[]{:S(2)}, u32[]{:S(2)}) collective-permute-start(bf16[832,384]{1,0:T(8,128)(2,1)S(1)} %get-tuple-element.17), channel_id=1, source_target_pairs={{1,2},{2,1},{3,4},{4,3},{5,6},{6,5},{7,8},{8,7},{9,10},{10,9},{11,... | collective-permute-start | bytes 1916936 | tf_op jit(solution)/shard_map/ppermute | solution.py:232
  9.3 10.2 %collective-permute-start.2 = (bf16[832,384]{1,0:T(8,128)(2,1)S(1)}, bf16[832,384]{1,0:T(8,128)(2,1)S(1)}, u32[]{:S(2)}, u32[]{:S(2)}) collective-permute-start(bf16[832,384]{1,0:T(8,128)(2,1)S(1)} %get-tuple-element.18), channel_id=1, source_target_pairs={{0,1},{1,0},{2,3},{3,2},{4,5},{5,4},{6,7},{7,6},{8,9},{9,8},{10,11... | collective-permute-start | bytes 1916936 | tf_op jit(solution)/shard_map/ppermute | solution.py:231
  17.9 1.6 %collective-permute-start.3 = (bf16[832,128]{1,0:T(8,128)(2,1)S(1)}, bf16[832,128]{1,0:T(8,128)(2,1)S(1)}, u32[]{:S(2)}, u32[]{:S(2)}) collective-permute-start(bf16[832,128]{1,0:T(8,128)(2,1)S(1)} %get-tuple-element.26), channel_id=1, source_target_pairs={{0,1},{1,0},{2,3},{3,2},{4,5},{5,4},{6,7},{7,6},{8,9},{9,8},{10,11... | collective-permute-start | bytes 638984 | tf_op jit(solution)/shard_map/ppermute | solution.py:242
  18.0 4.7 %collective-permute-start.5 = (bf16[832,128]{1,0:T(8,128)(2,1)S(1)}, bf16[832,128]{1,0:T(8,128)(2,1)S(1)}, u32[]{:S(2)}, u32[]{:S(2)}) collective-permute-start(bf16[832,128]{1,0:T(8,128)(2,1)S(1)} %get-tuple-element.25), channel_id=1, source_target_pairs={{1,2},{2,1},{3,4},{4,3},{5,6},{6,5},{7,8},{8,7},{9,10},{10,9},{11,... | collective-permute-start | bytes 638984 | tf_op jit(solution)/shard_map/ppermute | solution.py:241
  19.5 1.1 %copy-start.2 = (f32[1024,3,61]{0,2,1:T(8,128)S(1)}, f32[1024,3,61]{0,2,1:T(8,128)}, u32[]{:S(2)}) copy-start(f32[1024,3,61]{0,2,1:T(8,128)} %param.14) | copy-start | bytes 2248708
  32.2 4.3 %collective-permute-start.6 = (bf16[8,64,384]{2,1,0:T(8,128)(2,1)S(1)}, bf16[8,64,384]{2,1,0:T(8,128)(2,1)S(1)}, u32[]{:S(2)}, u32[]{:S(2)}) collective-permute-start(bf16[8,64,384]{2,1,0:T(8,128)(2,1)S(1)} %get-tuple-element.16), channel_id=1, source_target_pairs={{0,1},{1,0},{2,3},{3,2},{4,5},{5,4},{6,7},{7,6},{8,9},{9,8},{10,11... | collective-permute-start | bytes 1179656 | tf_op jit(solution)/shard_map/ppermute | solution.py:298

commit v6 on v5

--- a/solution.py
+++ b/solution.py
@@ -47,9 +47,38 @@
     return np.concatenate([weight * np.cos(turn), -weight * np.sin(turn)], axis=0)
 
 
-def pack(edge):
-    half = edge.shape[0] // 2
-    return jnp.concatenate([edge[:half], edge[half:]], axis=1)
+def pack_kernel(raw_hbm, near_ref, far_ref, edge_ref, edge_sem):
+    rows, samples = raw_hbm.shape
+    half = rows // 2
+    copies = [
+        pltpu.make_async_copy(raw_hbm.at[:, begin : begin + LANES], edge_ref.at[part], edge_sem.at[part])
+        for part, begin in enumerate((0, samples - LANES))
+    ]
+    for copy in copies:
+        copy.start()
+    low = lax.broadcasted_iota(jnp.int32, (half, LANES), 1) < EDGE
+    even = lax.axis_index("tm") % 2 == 0
+    for copy in copies:
+        copy.wait()
+    first = edge_ref[0].astype(jnp.float32)
+    last = edge_ref[1].astype(jnp.float32)
+    behind = jnp.where(low, first[:half], pltpu.roll(first[half:], EDGE, 1)).astype(jnp.bfloat16)
+    ahead = jnp.where(low, pltpu.roll(last[:half], EDGE, 1), last[half:]).astype(jnp.bfloat16)
+    near_ref[...] = jnp.where(even, ahead, behind)
+    far_ref[...] = jnp.where(even, behind, ahead)
+
+
+def face_kernel(raw_hbm, near_ref, far_ref, near_sem, far_sem):
+    rows = raw_hbm.shape[0]
+    even = lax.axis_index("chan") % 2 == 0
+    upper, lower = rows - REACH, 0
+    copies = []
+    for ref, sem, begin in ((far_ref, far_sem, jnp.where(even, lower, upper)), (near_ref, near_sem, jnp.where(even, upper, lower))):
+        part = pl.ds(pl.multiple_of(begin, EDGE), REACH)
+        copies.append(pltpu.make_async_copy(raw_hbm.at[part], ref, sem))
+        copies[-1].start()
+    for copy in copies:
+        copy.wait()
 
 
 def rolled(row, rows, shift):
@@ -217,19 +246,38 @@
 
     near_chan, far_chan = couples(n_chan)
     near_tm, far_tm = couples(n_tm)
-    even_tm = lax.axis_index("tm") % 2 == 0
     even_chan = lax.axis_index("chan") % 2 == 0
-
-    def facing(array):
-        upper, lower = array[rows - REACH :], array[:REACH]
-        return jnp.where(even_chan, upper, lower), jnp.where(even_chan, lower, upper)
-
-    ahead, behind = pack(raw[:, samples - EDGE :]), pack(raw[:, :EDGE])
-    first = lax.ppermute(jnp.where(even_tm, ahead, behind), "tm", near_tm)
-    second = lax.ppermute(jnp.where(even_tm, behind, ahead), "tm", far_tm)
-    to_near, to_far = facing(raw)
+    vmem = pl.BlockSpec(memory_space=pltpu.VMEM)
+    smem = pl.BlockSpec(memory_space=pltpu.SMEM)
+    hbm = pl.BlockSpec(memory_space=pl.ANY)
+    bf16 = jnp.bfloat16
+
+    packed = jax.ShapeDtypeStruct((rows // 2, LANES), bf16)
+    to_near, to_far = pl.pallas_call(
+        pack_kernel,
+        out_shape=(packed, packed),
+        in_specs=[hbm],
+        out_specs=(vmem, vmem),
+        scratch_shapes=[pltpu.VMEM((2, rows, LANES), bf16), pltpu.SemaphoreType.DMA((2,))],
+        cost_estimate=pl.CostEstimate(flops=rows * LANES, bytes_accessed=4 * rows * LANES, transcendentals=0),
+        compiler_params=pltpu.CompilerParams(vmem_limit_bytes=4 << 20),
+        name="pack",
+    )(raw)
+    first = lax.ppermute(to_near, "tm", near_tm)
+    second = lax.ppermute(to_far, "tm", far_tm)
+    facing = jax.ShapeDtypeStruct((REACH, samples), bf16)
+    to_near, to_far = pl.pallas_call(
+        face_kernel,
+        out_shape=(facing, facing),
+        in_specs=[hbm],
+        out_specs=(vmem, vmem),
+        scratch_shapes=[pltpu.SemaphoreType.DMA, pltpu.SemaphoreType.DMA],
+        cost_estimate=pl.CostEstimate(flops=0, bytes_accessed=8 * REACH * samples, transcendentals=0),
+        compiler_params=pltpu.CompilerParams(vmem_limit_bytes=2 << 20),
+        name="face",
+    )(raw)
+    far = lax.ppermute(to_far, "chan", far_chan)
     near = lax.ppermute(to_near, "chan", near_chan)
-    far = lax.ppermute(to_far, "chan", far_chan)
     sides = jnp.concatenate(
         [
             jnp.concatenate([first[:, :EDGE], second[:, :EDGE]], axis=1),
@@ -237,14 +285,10 @@
         ],
         axis=0,
     )
-    to_near, to_far = facing(sides)
-    far_sides = lax.ppermute(to_far, "chan", far_chan)
-    near_sides = lax.ppermute(to_near, "chan", near_chan)
-
-    vmem = pl.BlockSpec(memory_space=pltpu.VMEM)
-    smem = pl.BlockSpec(memory_space=pltpu.SMEM)
-    hbm = pl.BlockSpec(memory_space=pl.ANY)
-    bf16 = jnp.bfloat16
+    upper, lower = sides[rows - REACH :], sides[:REACH]
+    far_sides = lax.ppermute(jnp.where(even_chan, lower, upper), "chan", far_chan)
+    near_sides = lax.ppermute(jnp.where(even_chan, upper, lower), "chan", near_chan)
+
     early = 2 * (rows + REACH) * WIDE * WIDE + 2 * rank * templates * 3 * SLOT * 2 * F
     toep, hat, own_rows, near_rows = pl.pallas_call(
         functools.partial(early_kernel, samples),

time: 52.9 us -> 55.2 us (1.043)
  local copies, waits for them, and re-layouts: 2.77 us -> 7.28 us
  starting transfers between devices: 12.1 us -> 8.57 us
  Pallas kernels: 11.5 us -> 14.8 us
  other arithmetic: 3.31 us -> 0.96 us
  waiting for transfers between devices: 7.43 us -> 9.51 us
  blocking collectives: 15.3 us -> 13.5 us
    unnamed x16 -> x18, local copies, waits for them, and re-layouts: 1.16 us -> 5 us
    ppermute x1, starting transfers between devices: 2.9 us -> 0.09 us  [local(): near = lax.ppermute(to_near, 'chan', near_chan)]
    select_n x3 -> x1, other arithmetic: 2.38 us -> 0.03 us  [local(): jnp.where(even_chan, lower, upper)]
    pallas_call x0 -> x2, Pallas kernels: none -> 2.18 us  [the longest x1 1.25 us: local(): pl.pallas_call(face_kernel, out_shape=(facing, facing), in_specs=[hbm], o...]
    ppermute x4, waiting for transfers between devices: 6.07 us -> 8.15 us  [the longest x1 7.38 us: local(): second = lax.ppermute(to_far, 'tm', far_tm)]
    all_to_all x1, blocking collectives: 15.3 us -> 13.5 us  [local(): shares = lax.all_to_all(both, 'chan', 0, 0, axis_index_groups=members)]
    slice x1 -> x0, local copies, waits for them, and re-layouts: 1.38 us -> none  [pack(): return jnp.concatenate([edge[:half], edge[half:]], axis=1)]
    pallas_call x1, Pallas kernels: 2.12 us -> 3.22 us  [local(): pl.pallas_call(functools.partial(early_kernel, samples), out_shape=(jax.S...]
  transfers between devices with their start and end apart: 7 -> 7, of which waited for: 3 -> 3; matrix products, arithmetic and copies ran while one was open for 4% -> 4% of each run, Pallas kernels for 4% -> 8%
where the time goes in v6:
time: 55.2 us; the launch traced here: 54.8 us
  Pallas kernels  14.8 us (27%)
  blocking collectives  13.5 us (24%)
  waiting for transfers between devices  9.51 us (17%)
  starting transfers between devices  8.57 us (16%)
  local copies, waits for them, and re-layouts  7.28 us (13%)
  other arithmetic  0.96 us (2%)
    all_to_all x1, blocking collectives, local(): shares = lax.all_to_all(both, 'chan', 0, 0, axis_index_groups=members)  13.5 us
    pallas_call x1, Pallas kernels, local(): pl.pallas_call(functools.partial(score_kernel, chunks), out_shape=(jax.Sh...  9.35 us
    ppermute x1, waiting for transfers between devices, local(): second = lax.ppermute(to_far, 'tm', far_tm)  7.38 us
    unnamed x18, local copies, waits for them, and re-layouts  5 us
    pallas_call x1, Pallas kernels, local(): pl.pallas_call(functools.partial(early_kernel, samples), out_shape=(jax.S...  3.22 us
    ppermute x1, starting transfers between devices, local(): second = lax.ppermute(to_far, 'tm', far_tm)  3.17 us
    ppermute x1, starting transfers between devices, local(): other = lax.ppermute(send, 'chan', near_chan)  2.17 us
    ppermute x1, starting transfers between devices, local(): first = lax.ppermute(to_near, 'tm', near_tm)  1.66 us
  transfers between devices with their start and end apart: 7, of which 3 were waited for; matrix products, arithmetic and copies ran while one was open for 4% of the time, Pallas kernels for 8%

profile of v6, /device:TPU:128, one launch (start us, length us, event | category | flops | bytes accessed | tf_op | source)
XLA Modules:
  0.0 54.8 jit_solution(16906111101240819715)
XLA Ops:
  0.0 1.1 %copy-done = bf16[1024,384]{1,0:T(8,128)(2,1)S(1)} copy-done((bf16[1024,384]{1,0:T(8,128)(2,1)S(1)}, bf16[1024,384]{1,0:T(8,128)(2,1)}, u32[]{:S(2)}) %copy-start) | copy-done | bytes 786456
  1.1 0.9 %pack.1 = (bf16[512,128]{1,0:T(8,128)(2,1)}, bf16[512,128]{1,0:T(8,128)(2,1)S(1)}) custom-call(bf16[1024,384]{1,0:T(8,128)(2,1)S(1)} %copy-done), custom_call_target="tpu_custom_call" | custom-call | flops 131072 | bytes 524288 | tf_op jit(solution)/shard_map/pack/pallas_call | solution.py:256
  2.1 1.7 %collective-permute-start = (bf16[512,128]{1,0:T(8,128)(2,1)}, bf16[512,128]{1,0:T(8,128)(2,1)}, u32[]{:S(2)}, u32[]{:S(2)}) collective-permute-start(bf16[512,128]{1,0:T(8,128)(2,1)} %get-tuple-element.15), channel_id=1, source_target_pairs={{0,16},{16,0},{32,48},{48,32},{64,80},{80,64},{96,112},{112,96},{1... | collective-permute-start | bytes 393224 | tf_op jit(solution)/shard_map/ppermute | solution.py:266
  3.7 3.2 %collective-permute-start.1 = (bf16[512,128]{1,0:T(8,128)(2,1)S(1)}, bf16[512,128]{1,0:T(8,128)(2,1)}, u32[]{:S(2)}, u32[]{:S(2)}) collective-permute-start(bf16[512,128]{1,0:T(8,128)(2,1)S(1)} %get-tuple-element.16), channel_id=1, source_target_pairs={{16,32},{32,16},{48,64},{64,48},{80,96},{96,80},{112,128},{128,112... | collective-permute-start | bytes 393224 | tf_op jit(solution)/shard_map/ppermute | solution.py:267
  6.9 1.3 %face.1 = (bf16[832,384]{1,0:T(8,128)(2,1)}, bf16[832,384]{1,0:T(8,128)(2,1)S(1)}) custom-call(bf16[1024,384]{1,0:T(8,128)(2,1)S(1)} %copy-done), custom_call_target="tpu_custom_call" | custom-call | bytes 2555904 | tf_op jit(solution)/shard_map/face/pallas_call | solution.py:269
  8.2 0.1 collective-permute-start.2
  8.3 0.7 %collective-permute-start.4 = (bf16[832,384]{1,0:T(8,128)(2,1)S(1)}, bf16[832,384]{1,0:T(8,128)(2,1)S(1)}, u32[]{:S(2)}, u32[]{:S(2)}) collective-permute-start(bf16[832,384]{1,0:T(8,128)(2,1)S(1)} %get-tuple-element.19), channel_id=1, source_target_pairs={{1,2},{2,1},{3,4},{4,3},{5,6},{6,5},{7,8},{8,7},{9,10},{10,9},{11,... | collective-permute-start | bytes 1916936 | tf_op jit(solution)/shard_map/ppermute | solution.py:279
  9.0 0.0 copy-start.6
  9.0 0.0 copy-start.7
  9.0 0.0 collective-permute-done
  9.0 1.2 %fusion = (bf16[512,64]{1,0:T(8,128)(2,1)S(1)}, bf16[512,64]{1,0:T(8,128)(2,1)S(1)}) fusion(bf16[512,128]{1,0:T(8,128)(2,1)} %collective-permute-done), kind=kLoop, calls=%fused_computation.5 | loop fusion | bytes 262144 | tf_op jit(solution)/shard_map/slice | solution.py:283
  10.2 7.4 %collective-permute-done.1 = bf16[512,128]{1,0:T(8,128)(2,1)} collective-permute-done((bf16[512,128]{1,0:T(8,128)(2,1)S(1)}, bf16[512,128]{1,0:T(8,128)(2,1)}, u32[]{:S(2)}, u32[]{:S(2)}) %collective-permute-start.1) | collective-permute-done | bytes 131104 | tf_op jit(solution)/shard_map/ppermute | solution.py:267
  17.6 1.1 %fusion.1 = (bf16[512,64]{1,0:T(8,128)(2,1)S(1)}, bf16[512,64]{1,0:T(8,128)(2,1)S(1)}) fusion(bf16[512,128]{1,0:T(8,128)(2,1)} %collective-permute-done.1), kind=kLoop, calls=%fused_computation.6 | loop fusion | bytes 262144 | tf_op jit(solution)/shard_map/slice | solution.py:283
  18.7 0.1 maximum_maximum_fusion.sides_ref
  18.9 0.1 collective-permute-start.3
  19.0 0.7 %collective-permute-start.5 = (bf16[832,128]{1,0:T(8,128)(2,1)S(1)}, bf16[832,128]{1,0:T(8,128)(2,1)S(1)}, u32[]{:S(2)}, u32[]{:S(2)}) collective-permute-start(bf16[832,128]{1,0:T(8,128)(2,1)S(1)} %get-tuple-element.25), channel_id=1, source_target_pairs={{1,2},{2,1},{3,4},{4,3},{5,6},{6,5},{7,8},{8,7},{9,10},{10,9},{11,... | collective-permute-start | bytes 638984 | tf_op jit(solution)/shard_map/ppermute | solution.py:289
  19.7 0.8 %collective-permute-done.3.mate_sides_ref = bf16[832,128]{1,0:T(8,128)(2,1)S(1)} collective-permute-done((bf16[832,128]{1,0:T(8,128)(2,1)S(1)}, bf16[832,128]{1,0:T(8,128)(2,1)S(1)}, u32[]{:S(2)}, u32[]{:S(2)}) %collective-permute-start.3) | collective-permute-done | bytes 213024 | tf_op jit(solution)/shard_map/ppermute | solution.py:290
  20.5 0.0 collective-permute-done.2.mate_ref
  20.5 1.1 %copy-done.1 = bf16[1024,384]{1,0:T(8,128)(2,1)S(1)} copy-done((bf16[1024,384]{1,0:T(8,128)(2,1)S(1)}, bf16[1024,384]{1,0:T(8,128)(2,1)}, u32[]{:S(2)}) %copy-start.1) | copy-done | bytes 786456
  21.6 1.1 %copy-done.3 = f32[1024,3,61]{0,2,1:T(8,128)S(1)} copy-done((f32[1024,3,61]{0,2,1:T(8,128)S(1)}, f32[1024,3,61]{0,2,1:T(8,128)}, u32[]{:S(2)}) %copy-start.3) | copy-done | bytes 749592
  22.7 0.7 %copy-done.4 = bf16[61]{0:T(256)(128)(2,1)S(1)} copy-done((bf16[61]{0:T(256)(128)(2,1)S(1)}, bf16[61]{0:T(256)(128)(2,1)}, u32[]{:S(2)}) %copy-start.4) | copy-done | bytes 146
  23.4 0.9 %copy-done.8 = bf16[192,512]{1,0:T(8,128)(2,1)S(1)} copy-done((bf16[192,512]{1,0:T(8,128)(2,1)S(1)}, bf16[192,512]{1,0:T(8,128)(2,1)}, u32[]{:S(2)}) %copy-start.8) | copy-done | bytes 196632
  24.3 3.2 %early.1 = (bf16[512,512]{1,0:T(8,128)(2,1)S(1)}, f32[3,1024,512]{2,1,0:T(8,128)S(1)}, bf16[1024,512]{1,0:T(8,128)(2,1)S(1)}, bf16[832,512]{1,0:T(8,128)(2,1)S(1)}) custom-call(bf16[1,61]{1,0:T(2,128)(2,1)S(1)} %bitcast.4, f32[3,61,1024]{2,1,0:T(8,128)S(1)} %bitcast.3, bf16[192,512]{1,0:T(8,128)(2,1)S(1)} %copy-done.8, bf16[1024,384]{1,0:T(8,128)(2,1)S(1)} %copy-done.1, ...), custom_call_target="tpu_custom_call" | custom-call | flops 1577058304 | bytes 12582912 | tf_op jit(solution)/shard_map/early/pallas_call | solution.py:293
  27.5 0.0 collective-permute-done.5.far_sides_ref
  27.5 0.0 collective-permute-done.4.far_ref
  27.6 0.0 copy-done.2
  27.6 9.4 %score.1 = (f32[8,64,384]{2,1,0:T(8,128)S(1)}, bf16[8,64,384]{2,1,0:T(8,128)(2,1)S(1)}) custom-call(s32[8]{0:T(128)S(1)} %copy-done.5, bf16[512,512]{1,0:T(8,128)(2,1)S(1)} %get-tuple-element.18.toep_ref, bf16[832,384]{1,0:T(8,128)(2,1)S(1)} %collective-permute-done.4.far_ref, bf16[832,128]{1,0:T(8,128)(2,1)S(1)} %collective-permute-done.5.far_sides_ref, ...), custom_call_target="tpu_custom_call" | custom-call | flops 6610223104 | bytes 16777216 | tf_op jit(solution)/shard_map/score/pallas_call | solution.py:313
  37.0 2.2 %collective-permute-start.6 = (bf16[8,64,384]{2,1,0:T(8,128)(2,1)S(1)}, bf16[8,64,384]{2,1,0:T(8,128)(2,1)S(1)}, u32[]{:S(2)}, u32[]{:S(2)}) collective-permute-start(bf16[8,64,384]{2,1,0:T(8,128)(2,1)S(1)} %get-tuple-element.24), channel_id=1, source_target_pairs={{0,1},{1,0},{2,3},{3,2},{4,5},{5,4},{6,7},{7,6},{8,9},{9,8},{10,11... | collective-permute-start | bytes 1179656 | tf_op jit(solution)/shard_map/ppermute | solution.py:342
  39.1 1.3 %collective-permute-done.6 = bf16[8,64,384]{2,1,0:T(8,128)(2,1)S(1)} collective-permute-done((bf16[8,64,384]{2,1,0:T(8,128)(2,1)S(1)}, bf16[8,64,384]{2,1,0:T(8,128)(2,1)S(1)}, u32[]{:S(2)}, u32[]{:S(2)}) %collective-permute-start.6) | collective-permute-done | bytes 393248 | tf_op jit(solution)/shard_map/ppermute | solution.py:342
  40.5 0.1 add_convert_fusion
  40.6 13.5 %all_to_all.5 = bf16[8,64,384]{2,1,0:T(8,128)(2,1)S(1)} all-to-all(bf16[8,64,384]{2,1,0:T(8,128)(2,1)S(1)} %add_convert_fusion), channel_id=1, replica_groups={{0,2,4,6,8,10,12,14},{1,3,5,7,9,11,13,15},{16,18,20,22,24,26,28,30},{17..., dimensions={0} | all-to-all | bytes 786432 | tf_op jit(solution)/shard_map/all_to_all | solution.py:345
  54.1 0.7 %convert_reduce_fusion = f32[64,384]{1,0:T(8,128)} fusion(bf16[8,64,384]{2,1,0:T(8,128)(2,1)S(1)} %all_to_all.5), kind=kLoop, calls=%fused_computation | loop fusion | flops 368640 | bytes 491520 | tf_op jit(solution)/shard_map/reduce_sum | solution.py:346
  (11 shorter events, 0.1 us)
Async XLA Ops:
  0.0 1.1 %copy-start = (bf16[1024,384]{1,0:T(8,128)(2,1)S(1)}, bf16[1024,384]{1,0:T(8,128)(2,1)}, u32[]{:S(2)}) copy-start(bf16[1024,384]{1,0:T(8,128)(2,1)} %raw_ref.1) | copy-start | bytes 2359300
  1.1 26.4 %copy-start.2 = (bf16[1024,1024]{1,0:T(8,128)(2,1)S(1)}, bf16[1024,1024]{1,0:T(8,128)(2,1)}, u32[]{:S(2)}) copy-start(bf16[1024,1024]{1,0:T(8,128)(2,1)} %white_hbm.1) | copy-start | bytes 6291460
  1.1 26.4 %copy-start.5 = (s32[8]{0:T(128)S(1)}, s32[8]{0:T(128)}, u32[]{:S(2)}) copy-start(s32[8]{0:T(128)} %offsets_ref.1) | copy-start | bytes 100
  2.1 7.0 %collective-permute-start = (bf16[512,128]{1,0:T(8,128)(2,1)}, bf16[512,128]{1,0:T(8,128)(2,1)}, u32[]{:S(2)}, u32[]{:S(2)}) collective-permute-start(bf16[512,128]{1,0:T(8,128)(2,1)} %get-tuple-element.15), channel_id=1, source_target_pairs={{0,16},{16,0},{32,48},{48,32},{64,80},{80,64},{96,112},{112,96},{1... | collective-permute-start | bytes 393224 | tf_op jit(solution)/shard_map/ppermute | solution.py:266
  3.7 13.9 %collective-permute-start.1 = (bf16[512,128]{1,0:T(8,128)(2,1)S(1)}, bf16[512,128]{1,0:T(8,128)(2,1)}, u32[]{:S(2)}, u32[]{:S(2)}) collective-permute-start(bf16[512,128]{1,0:T(8,128)(2,1)S(1)} %get-tuple-element.16), channel_id=1, source_target_pairs={{16,32},{32,16},{48,64},{64,48},{80,96},{96,80},{112,128},{128,112... | collective-permute-start | bytes 393224 | tf_op jit(solution)/shard_map/ppermute | solution.py:267
  8.2 12.3 %collective-permute-start.2 = (bf16[832,384]{1,0:T(8,128)(2,1)}, bf16[832,384]{1,0:T(8,128)(2,1)}, u32[]{:S(2)}, u32[]{:S(2)}) collective-permute-start(bf16[832,384]{1,0:T(8,128)(2,1)} %get-tuple-element.17), channel_id=1, source_target_pairs={{0,1},{1,0},{2,3},{3,2},{4,5},{5,4},{6,7},{7,6},{8,9},{9,8},{10,11... | collective-permute-start | bytes 1916936 | tf_op jit(solution)/shard_map/ppermute | solution.py:280
  8.3 19.3 %collective-permute-start.4 = (bf16[832,384]{1,0:T(8,128)(2,1)S(1)}, bf16[832,384]{1,0:T(8,128)(2,1)S(1)}, u32[]{:S(2)}, u32[]{:S(2)}) collective-permute-start(bf16[832,384]{1,0:T(8,128)(2,1)S(1)} %get-tuple-element.19), channel_id=1, source_target_pairs={{1,2},{2,1},{3,4},{4,3},{5,6},{6,5},{7,8},{8,7},{9,10},{10,9},{11,... | collective-permute-start | bytes 1916936 | tf_op jit(solution)/shard_map/ppermute | solution.py:279
  9.0 18.6 %copy-start.6 = (bf16[2,512,512]{2,1,0:T(8,128)(2,1)S(1)}, bf16[2,512,512]{2,1,0:T(8,128)(2,1)}, u32[]{:S(2)}) copy-start(bf16[2,512,512]{2,1,0:T(8,128)(2,1)} %constant.27.clone.forward_hbm) | copy-start | bytes 3145732
  9.0 18.6 %copy-start.7 = (bf16[2,512,384]{2,1,0:T(8,128)(2,1)S(1)}, bf16[2,512,384]{2,1,0:T(8,128)(2,1)}, u32[]{:S(2)}) copy-start(bf16[2,512,384]{2,1,0:T(8,128)(2,1)} %constant.28.clone.inverse_hbm) | copy-start | bytes 2359300
  18.9 1.6 %collective-permute-start.3 = (bf16[832,128]{1,0:T(8,128)(2,1)S(1)}, bf16[832,128]{1,0:T(8,128)(2,1)S(1)}, u32[]{:S(2)}, u32[]{:S(2)}) collective-permute-start(bf16[832,128]{1,0:T(8,128)(2,1)S(1)} %get-tuple-element.26), channel_id=1, source_target_pairs={{0,1},{1,0},{2,3},{3,2},{4,5},{5,4},{6,7},{7,6},{8,9},{9,8},{10,11... | collective-permute-start | bytes 638984 | tf_op jit(solution)/shard_map/ppermute | solution.py:290
  19.0 8.5 %collective-permute-start.5 = (bf16[832,128]{1,0:T(8,128)(2,1)S(1)}, bf16[832,128]{1,0:T(8,128)(2,1)S(1)}, u32[]{:S(2)}, u32[]{:S(2)}) collective-permute-start(bf16[832,128]{1,0:T(8,128)(2,1)S(1)} %get-tuple-element.25), channel_id=1, source_target_pairs={{1,2},{2,1},{3,4},{4,3},{5,6},{6,5},{7,8},{8,7},{9,10},{10,9},{11,... | collective-permute-start | bytes 638984 | tf_op jit(solution)/shard_map/ppermute | solution.py:289
  20.5 1.1 %copy-start.1 = (bf16[1024,384]{1,0:T(8,128)(2,1)S(1)}, bf16[1024,384]{1,0:T(8,128)(2,1)}, u32[]{:S(2)}) copy-start(bf16[1024,384]{1,0:T(8,128)(2,1)} %raw_ref.1) | copy-start | bytes 2359300
  21.6 1.1 %copy-start.3 = (f32[1024,3,61]{0,2,1:T(8,128)S(1)}, f32[1024,3,61]{0,2,1:T(8,128)}, u32[]{:S(2)}) copy-start(f32[1024,3,61]{0,2,1:T(8,128)} %param.14) | copy-start | bytes 2248708
  22.7 0.7 %copy-start.4 = (bf16[61]{0:T(256)(128)(2,1)S(1)}, bf16[61]{0:T(256)(128)(2,1)}, u32[]{:S(2)}) copy-start(bf16[61]{0:T(256)(128)(2,1)} %param.10) | copy-start | bytes 370
  23.4 0.9 %copy-start.8 = (bf16[192,512]{1,0:T(8,128)(2,1)S(1)}, bf16[192,512]{1,0:T(8,128)(2,1)}, u32[]{:S(2)}) copy-start(bf16[192,512]{1,0:T(8,128)(2,1)} %constant.26.clone.spread_ref) | copy-start | bytes 589828
  37.0 3.5 %collective-permute-start.6 = (bf16[8,64,384]{2,1,0:T(8,128)(2,1)S(1)}, bf16[8,64,384]{2,1,0:T(8,128)(2,1)S(1)}, u32[]{:S(2)}, u32[]{:S(2)}) collective-permute-start(bf16[8,64,384]{2,1,0:T(8,128)(2,1)S(1)} %get-tuple-element.24), channel_id=1, source_target_pairs={{0,1},{1,0},{2,3},{3,2},{4,5},{5,4},{6,7},{7,6},{8,9},{9,8},{10,11... | collective-permute-start | bytes 1179656 | tf_op jit(solution)/shard_map/ppermute | solution.py:342

commit v7 on v5

--- a/solution.py
+++ b/solution.py
@@ -224,12 +224,14 @@
         upper, lower = array[rows - REACH :], array[:REACH]
         return jnp.where(even_chan, upper, lower), jnp.where(even_chan, lower, upper)
 
+    to_near, to_far = facing(raw)
+    far = lax.ppermute(to_far, "chan", far_chan)
+    near = lax.ppermute(to_near, "chan", near_chan)
     ahead, behind = pack(raw[:, samples - EDGE :]), pack(raw[:, :EDGE])
+    to_second = jnp.where(even_tm, behind, ahead)
+    to_second, near = lax.optimization_barrier((to_second, near))
     first = lax.ppermute(jnp.where(even_tm, ahead, behind), "tm", near_tm)
-    second = lax.ppermute(jnp.where(even_tm, behind, ahead), "tm", far_tm)
-    to_near, to_far = facing(raw)
-    near = lax.ppermute(to_near, "chan", near_chan)
-    far = lax.ppermute(to_far, "chan", far_chan)
+    second = lax.ppermute(to_second, "tm", far_tm)
     sides = jnp.concatenate(
         [
             jnp.concatenate([first[:, :EDGE], second[:, :EDGE]], axis=1),
@@ -245,7 +247,6 @@
     smem = pl.BlockSpec(memory_space=pltpu.SMEM)
     hbm = pl.BlockSpec(memory_space=pl.ANY)
     bf16 = jnp.bfloat16
-    early = 2 * (rows + REACH) * WIDE * WIDE + 2 * rank * templates * 3 * SLOT * 2 * F
     toep, hat, own_rows, near_rows = pl.pallas_call(
         functools.partial(early_kernel, samples),
         out_shape=(
@@ -257,7 +258,7 @@
         in_specs=[vmem] * 7,
         out_specs=(vmem,) * 4,
         scratch_shapes=[pltpu.VMEM((rows, WIDE), bf16)],
-        cost_estimate=pl.CostEstimate(flops=early, bytes_accessed=12 << 20, transcendentals=0),
+        cost_estimate=pl.CostEstimate(flops=1024, bytes_accessed=1024, transcendentals=0),
         compiler_params=pltpu.CompilerParams(vmem_limit_bytes=24 << 20),
         name="early",
     )(band_taps[None], temporal.transpose(1, 2, 0), jnp.asarray(split_matrix(taps)), raw, sides, near, near_sides)

time: 52.9 us -> 62.4 us (1.18)
  the two profiles are of different devices: /device:TPU:128 before, /device:TPU:88 now
where the time goes in v7:
time: 62.4 us; the launch traced here: 62.2 us
  blocking collectives  20.4 us (33%)
  starting transfers between devices  18.5 us (30%)
  Pallas kernels  11.7 us (19%)
  waiting for transfers between devices  5.95 us (10%)
  other arithmetic  3.78 us (6%)
  local copies, waits for them, and re-layouts  1.64 us (3%)
    all_to_all x1, blocking collectives, local(): shares = lax.all_to_all(both, 'chan', 0, 0, axis_index_groups=members)  20.4 us
    pallas_call x1, Pallas kernels, local(): pl.pallas_call(functools.partial(score_kernel, chunks), out_shape=(jax.Sh...  9.59 us
    ppermute x1, starting transfers between devices, local(): second = lax.ppermute(to_second, 'tm', far_tm)  6.88 us
    ppermute x1, starting transfers between devices, local(): other = lax.ppermute(send, 'chan', near_chan)  6.8 us
    ppermute x1, waiting for transfers between devices, local(): second = lax.ppermute(to_second, 'tm', far_tm)  4.17 us
    select_n x2, other arithmetic, facing(): jnp.where(even_chan, lower, upper)  2.69 us
    ppermute x1, starting transfers between devices, local(): near_sides = lax.ppermute(to_near, 'chan', near_chan)  2.63 us
    pallas_call x1, Pallas kernels, local(): pl.pallas_call(functools.partial(early_kernel, samples), out_shape=(jax.S...  2.12 us
  transfers between devices with their start and end apart: 7, of which 3 were waited for; matrix products, arithmetic and copies ran while one was open for 3% of the time, Pallas kernels for 3%

profile of v7, /device:TPU:88, one launch (start us, length us, event | category | flops | bytes accessed | tf_op | source)
XLA Modules:
  0.0 62.2 jit_solution(12259894071572382904)
XLA Ops:
  0.0 0.0 copy-start.1
  0.0 0.0 copy-start.3
  0.0 0.0 copy-start.5
  0.1 2.7 %broadcast_select_fusion = (bf16[832,384]{1,0:T(8,128)(2,1)}, bf16[832,384]{1,0:T(8,128)(2,1)}) fusion(pred[]{:T(512)S(6)} %eq.10, bf16[1024,384]{1,0:T(8,128)(2,1)} %raw_ref.1), kind=kLoop, calls=%fused_computation.2 | loop fusion | flops 638976 | bytes 2555905 | tf_op jit(solution)/shard_map/jit(_where)/select_n | solution.py:225
  2.7 0.0 collective-permute-start.1
  2.7 1.4 %fusion = (bf16[512,64]{1,0:T(8,128)(2,1)S(1)}, bf16[512,64]{1,0:T(8,128)(2,1)S(1)}, bf16[512,64]{1,0:T(8,128)(2,1)S(1)}, bf16[512,64]{1,0:T(8,128)(2,1)S(1)}) fusion(bf16[1024,384]{1,0:T(8,128)(2,1)} %raw_ref.1), kind=kLoop, calls=%fused_computation.11 | loop fusion | bytes 524288 | tf_op jit(solution)/shard_map/slice | solution.py:52
  4.1 0.2 broadcast_select_fusion.5
  4.3 0.8 %collective-permute-start = (bf16[512,128]{1,0:T(8,128)(2,1)S(1)}, bf16[512,128]{1,0:T(8,128)(2,1)S(1)}, u32[]{:S(2)}, u32[]{:S(2)}) collective-permute-start(bf16[512,128]{1,0:T(8,128)(2,1)S(1)} %get-tuple-element.27), channel_id=1, source_target_pairs={{0,16},{16,0},{32,48},{48,32},{64,80},{80,64},{96,112},{112,96},{1... | collective-permute-start | bytes 393224 | tf_op jit(solution)/shard_map/ppermute | solution.py:233
  5.1 0.7 %collective-permute-start.4 = (bf16[832,384]{1,0:T(8,128)(2,1)}, bf16[832,384]{1,0:T(8,128)(2,1)S(1)}, u32[]{:S(2)}, u32[]{:S(2)}) collective-permute-start(bf16[832,384]{1,0:T(8,128)(2,1)} %get-tuple-element.21), channel_id=1, source_target_pairs={{1,2},{2,1},{3,4},{4,3},{5,6},{6,5},{7,8},{8,7},{9,10},{10,9},{11,... | collective-permute-start | bytes 1916936 | tf_op jit(solution)/shard_map/ppermute | solution.py:228
  5.8 0.0 collective-permute-done.1.mate_ref
  5.8 6.9 %collective-permute-start.2 = (bf16[512,128]{1,0:T(8,128)(2,1)S(1)}, bf16[512,128]{1,0:T(8,128)(2,1)S(1)}, u32[]{:S(2)}, u32[]{:S(2)}) collective-permute-start(bf16[512,128]{1,0:T(8,128)(2,1)S(1)} %get-tuple-element.13), channel_id=1, source_target_pairs={{16,32},{32,16},{48,64},{64,48},{80,96},{96,80},{112,128},{128,112... | collective-permute-start | bytes 393224 | tf_op jit(solution)/shard_map/ppermute | solution.py:234
  12.7 0.0 collective-permute-done
  12.7 0.1 fusion.1
  12.8 4.2 %collective-permute-done.2 = bf16[512,128]{1,0:T(8,128)(2,1)S(1)} collective-permute-done((bf16[512,128]{1,0:T(8,128)(2,1)S(1)}, bf16[512,128]{1,0:T(8,128)(2,1)S(1)}, u32[]{:S(2)}, u32[]{:S(2)}) %collective-permute-start.2) | collective-permute-done | bytes 131104 | tf_op jit(solution)/shard_map/ppermute | solution.py:234
  17.0 0.1 fusion.2
  17.1 0.1 maximum_maximum_fusion.sides_ref
  17.3 2.6 %collective-permute-start.3 = (bf16[832,128]{1,0:T(8,128)(2,1)S(1)}, bf16[832,128]{1,0:T(8,128)(2,1)S(1)}, u32[]{:S(2)}, u32[]{:S(2)}) collective-permute-start(bf16[832,128]{1,0:T(8,128)(2,1)S(1)} %get-tuple-element.30), channel_id=1, source_target_pairs={{0,1},{1,0},{2,3},{3,2},{4,5},{5,4},{6,7},{7,6},{8,9},{9,8},{10,11... | collective-permute-start | bytes 638984 | tf_op jit(solution)/shard_map/ppermute | solution.py:244
  19.9 0.7 %collective-permute-start.5 = (bf16[832,128]{1,0:T(8,128)(2,1)S(1)}, bf16[832,128]{1,0:T(8,128)(2,1)S(1)}, u32[]{:S(2)}, u32[]{:S(2)}) collective-permute-start(bf16[832,128]{1,0:T(8,128)(2,1)S(1)} %get-tuple-element.29), channel_id=1, source_target_pairs={{1,2},{2,1},{3,4},{4,3},{5,6},{6,5},{7,8},{8,7},{9,10},{10,9},{11,... | collective-permute-start | bytes 638984 | tf_op jit(solution)/shard_map/ppermute | solution.py:243
  20.6 0.4 collective-permute-done.3.mate_sides_ref
  21.0 0.0 copy-done.2
  21.0 0.0 copy-done
  21.0 0.0 copy-done.1
  21.0 0.0 copy-done.3
  21.1 2.1 %early.1 = (bf16[512,512]{1,0:T(8,128)(2,1)S(1)}, f32[3,1024,512]{2,1,0:T(8,128)S(1)}, bf16[1024,512]{1,0:T(8,128)(2,1)S(1)}, bf16[832,512]{1,0:T(8,128)(2,1)S(1)}) custom-call(bf16[1,61]{1,0:T(2,128)(2,1)S(1)} %bitcast.4, f32[3,61,1024]{2,1,0:T(8,128)S(1)} %bitcast.3, bf16[192,512]{1,0:T(8,128)(2,1)S(1)} %copy-done.2, bf16[1024,384]{1,0:T(8,128)(2,1)S(1)} %copy-done, ...), custom_call_target="tpu_custom_call" | custom-call | flops 1024 | bytes 1024 | tf_op jit(solution)/shard_map/early/pallas_call | solution.py:250
  23.2 0.0 collective-permute-done.4.far_ref
  23.2 0.0 collective-permute-done.5.far_sides_ref
  23.2 9.6 %score.1 = (f32[8,64,384]{2,1,0:T(8,128)S(1)}, bf16[8,64,384]{2,1,0:T(8,128)(2,1)S(1)}) custom-call(s32[8]{0:T(128)S(1)} %copy-done.5, bf16[512,512]{1,0:T(8,128)(2,1)S(1)} %get-tuple-element.15.toep_ref, bf16[832,384]{1,0:T(8,128)(2,1)S(1)} %collective-permute-done.4.far_ref, bf16[832,128]{1,0:T(8,128)(2,1)S(1)} %collective-permute-done.5.far_sides_ref, ...), custom_call_target="tpu_custom_call" | custom-call | flops 6610223104 | bytes 16777216 | tf_op jit(solution)/shard_map/score/pallas_call | solution.py:270
  32.8 6.8 %collective-permute-start.6 = (bf16[8,64,384]{2,1,0:T(8,128)(2,1)S(1)}, bf16[8,64,384]{2,1,0:T(8,128)(2,1)S(1)}, u32[]{:S(2)}, u32[]{:S(2)}) collective-permute-start(bf16[8,64,384]{2,1,0:T(8,128)(2,1)S(1)} %get-tuple-element.20), channel_id=1, source_target_pairs={{0,1},{1,0},{2,3},{3,2},{4,5},{5,4},{6,7},{7,6},{8,9},{9,8},{10,11... | collective-permute-start | bytes 1179656 | tf_op jit(solution)/shard_map/ppermute | solution.py:299
  39.6 1.3 %collective-permute-done.6 = bf16[8,64,384]{2,1,0:T(8,128)(2,1)S(1)} collective-permute-done((bf16[8,64,384]{2,1,0:T(8,128)(2,1)S(1)}, bf16[8,64,384]{2,1,0:T(8,128)(2,1)S(1)}, u32[]{:S(2)}, u32[]{:S(2)}) %collective-permute-start.6) | collective-permute-done | bytes 393248 | tf_op jit(solution)/shard_map/ppermute | solution.py:299
  41.0 0.1 add_convert_fusion
  41.1 20.4 %all_to_all.5 = bf16[8,64,384]{2,1,0:T(8,128)(2,1)S(1)} all-to-all(bf16[8,64,384]{2,1,0:T(8,128)(2,1)S(1)} %add_convert_fusion), channel_id=1, replica_groups={{0,2,4,6,8,10,12,14},{1,3,5,7,9,11,13,15},{16,18,20,22,24,26,28,30},{17..., dimensions={0} | all-to-all | bytes 786432 | tf_op jit(solution)/shard_map/all_to_all | solution.py:302
  61.5 0.7 %convert_reduce_fusion = f32[64,384]{1,0:T(8,128)} fusion(bf16[8,64,384]{2,1,0:T(8,128)(2,1)S(1)} %all_to_all.5), kind=kLoop, calls=%fused_computation | loop fusion | flops 368640 | bytes 491520 | tf_op jit(solution)/shard_map/reduce_sum | solution.py:303
  (10 shorter events, 0.1 us)
Async XLA Ops:
  0.0 21.0 %copy-start.2 = (bf16[192,512]{1,0:T(8,128)(2,1)S(1)}, bf16[192,512]{1,0:T(8,128)(2,1)}, u32[]{:S(2)}) copy-start(bf16[192,512]{1,0:T(8,128)(2,1)} %constant.33.clone.spread_ref) | copy-start | bytes 589828
  0.0 23.2 %copy-start.6 = (bf16[2,512,512]{2,1,0:T(8,128)(2,1)S(1)}, bf16[2,512,512]{2,1,0:T(8,128)(2,1)}, u32[]{:S(2)}) copy-start(bf16[2,512,512]{2,1,0:T(8,128)(2,1)} %constant.34.clone.forward_hbm) | copy-start | bytes 3145732
  0.0 21.0 %copy-start = (bf16[1024,384]{1,0:T(8,128)(2,1)S(1)}, bf16[1024,384]{1,0:T(8,128)(2,1)}, u32[]{:S(2)}) copy-start(bf16[1024,384]{1,0:T(8,128)(2,1)} %raw_ref.1) | copy-start | bytes 2359300
  0.0 21.0 %copy-start.1 = (f32[1024,3,61]{0,2,1:T(8,128)S(1)}, f32[1024,3,61]{0,2,1:T(8,128)}, u32[]{:S(2)}) copy-start(f32[1024,3,61]{0,2,1:T(8,128)} %param.14) | copy-start | bytes 2248708
  0.0 21.0 %copy-start.3 = (bf16[61]{0:T(256)(128)(2,1)S(1)}, bf16[61]{0:T(256)(128)(2,1)}, u32[]{:S(2)}) copy-start(bf16[61]{0:T(256)(128)(2,1)} %param.10) | copy-start | bytes 370
  0.0 23.2 %copy-start.5 = (s32[8]{0:T(128)S(1)}, s32[8]{0:T(128)}, u32[]{:S(2)}) copy-start(s32[8]{0:T(128)} %offsets_ref.1) | copy-start | bytes 100
  2.7 3.1 %collective-permute-start.1 = (bf16[832,384]{1,0:T(8,128)(2,1)}, bf16[832,384]{1,0:T(8,128)(2,1)S(1)}, u32[]{:S(2)}, u32[]{:S(2)}) collective-permute-start(bf16[832,384]{1,0:T(8,128)(2,1)} %get-tuple-element.22), channel_id=1, source_target_pairs={{0,1},{1,0},{2,3},{3,2},{4,5},{5,4},{6,7},{7,6},{8,9},{9,8},{10,11... | collective-permute-start | bytes 1916936 | tf_op jit(solution)/shard_map/ppermute | solution.py:229
  2.7 20.5 %copy-start.4 = (bf16[1024,1024]{1,0:T(8,128)(2,1)S(1)}, bf16[1024,1024]{1,0:T(8,128)(2,1)}, u32[]{:S(2)}) copy-start(bf16[1024,1024]{1,0:T(8,128)(2,1)} %white_hbm.1) | copy-start | bytes 6291460
  2.7 20.5 %copy-start.7 = (bf16[2,512,384]{2,1,0:T(8,128)(2,1)S(1)}, bf16[2,512,384]{2,1,0:T(8,128)(2,1)}, u32[]{:S(2)}) copy-start(bf16[2,512,384]{2,1,0:T(8,128)(2,1)} %constant.35.clone.inverse_hbm) | copy-start | bytes 2359300
  4.3 8.4 %collective-permute-start = (bf16[512,128]{1,0:T(8,128)(2,1)S(1)}, bf16[512,128]{1,0:T(8,128)(2,1)S(1)}, u32[]{:S(2)}, u32[]{:S(2)}) collective-permute-start(bf16[512,128]{1,0:T(8,128)(2,1)S(1)} %get-tuple-element.27), channel_id=1, source_target_pairs={{0,16},{16,0},{32,48},{48,32},{64,80},{80,64},{96,112},{112,96},{1... | collective-permute-start | bytes 393224 | tf_op jit(solution)/shard_map/ppermute | solution.py:233
  5.1 18.1 %collective-permute-start.4 = (bf16[832,384]{1,0:T(8,128)(2,1)}, bf16[832,384]{1,0:T(8,128)(2,1)S(1)}, u32[]{:S(2)}, u32[]{:S(2)}) collective-permute-start(bf16[832,384]{1,0:T(8,128)(2,1)} %get-tuple-element.21), channel_id=1, source_target_pairs={{1,2},{2,1},{3,4},{4,3},{5,6},{6,5},{7,8},{8,7},{9,10},{10,9},{11,... | collective-permute-start | bytes 1916936 | tf_op jit(solution)/shard_map/ppermute | solution.py:228
  5.8 11.2 %collective-permute-start.2 = (bf16[512,128]{1,0:T(8,128)(2,1)S(1)}, bf16[512,128]{1,0:T(8,128)(2,1)S(1)}, u32[]{:S(2)}, u32[]{:S(2)}) collective-permute-start(bf16[512,128]{1,0:T(8,128)(2,1)S(1)} %get-tuple-element.13), channel_id=1, source_target_pairs={{16,32},{32,16},{48,64},{64,48},{80,96},{96,80},{112,128},{128,112... | collective-permute-start | bytes 393224 | tf_op jit(solution)/shard_map/ppermute | solution.py:234
  17.3 3.7 %collective-permute-start.3 = (bf16[832,128]{1,0:T(8,128)(2,1)S(1)}, bf16[832,128]{1,0:T(8,128)(2,1)S(1)}, u32[]{:S(2)}, u32[]{:S(2)}) collective-permute-start(bf16[832,128]{1,0:T(8,128)(2,1)S(1)} %get-tuple-element.30), channel_id=1, source_target_pairs={{0,1},{1,0},{2,3},{3,2},{4,5},{5,4},{6,7},{7,6},{8,9},{9,8},{10,11... | collective-permute-start | bytes 638984 | tf_op jit(solution)/shard_map/ppermute | solution.py:244
  19.9 3.2 %collective-permute-start.5 = (bf16[832,128]{1,0:T(8,128)(2,1)S(1)}, bf16[832,128]{1,0:T(8,128)(2,1)S(1)}, u32[]{:S(2)}, u32[]{:S(2)}) collective-permute-start(bf16[832,128]{1,0:T(8,128)(2,1)S(1)} %get-tuple-element.29), channel_id=1, source_target_pairs={{1,2},{2,1},{3,4},{4,3},{5,6},{6,5},{7,8},{8,7},{9,10},{10,9},{11,... | collective-permute-start | bytes 638984 | tf_op jit(solution)/shard_map/ppermute | solution.py:243
  32.8 8.2 %collective-permute-start.6 = (bf16[8,64,384]{2,1,0:T(8,128)(2,1)S(1)}, bf16[8,64,384]{2,1,0:T(8,128)(2,1)S(1)}, u32[]{:S(2)}, u32[]{:S(2)}) collective-permute-start(bf16[8,64,384]{2,1,0:T(8,128)(2,1)S(1)} %get-tuple-element.20), channel_id=1, source_target_pairs={{0,1},{1,0},{2,3},{3,2},{4,5},{5,4},{6,7},{7,6},{8,9},{9,8},{10,11... | collective-permute-start | bytes 1179656 | tf_op jit(solution)/shard_map/ppermute | solution.py:299

commit v8 on v5

--- a/solution.py
+++ b/solution.py
@@ -213,7 +213,7 @@
     n_tm = lax.axis_size("tm")
     n_chan = lax.axis_size("chan")
     own = templates // n_chan
-    chunks = 2
+    chunks = 1
 
     near_chan, far_chan = couples(n_chan)
     near_tm, far_tm = couples(n_tm)
@@ -227,9 +227,11 @@
     ahead, behind = pack(raw[:, samples - EDGE :]), pack(raw[:, :EDGE])
     first = lax.ppermute(jnp.where(even_tm, ahead, behind), "tm", near_tm)
     second = lax.ppermute(jnp.where(even_tm, behind, ahead), "tm", far_tm)
-    to_near, to_far = facing(raw)
+    upper = rows - REACH
+    to_far = lax.dynamic_slice_in_dim(raw, jnp.where(even_chan, 0, upper), REACH, 0)
+    to_near = lax.dynamic_slice_in_dim(raw, jnp.where(even_chan, upper, 0), REACH, 0)
+    far = lax.ppermute(to_far, "chan", far_chan)
     near = lax.ppermute(to_near, "chan", near_chan)
-    far = lax.ppermute(to_far, "chan", far_chan)
     sides = jnp.concatenate(
         [
             jnp.concatenate([first[:, :EDGE], second[:, :EDGE]], axis=1),
@@ -245,7 +247,6 @@
     smem = pl.BlockSpec(memory_space=pltpu.SMEM)
     hbm = pl.BlockSpec(memory_space=pl.ANY)
     bf16 = jnp.bfloat16
-    early = 2 * (rows + REACH) * WIDE * WIDE + 2 * rank * templates * 3 * SLOT * 2 * F
     toep, hat, own_rows, near_rows = pl.pallas_call(
         functools.partial(early_kernel, samples),
         out_shape=(
@@ -257,7 +258,7 @@
         in_specs=[vmem] * 7,
         out_specs=(vmem,) * 4,
         scratch_shapes=[pltpu.VMEM((rows, WIDE), bf16)],
-        cost_estimate=pl.CostEstimate(flops=early, bytes_accessed=12 << 20, transcendentals=0),
+        cost_estimate=pl.CostEstimate(flops=1024, bytes_accessed=1024, transcendentals=0),
         compiler_params=pltpu.CompilerParams(vmem_limit_bytes=24 << 20),
         name="early",
     )(band_taps[None], temporal.transpose(1, 2, 0), jnp.asarray(split_matrix(taps)), raw, sides, near, near_sides)

time: 52.9 us -> 52 us (0.983)
  other arithmetic: 3.31 us -> 1.15 us
  starting transfers between devices: 12.1 us -> 13.3 us
    dynamic_slice x0 -> x1, local copies, waits for them, and re-layouts: none -> 1.56 us  [local(): lax.dynamic_slice_in_dim(raw, jnp.where(even_chan, 0, upper), REACH, 0)]
    select_n x2 -> x1, other arithmetic: 1.56 us -> 0.03 us  [facing(): jnp.where(even_chan, lower, upper)]
    ppermute x1, starting transfers between devices: 2.97 us -> 4.1 us  [local(): other = lax.ppermute(send, 'chan', near_chan)]
    unnamed x16, local copies, waits for them, and re-layouts: 1.16 us -> 0.04 us
    select_n x1, other arithmetic: 0.82 us -> 0.17 us  [local(): first = lax.ppermute(jnp.where(even_tm, ahead, behind), 'tm', near_tm)]
where the time goes in v8:
time: 52 us; the launch traced here: 51.8 us
  blocking collectives  15.3 us (29%)
  starting transfers between devices  13.3 us (26%)
  Pallas kernels  11.2 us (22%)
  waiting for transfers between devices  7.39 us (14%)
  local copies, waits for them, and re-layouts  3.2 us (6%)
  other arithmetic  1.15 us (2%)
    all_to_all x1, blocking collectives, local(): shares = lax.all_to_all(both, 'chan', 0, 0, axis_index_groups=members)  15.3 us
    pallas_call x1, Pallas kernels, local(): pl.pallas_call(functools.partial(score_kernel, chunks), out_shape=(jax.Sh...  9.05 us
    ppermute x1, waiting for transfers between devices, local(): second = lax.ppermute(jnp.where(even_tm, behind, ahead), 'tm', far_tm)  5.26 us
    ppermute x1, starting transfers between devices, local(): other = lax.ppermute(send, 'chan', near_chan)  4.1 us
    ppermute x1, starting transfers between devices, local(): second = lax.ppermute(jnp.where(even_tm, behind, ahead), 'tm', far_tm)  3.17 us
    ppermute x1, starting transfers between devices, local(): near = lax.ppermute(to_near, 'chan', near_chan)  2.9 us
    pallas_call x1, Pallas kernels, local(): pl.pallas_call(functools.partial(early_kernel, samples), out_shape=(jax.S...  2.12 us
    ppermute x1, starting transfers between devices, local(): first = lax.ppermute(jnp.where(even_tm, ahead, behind), 'tm', near_tm)  1.66 us
  transfers between devices with their start and end apart: 7, of which 3 were waited for; matrix products, arithmetic and copies ran while one was open for 4% of the time, Pallas kernels for 4%

profile of v8, /device:TPU:128, one launch (start us, length us, event | category | flops | bytes accessed | tf_op | source)
XLA Modules:
  0.0 51.8 jit_solution(17135925440447400533)
XLA Ops:
  0.0 0.0 copy-start.1
  0.0 0.0 copy-start.3
  0.0 0.0 copy-start.5
  0.1 1.4 %fusion = (bf16[512,64]{1,0:T(8,128)(2,1)S(1)}, bf16[512,64]{1,0:T(8,128)(2,1)S(1)}, bf16[512,64]{1,0:T(8,128)(2,1)S(1)}, bf16[512,64]{1,0:T(8,128)(2,1)S(1)}) fusion(bf16[1024,384]{1,0:T(8,128)(2,1)} %raw_ref.1), kind=kLoop, calls=%fused_computation.11 | loop fusion | bytes 524288 | tf_op jit(solution)/shard_map/slice | solution.py:52
  1.4 0.2 broadcast_select_fusion.3
  1.6 1.7 %collective-permute-start = (bf16[512,128]{1,0:T(8,128)(2,1)S(1)}, bf16[512,128]{1,0:T(8,128)(2,1)S(1)}, u32[]{:S(2)}, u32[]{:S(2)}) collective-permute-start(bf16[512,128]{1,0:T(8,128)(2,1)S(1)} %get-tuple-element.23), channel_id=1, source_target_pairs={{0,16},{16,0},{32,48},{48,32},{64,80},{80,64},{96,112},{112,96},{1... | collective-permute-start | bytes 393224 | tf_op jit(solution)/shard_map/ppermute | solution.py:228
  3.3 3.2 %collective-permute-start.1 = (bf16[512,128]{1,0:T(8,128)(2,1)S(1)}, bf16[512,128]{1,0:T(8,128)(2,1)S(1)}, u32[]{:S(2)}, u32[]{:S(2)}) collective-permute-start(bf16[512,128]{1,0:T(8,128)(2,1)S(1)} %get-tuple-element.24), channel_id=1, source_target_pairs={{16,32},{32,16},{48,64},{64,48},{80,96},{96,80},{112,128},{128,112... | collective-permute-start | bytes 393224 | tf_op jit(solution)/shard_map/ppermute | solution.py:229
  6.5 0.0 copy-start.4
  6.5 0.0 copy-start.7
  6.5 1.6 %constant_dynamic-slice_fusion = (bf16[832,384]{1,0:T(8,128)(2,1)S(1)}, bf16[832,384]{1,0:T(8,128)(2,1)S(1)}) fusion(bf16[1024,384]{1,0:T(8,128)(2,1)} %raw_ref.1, s32[]{:T(128)S(6)} %select_n.52, s32[]{:T(128)S(6)} %select_n.49), kind=kLoop, calls=%fused_computation.9 | loop fusion | bytes 2555912 | tf_op jit(solution)/shard_map/dynamic_slice | solution.py:231
  8.1 0.7 %collective-permute-start.4 = (bf16[832,384]{1,0:T(8,128)(2,1)S(1)}, bf16[832,384]{1,0:T(8,128)(2,1)S(1)}, u32[]{:S(2)}, u32[]{:S(2)}) collective-permute-start(bf16[832,384]{1,0:T(8,128)(2,1)S(1)} %get-tuple-element.17), channel_id=1, source_target_pairs={{1,2},{2,1},{3,4},{4,3},{5,6},{6,5},{7,8},{8,7},{9,10},{10,9},{11,... | collective-permute-start | bytes 1916936 | tf_op jit(solution)/shard_map/ppermute | solution.py:233
  8.8 2.9 %collective-permute-start.2 = (bf16[832,384]{1,0:T(8,128)(2,1)S(1)}, bf16[832,384]{1,0:T(8,128)(2,1)S(1)}, u32[]{:S(2)}, u32[]{:S(2)}) collective-permute-start(bf16[832,384]{1,0:T(8,128)(2,1)S(1)} %get-tuple-element.18), channel_id=1, source_target_pairs={{0,1},{1,0},{2,3},{3,2},{4,5},{5,4},{6,7},{7,6},{8,9},{9,8},{10,11... | collective-permute-start | bytes 1916936 | tf_op jit(solution)/shard_map/ppermute | solution.py:234
  11.7 0.0 collective-permute-done
  11.7 0.1 fusion.1
  11.8 5.3 %collective-permute-done.1 = bf16[512,128]{1,0:T(8,128)(2,1)S(1)} collective-permute-done((bf16[512,128]{1,0:T(8,128)(2,1)S(1)}, bf16[512,128]{1,0:T(8,128)(2,1)S(1)}, u32[]{:S(2)}, u32[]{:S(2)}) %collective-permute-start.1) | collective-permute-done | bytes 131104 | tf_op jit(solution)/shard_map/ppermute | solution.py:229
  17.1 0.1 fusion.2
  17.2 0.1 maximum_maximum_fusion.sides_ref
  17.4 0.1 collective-permute-start.3
  17.5 0.7 %collective-permute-start.5 = (bf16[832,128]{1,0:T(8,128)(2,1)S(1)}, bf16[832,128]{1,0:T(8,128)(2,1)S(1)}, u32[]{:S(2)}, u32[]{:S(2)}) collective-permute-start(bf16[832,128]{1,0:T(8,128)(2,1)S(1)} %get-tuple-element.25), channel_id=1, source_target_pairs={{1,2},{2,1},{3,4},{4,3},{5,6},{6,5},{7,8},{8,7},{9,10},{10,9},{11,... | collective-permute-start | bytes 638984 | tf_op jit(solution)/shard_map/ppermute | solution.py:243
  18.1 0.8 %collective-permute-done.3.mate_sides_ref = bf16[832,128]{1,0:T(8,128)(2,1)S(1)} collective-permute-done((bf16[832,128]{1,0:T(8,128)(2,1)S(1)}, bf16[832,128]{1,0:T(8,128)(2,1)S(1)}, u32[]{:S(2)}, u32[]{:S(2)}) %collective-permute-start.3) | collective-permute-done | bytes 213024 | tf_op jit(solution)/shard_map/ppermute | solution.py:244
  18.9 0.0 collective-permute-done.2.mate_ref
  18.9 0.0 copy-done.2
  18.9 0.0 copy-done
  18.9 2.1 %early.1 = (bf16[512,512]{1,0:T(8,128)(2,1)S(1)}, f32[3,1024,512]{2,1,0:T(8,128)S(1)}, bf16[1024,512]{1,0:T(8,128)(2,1)S(1)}, bf16[832,512]{1,0:T(8,128)(2,1)S(1)}) custom-call(bf16[1,61]{1,0:T(2,128)(2,1)S(1)} %bitcast.4, f32[3,61,1024]{2,1,0:T(8,128)S(1)} %bitcast.3, bf16[192,512]{1,0:T(8,128)(2,1)S(1)} %copy-done.2, bf16[1024,384]{1,0:T(8,128)(2,1)S(1)} %copy-done, ...), custom_call_target="tpu_custom_call" | custom-call | flops 1024 | bytes 1024 | tf_op jit(solution)/shard_map/early/pallas_call | solution.py:250
  21.1 0.0 collective-permute-done.5.far_sides_ref
  21.1 0.0 collective-permute-done.4.far_ref
  21.1 9.0 %score.1 = (f32[8,64,384]{2,1,0:T(8,128)S(1)}, bf16[8,64,384]{2,1,0:T(8,128)(2,1)S(1)}) custom-call(s32[8]{0:T(128)S(1)} %copy-done.5, bf16[512,512]{1,0:T(8,128)(2,1)S(1)} %get-tuple-element.11.toep_ref, bf16[832,384]{1,0:T(8,128)(2,1)S(1)} %collective-permute-done.4.far_ref, bf16[832,128]{1,0:T(8,128)(2,1)S(1)} %collective-permute-done.5.far_sides_ref, ...), custom_call_target="tpu_custom_call" | custom-call | flops 6610223104 | bytes 16777216 | tf_op jit(solution)/shard_map/score/pallas_call | solution.py:270
  30.2 4.1 %collective-permute-start.6 = (bf16[8,64,384]{2,1,0:T(8,128)(2,1)S(1)}, bf16[8,64,384]{2,1,0:T(8,128)(2,1)S(1)}, u32[]{:S(2)}, u32[]{:S(2)}) collective-permute-start(bf16[8,64,384]{2,1,0:T(8,128)(2,1)S(1)} %get-tuple-element.16), channel_id=1, source_target_pairs={{0,1},{1,0},{2,3},{3,2},{4,5},{5,4},{6,7},{7,6},{8,9},{9,8},{10,11... | collective-permute-start | bytes 1179656 | tf_op jit(solution)/shard_map/ppermute | solution.py:299
  34.3 1.3 %collective-permute-done.6 = bf16[8,64,384]{2,1,0:T(8,128)(2,1)S(1)} collective-permute-done((bf16[8,64,384]{2,1,0:T(8,128)(2,1)S(1)}, bf16[8,64,384]{2,1,0:T(8,128)(2,1)S(1)}, u32[]{:S(2)}, u32[]{:S(2)}) %collective-permute-start.6) | collective-permute-done | bytes 393248 | tf_op jit(solution)/shard_map/ppermute | solution.py:299
  35.6 0.1 add_convert_fusion
  35.8 15.3 %all_to_all.5 = bf16[8,64,384]{2,1,0:T(8,128)(2,1)S(1)} all-to-all(bf16[8,64,384]{2,1,0:T(8,128)(2,1)S(1)} %add_convert_fusion), channel_id=1, replica_groups={{0,2,4,6,8,10,12,14},{1,3,5,7,9,11,13,15},{16,18,20,22,24,26,28,30},{17..., dimensions={0} | all-to-all | bytes 786432 | tf_op jit(solution)/shard_map/all_to_all | solution.py:302
  51.1 0.7 %convert_reduce_fusion = f32[64,384]{1,0:T(8,128)} fusion(bf16[8,64,384]{2,1,0:T(8,128)(2,1)S(1)} %all_to_all.5), kind=kLoop, calls=%fused_computation | loop fusion | flops 368640 | bytes 491520 | tf_op jit(solution)/shard_map/reduce_sum | solution.py:303
  (10 shorter events, 0.1 us)
Async XLA Ops:
  0.0 18.9 %copy-start.2 = (bf16[192,512]{1,0:T(8,128)(2,1)S(1)}, bf16[192,512]{1,0:T(8,128)(2,1)}, u32[]{:S(2)}) copy-start(bf16[192,512]{1,0:T(8,128)(2,1)} %constant.38.clone.spread_ref) | copy-start | bytes 589828
  0.0 21.1 %copy-start.6 = (bf16[2,512,512]{2,1,0:T(8,128)(2,1)S(1)}, bf16[2,512,512]{2,1,0:T(8,128)(2,1)}, u32[]{:S(2)}) copy-start(bf16[2,512,512]{2,1,0:T(8,128)(2,1)} %constant.39.clone.forward_hbm) | copy-start | bytes 3145732
  0.0 18.9 %copy-start = (bf16[1024,384]{1,0:T(8,128)(2,1)S(1)}, bf16[1024,384]{1,0:T(8,128)(2,1)}, u32[]{:S(2)}) copy-start(bf16[1024,384]{1,0:T(8,128)(2,1)} %raw_ref.1) | copy-start | bytes 2359300
  0.0 18.9 %copy-start.1 = (f32[1024,3,61]{0,2,1:T(8,128)S(1)}, f32[1024,3,61]{0,2,1:T(8,128)}, u32[]{:S(2)}) copy-start(f32[1024,3,61]{0,2,1:T(8,128)} %param.14) | copy-start | bytes 2248708
  0.0 18.9 %copy-start.3 = (bf16[61]{0:T(256)(128)(2,1)S(1)}, bf16[61]{0:T(256)(128)(2,1)}, u32[]{:S(2)}) copy-start(bf16[61]{0:T(256)(128)(2,1)} %param.10) | copy-start | bytes 370
  0.0 21.1 %copy-start.5 = (s32[8]{0:T(128)S(1)}, s32[8]{0:T(128)}, u32[]{:S(2)}) copy-start(s32[8]{0:T(128)} %offsets_ref.1) | copy-start | bytes 100
  1.6 10.1 %collective-permute-start = (bf16[512,128]{1,0:T(8,128)(2,1)S(1)}, bf16[512,128]{1,0:T(8,128)(2,1)S(1)}, u32[]{:S(2)}, u32[]{:S(2)}) collective-permute-start(bf16[512,128]{1,0:T(8,128)(2,1)S(1)} %get-tuple-element.23), channel_id=1, source_target_pairs={{0,16},{16,0},{32,48},{48,32},{64,80},{80,64},{96,112},{112,96},{1... | collective-permute-start | bytes 393224 | tf_op jit(solution)/shard_map/ppermute | solution.py:228
  3.3 13.8 %collective-permute-start.1 = (bf16[512,128]{1,0:T(8,128)(2,1)S(1)}, bf16[512,128]{1,0:T(8,128)(2,1)S(1)}, u32[]{:S(2)}, u32[]{:S(2)}) collective-permute-start(bf16[512,128]{1,0:T(8,128)(2,1)S(1)} %get-tuple-element.24), channel_id=1, source_target_pairs={{16,32},{32,16},{48,64},{64,48},{80,96},{96,80},{112,128},{128,112... | collective-permute-start | bytes 393224 | tf_op jit(solution)/shard_map/ppermute | solution.py:229
  6.5 14.6 %copy-start.4 = (bf16[1024,1024]{1,0:T(8,128)(2,1)S(1)}, bf16[1024,1024]{1,0:T(8,128)(2,1)}, u32[]{:S(2)}) copy-start(bf16[1024,1024]{1,0:T(8,128)(2,1)} %white_hbm.1) | copy-start | bytes 6291460
  6.5 14.6 %copy-start.7 = (bf16[2,512,384]{2,1,0:T(8,128)(2,1)S(1)}, bf16[2,512,384]{2,1,0:T(8,128)(2,1)}, u32[]{:S(2)}) copy-start(bf16[2,512,384]{2,1,0:T(8,128)(2,1)} %constant.40.clone.inverse_hbm) | copy-start | bytes 2359300
  8.1 13.0 %collective-permute-start.4 = (bf16[832,384]{1,0:T(8,128)(2,1)S(1)}, bf16[832,384]{1,0:T(8,128)(2,1)S(1)}, u32[]{:S(2)}, u32[]{:S(2)}) collective-permute-start(bf16[832,384]{1,0:T(8,128)(2,1)S(1)} %get-tuple-element.17), channel_id=1, source_target_pairs={{1,2},{2,1},{3,4},{4,3},{5,6},{6,5},{7,8},{8,7},{9,10},{10,9},{11,... | collective-permute-start | bytes 1916936 | tf_op jit(solution)/shard_map/ppermute | solution.py:233
  8.8 10.1 %collective-permute-start.2 = (bf16[832,384]{1,0:T(8,128)(2,1)S(1)}, bf16[832,384]{1,0:T(8,128)(2,1)S(1)}, u32[]{:S(2)}, u32[]{:S(2)}) collective-permute-start(bf16[832,384]{1,0:T(8,128)(2,1)S(1)} %get-tuple-element.18), channel_id=1, source_target_pairs={{0,1},{1,0},{2,3},{3,2},{4,5},{5,4},{6,7},{7,6},{8,9},{9,8},{10,11... | collective-permute-start | bytes 1916936 | tf_op jit(solution)/shard_map/ppermute | solution.py:234
  17.4 1.6 %collective-permute-start.3 = (bf16[832,128]{1,0:T(8,128)(2,1)S(1)}, bf16[832,128]{1,0:T(8,128)(2,1)S(1)}, u32[]{:S(2)}, u32[]{:S(2)}) collective-permute-start(bf16[832,128]{1,0:T(8,128)(2,1)S(1)} %get-tuple-element.26), channel_id=1, source_target_pairs={{0,1},{1,0},{2,3},{3,2},{4,5},{5,4},{6,7},{7,6},{8,9},{9,8},{10,11... | collective-permute-start | bytes 638984 | tf_op jit(solution)/shard_map/ppermute | solution.py:244
  17.5 3.6 %collective-permute-start.5 = (bf16[832,128]{1,0:T(8,128)(2,1)S(1)}, bf16[832,128]{1,0:T(8,128)(2,1)S(1)}, u32[]{:S(2)}, u32[]{:S(2)}) collective-permute-start(bf16[832,128]{1,0:T(8,128)(2,1)S(1)} %get-tuple-element.25), channel_id=1, source_target_pairs={{1,2},{2,1},{3,4},{4,3},{5,6},{6,5},{7,8},{8,7},{9,10},{10,9},{11,... | collective-permute-start | bytes 638984 | tf_op jit(solution)/shard_map/ppermute | solution.py:243
  30.2 5.5 %collective-permute-start.6 = (bf16[8,64,384]{2,1,0:T(8,128)(2,1)S(1)}, bf16[8,64,384]{2,1,0:T(8,128)(2,1)S(1)}, u32[]{:S(2)}, u32[]{:S(2)}) collective-permute-start(bf16[8,64,384]{2,1,0:T(8,128)(2,1)S(1)} %get-tuple-element.16), channel_id=1, source_target_pairs={{0,1},{1,0},{2,3},{3,2},{4,5},{5,4},{6,7},{7,6},{8,9},{9,8},{10,11... | collective-permute-start | bytes 1179656 | tf_op jit(solution)/shard_map/ppermute | solution.py:299
